TPU v7x, 512 devices: a whole 4x4x16 slice. The times are simulated.
512 devices in a mesh: context: 64 (over x_hi, z, core), tensor: 8 (over y, x_lo).
Axes of the slice: x: 4 (x_hi: 2, x_lo: 2; x = x_hi * 2 + x_lo), y: 4, z: 16, core: 2. Of those that a mesh axis runs over, the one named last changes fastest.
Arguments:
- query: bfloat16 [2, 8192, 8192], P(None, 'context', 'tensor'), may hold values from -6 to 6
- key: bfloat16 [2, 8192, 8192], P(None, 'context', 'tensor'), may hold values from -6 to 6
- value: bfloat16 [2, 8192, 8192], P(None, 'context', 'tensor'), may hold values from -6 to 6
- grad_out: bfloat16 [2, 8192, 8192], P(None, 'context', 'tensor'), may hold values from -6 to 6
- residue: float32 [16, 256], replicated, may hold values from -0.06 to 0.06
- rate: float32 [16, 256], replicated, may hold values from 0 to 1, as said below
Outputs:
- mixed: bfloat16 [2, 8192, 8192], P(None, 'context', 'tensor')
- grad_query: bfloat16 [2, 8192, 8192], P(None, 'context', 'tensor')
- grad_key: bfloat16 [2, 8192, 8192], P(None, 'context', 'tensor')
- grad_value: bfloat16 [2, 8192, 8192], P(None, 'context', 'tensor')
- grad_residue: float32 [16, 256], replicated
Inputs may be any that keep to these rules, and one draw needn't show every extreme that they name: Every rate lies between 0.25 / 8192 and 1/24.
All inputs are finite; a program needn't handle non-finite values.
Results may differ from a plain program's by a relative error of at most 0.0055.
Values sent between devices are 32-bit elements; how exact they have to be, the bound alone decides.
No kernel may reach another device: no remote copies, remote signals or barrier semaphores. Data moves between devices by JAX's collectives and lax.ppermute only.
A program may use at most 128 MiB of HBM per device.

v0:
```python
import jax
import jax.numpy as jnp
from jax import lax
from jax.sharding import PartitionSpec as P

highest = lax.Precision.HIGHEST


def to_work(source, filters):
    seq_count, row_count, channels = source.shape
    repeat = channels // filters
    return (
        source.reshape(seq_count, row_count, repeat, filters)
        .transpose(3, 0, 2, 1)
        .reshape(filters, seq_count * repeat, row_count)
    )


def from_work(source, seq_count):
    filters, columns, row_count = source.shape
    repeat = columns // seq_count
    return (
        source.reshape(filters, seq_count, repeat, row_count)
        .transpose(1, 3, 2, 0)
        .reshape(seq_count, row_count, repeat * filters)
    )


def local(query, key, value, grad_out, residue, rate):
    seq_count, block_len, channels = query.shape
    mode_count, filters = residue.shape
    key_work = to_work(key, filters).astype(jnp.float32)
    value_work = to_work(value, filters).astype(jnp.float32)
    query_work = to_work(query, filters).astype(jnp.float32)
    grad_work = to_work(grad_out, filters).astype(jnp.float32)
    inputs = key_work * value_work
    upstream = grad_work * query_work
    columns = inputs.shape[1]
    position = jnp.arange(block_len, dtype=jnp.float32)
    centre = 0.5 * (block_len - 1)
    lower_mask = position[:, None] >= position[None, :]
    group_size = min(filters, 128)
    group_count = filters // group_size

    def grouped(source):
        return source.reshape((group_count, group_size) + source.shape[1:])

    def local_terms(operands):
        inputs_part, upstream_part, residue_part, rate_part = operands
        offset = rate_part[:, :, None] * (position - centre)
        falling = jnp.exp(-offset)
        rising = jnp.exp(offset)
        toeplitz = jnp.einsum(
            "fna,fnb->fab", falling * residue_part[:, :, None], rising, precision=highest
        )
        toeplitz = jnp.where(lower_mask, toeplitz, 0.0)
        near_fwd = jnp.einsum("fab,fkb->fka", toeplitz, inputs_part, precision=highest)
        near_bwd = jnp.einsum("fab,fka->fkb", toeplitz, upstream_part, precision=highest)
        pair_sums = jnp.einsum("fka,fkb->fab", upstream_part, inputs_part, precision=highest)
        pair_sums = jnp.where(lower_mask, pair_sums, 0.0)
        weighted = jnp.einsum("fab,fnb->fna", pair_sums, rising, precision=highest)
        within = jnp.sum(falling * weighted, axis=2)
        to_end = jnp.exp(-rate_part[:, :, None] * (block_len - 1.0 - position))
        from_start = jnp.exp(-rate_part[:, :, None] * position)
        send_up = jnp.einsum("fnb,fkb->knf", to_end, inputs_part, precision=highest)
        send_down = jnp.einsum("fnb,fkb->knf", from_start, upstream_part, precision=highest)
        return (near_fwd, near_bwd, within, send_up, send_down)

    results = lax.map(
        local_terms, (grouped(inputs), grouped(upstream), grouped(residue.T), grouped(rate.T))
    )
    near_fwd = results[0].reshape(inputs.shape)
    near_bwd = results[1].reshape(inputs.shape)
    within = results[2].reshape(filters, mode_count).T
    send_up = jnp.moveaxis(results[3], 0, 2).reshape(columns, mode_count, filters)
    send_down = jnp.moveaxis(results[4], 0, 2).reshape(columns, mode_count, filters)
    own_index = lax.axis_index("context")
    pieces = (
        lax.all_gather(send_up[None], "context", axis=0, tiled=True),
        lax.all_gather(send_down[None], "context", axis=0, tiled=True),
    )
    piece_rows = pieces[0].shape[0]
    source_index = jnp.arange(piece_rows, dtype=jnp.int32)
    gap_up = own_index - 1 - source_index
    gap_down = source_index - own_index - 1
    span_up = (block_len * jnp.maximum(gap_up, 0)).astype(jnp.float32)
    span_down = (block_len * jnp.maximum(gap_down, 0)).astype(jnp.float32)
    weight_up = jnp.where(
        (gap_up >= 0)[:, None, None], jnp.exp(-rate[None] * span_up[:, None, None]), 0.0
    )
    weight_down = jnp.where(
        (gap_down >= 0)[:, None, None], jnp.exp(-rate[None] * span_down[:, None, None]), 0.0
    )
    summed_up = jnp.sum(weight_up[:, None] * pieces[0], axis=0)
    summed_down = jnp.sum(weight_down[:, None] * pieces[1], axis=0)
    into_rows = residue[:, :, None] * jnp.exp(-rate[:, :, None] * (position + 1.0))
    back_rows = residue[:, :, None] * jnp.exp(-rate[:, :, None] * (block_len - position))
    mixed_z = near_fwd + jnp.einsum("nfa,knf->fka", into_rows, summed_up, precision=highest)
    grad_u = near_bwd + jnp.einsum("nfb,knf->fkb", back_rows, summed_down, precision=highest)
    mixed = from_work((query_work * mixed_z).astype(jnp.bfloat16), seq_count)
    grad_query = from_work((grad_work * mixed_z).astype(jnp.bfloat16), seq_count)
    grad_key = from_work((grad_u * value_work).astype(jnp.bfloat16), seq_count)
    grad_value = from_work((grad_u * key_work).astype(jnp.bfloat16), seq_count)
    own_terms = within + jnp.exp(-rate) * jnp.sum(summed_up * send_down, axis=0)
    summed = lax.psum(own_terms, ("context", "tensor"))
    grad_residue = summed / float(seq_count * block_len * lax.axis_size("context"))
    return (mixed, grad_query, grad_key, grad_value, grad_residue)


def solution(mesh):
    in_specs = (
        P(None, "context", "tensor"),
        P(None, "context", "tensor"),
        P(None, "context", "tensor"),
        P(None, "context", "tensor"),
        P(),
        P(),
    )
    out_specs = (
        P(None, "context", "tensor"),
        P(None, "context", "tensor"),
        P(None, "context", "tensor"),
        P(None, "context", "tensor"),
        P(),
    )
    return jax.shard_map(local, mesh=mesh, in_specs=in_specs, out_specs=out_specs, check_vma=False)
```

profile of v0, /device:TPU:1, one launch (start us, length us, event | category | flops | bytes accessed | tf_op | source)
XLA Modules:
  0.0 637.5 jit_solution(12570698685817545872)
XLA Ops:
  7.3 1.4 convert_multiply_fusion.1
  9.9 1.4 convert_multiply_fusion
  11.3 1.4 mul.244
  12.7 1.6 copy.49
  15.3 144.2 %while.22 = (s32[]{:T(128)}, f32[2,128,8,128]{3,2,1,0:T(8,128)}, f32[2,128,8,128]{3,2,1,0:T(8,128)}, f32[2,128,16]{2,1,0:T(8,128)S(1)}, f32[2,8,16,128]{2,1,3,0:...) while((s32[]{:T(128)}, f32[2,128,8,128]{3,2,1,0:T(8,128)}, ...), condition=%wide.region_2.3_spmd.clone.clone, body=%wide.region_0.2_spmd.clone.clone.sunk | while | flops 1468809472 | bytes 57032424 | solution.py:69
  15.8 14.2 %fusion.132 = f32[128,128,128]{2,1,0:T(8,128)S(1)} fusion(f32[128,16]{1,0:T(8,128)S(1)} %dynamic-slice_bitcast_fusion.4, f32[128]{0:T(128)S(1)} %iota_add_fusion.3, f32[128,16]{1,0:T(8,128)S(1)} %get-tuple-element.320), kind=kOutput, calls=%fused_computation.16.clone.1 | convolution fusion | flops 403701760 | bytes 8405504 | tf_op jit(solution)/shard_map/while/body/eval_jaxpr/fna,fnb->fab/dot_general | solution.py:53
  30.1 13.1 %fusion.133 = f32[2,128,8,128]{3,2,1,0:T(8,128)S(1)} fusion(f32[2,128,8,128]{3,2,1,0:T(8,128)S(1)} %copy-done.4, s32[]{:T(128)} %get-tuple-element.333, f32[128,128,128]{2,1,0:T(8,128)S(1)} %fusion.132, pred[128,128]{1,0:T(8,128)(4,1)S(1)} %iota_compare_fusion.2, f32[2,128,8,128]{3,2,1,0:T(8,128)S(1)} %get-tuple-element.350), kind=kOutput, calls=%fused_computation.20.clone.1 | convolution fusion | flops 203423744 | bytes 9454592 | tf_op jit(solution)/shard_map/while/body/eval_jaxpr/fab,fkb->fka/dot_general | solution.py:57
  43.2 8.1 %fusion.134 = f32[2,128,8,128]{3,2,1,0:T(8,128)} fusion(f32[2,128,8,128]{3,2,1,0:T(8,128)} %get-tuple-element.335, s32[]{:T(128)} %get-tuple-element.333, f32[128,128,128]{2,1,0:T(8,128)S(1)} %fusion.132, pred[128,128]{1,0:T(8,128)(4,1)S(1)} %iota_compare_fusion.2, f32[2,128,8,128]{3,2,1,0:T(8,128)S(1)} %get-tuple-element.353), kind=kOutput, calls=%fused_computation.22.clone.1 | convolution fusion | flops 203423744 | bytes 9454592 | tf_op jit(solution)/shard_map/while/body/eval_jaxpr/fab,fka->fkb/dot_general | solution.py:58
  51.4 13.6 %fusion.135 = f32[128,128,128]{2,1,0:T(8,128)S(1)} fusion(f32[2,128,8,128]{3,2,1,0:T(8,128)S(1)} %get-tuple-element.353, s32[]{:T(128)} %get-tuple-element.333, f32[2,128,8,128]{3,2,1,0:T(8,128)S(1)} %get-tuple-element.350), kind=kOutput, calls=%fused_computation.34.clone.1 | convolution fusion | flops 201326592 | bytes 9438208 | tf_op jit(solution)/shard_map/while/body/eval_jaxpr/fka,fkb->fab/dot_general | solution.py:59
  65.0 13.4 %fusion.136 = f32[128,16]{1,0:T(8,128)S(1)} fusion(f32[128,128,128]{2,1,0:T(8,128)S(1)} %fusion.135, pred[128,128]{1,0:T(8,128)(4,1)S(1)} %iota_compare_fusion.2, f32[128]{0:T(128)S(1)} %iota_add_fusion.3, f32[128,16]{1,0:T(8,128)S(1)} %get-tuple-element.320), kind=kOutput, calls=%fused_computation.18.clone.1 | convolution fusion | flops 406059008 | bytes 8421888 | tf_op jit(solution)/shard_map/while/body/eval_jaxpr/fab,fnb->fna/dot_general | solution.py:61
  78.4 1.8 fusion.137
  80.2 1.0 copy-done.3
  81.2 1.8 fusion.138
  83.4 14.5 %fusion.132 = f32[128,128,128]{2,1,0:T(8,128)S(1)} fusion(f32[128,16]{1,0:T(8,128)S(1)} %dynamic-slice_bitcast_fusion.4, f32[128]{0:T(128)S(1)} %iota_add_fusion.3, f32[128,16]{1,0:T(8,128)S(1)} %get-tuple-element.320), kind=kOutput, calls=%fused_computation.16.clone.1 | convolution fusion | flops 403701760 | bytes 8405504 | tf_op jit(solution)/shard_map/while/body/eval_jaxpr/fna,fnb->fab/dot_general | solution.py:53
  97.9 13.1 %fusion.133 = f32[2,128,8,128]{3,2,1,0:T(8,128)S(1)} fusion(f32[2,128,8,128]{3,2,1,0:T(8,128)S(1)} %copy-done.4, s32[]{:T(128)} %get-tuple-element.333, f32[128,128,128]{2,1,0:T(8,128)S(1)} %fusion.132, pred[128,128]{1,0:T(8,128)(4,1)S(1)} %iota_compare_fusion.2, f32[2,128,8,128]{3,2,1,0:T(8,128)S(1)} %get-tuple-element.350), kind=kOutput, calls=%fused_computation.20.clone.1 | convolution fusion | flops 203423744 | bytes 9454592 | tf_op jit(solution)/shard_map/while/body/eval_jaxpr/fab,fkb->fka/dot_general | solution.py:57
  111.0 8.1 %fusion.134 = f32[2,128,8,128]{3,2,1,0:T(8,128)} fusion(f32[2,128,8,128]{3,2,1,0:T(8,128)} %get-tuple-element.335, s32[]{:T(128)} %get-tuple-element.333, f32[128,128,128]{2,1,0:T(8,128)S(1)} %fusion.132, pred[128,128]{1,0:T(8,128)(4,1)S(1)} %iota_compare_fusion.2, f32[2,128,8,128]{3,2,1,0:T(8,128)S(1)} %get-tuple-element.353), kind=kOutput, calls=%fused_computation.22.clone.1 | convolution fusion | flops 203423744 | bytes 9454592 | tf_op jit(solution)/shard_map/while/body/eval_jaxpr/fab,fka->fkb/dot_general | solution.py:58
  119.1 13.4 %fusion.135 = f32[128,128,128]{2,1,0:T(8,128)S(1)} fusion(f32[2,128,8,128]{3,2,1,0:T(8,128)S(1)} %get-tuple-element.353, s32[]{:T(128)} %get-tuple-element.333, f32[2,128,8,128]{3,2,1,0:T(8,128)S(1)} %get-tuple-element.350), kind=kOutput, calls=%fused_computation.34.clone.1 | convolution fusion | flops 201326592 | bytes 9438208 | tf_op jit(solution)/shard_map/while/body/eval_jaxpr/fka,fkb->fab/dot_general | solution.py:59
  132.5 13.6 %fusion.136 = f32[128,16]{1,0:T(8,128)S(1)} fusion(f32[128,128,128]{2,1,0:T(8,128)S(1)} %fusion.135, pred[128,128]{1,0:T(8,128)(4,1)S(1)} %iota_compare_fusion.2, f32[128]{0:T(128)S(1)} %iota_add_fusion.3, f32[128,16]{1,0:T(8,128)S(1)} %get-tuple-element.320), kind=kOutput, calls=%fused_computation.18.clone.1 | convolution fusion | flops 406059008 | bytes 8421888 | tf_op jit(solution)/shard_map/while/body/eval_jaxpr/fab,fnb->fna/dot_general | solution.py:61
  146.2 1.8 fusion.137
  148.0 1.0 copy-done.3
  149.0 1.8 fusion.138
  160.5 2.2 copy.66
  163.6 2.5 reshape.174
  166.1 2.5 reshape.175
  168.6 1.5 reshape.176
  170.1 1.5 reshape.177
  171.6 1.6 copy.68
  173.3 2.2 copy.45
  175.6 2.3 copy.55
  177.8 1.4 copy.59
  179.3 1.4 copy.61
  182.2 148.5 %all-gather.5.cloned.1.call-done = f32[64,8,16,256]{3,2,1,0:T(8,128)} async-done(((f32[1,8,16,256]{3,2,1,0:T(8,128)}), f32[64,8,16,256]{3,2,1,0:T(8,128)}) %all-gather.5.cloned.1.call-update) | async-done | bytes 8388624 | tf_op jit(solution)/shard_map/all_gather | solution.py:80
  330.7 163.1 %all-gather.3.cloned.1.call-done = f32[64,8,16,256]{3,2,1,0:T(8,128)} async-done(((f32[1,8,16,256]{3,2,1,0:T(8,128)}), f32[64,8,16,256]{3,2,1,0:T(8,128)}) %all-gather.3.cloned.1.call-update) | async-done | bytes 8388624 | tf_op jit(solution)/shard_map/all_gather | solution.py:79
  493.9 8.0 %multiply_reduce_fusion = (f32[8,16,256]{2,1,0:T(8,128)S(1)}, f32[8,16,256]{2,1,0:T(8,128)}) fusion(f32[64,8,16,256]{3,2,1,0:T(8,128)} %all-gather.5.cloned.1.call-done, f32[64,16,256]{2,1,0:T(8,128)S(1)} %get-tuple-element.253, f32[64,8,16,256]{3,2,1,0:T(8,128)} %all-gather.3.cloned.1.call-done, f32[64,16,256]{2,1,0:T(8,128)S(1)} %get-tuple-element.254), kind=kLoop, calls=%fused_computation.68 | loop fusion | flops 8323072 | bytes 19136512 | tf_op jit(solution)/shard_map/reduce_sum | solution.py:95
  501.9 1.4 copy.53
  504.3 1.7 copy.65
  506.0 1.4 bitcast_add_fusion
  507.4 101.2 %psum.7 = f32[16,256]{1,0:T(8,128)S(1)} all-reduce(f32[16,256]{1,0:T(8,128)} %bitcast_add_fusion), channel_id=1, replica_groups=mesh['context'=64,'tensor'=8] {'context','tensor'}, use_global_device_ids=true, to_apply=%region_6.7 | all-reduce | flops 4096 | bytes 32768 | tf_op jit(solution)/shard_map/psum | solution.py:105
  609.2 5.3 multiply_convert_fusion.2
  614.4 1.5 copy.54
  615.9 1.2 reshape.161
  617.1 1.5 copy.56
  618.6 1.2 reshape.163
  620.2 4.9 multiply_convert_fusion
  625.1 1.5 copy.60
  626.6 1.2 reshape.166
  627.8 1.5 copy.62
  629.3 1.2 reshape.168
  (63 shorter events, 8.0 us)
Async XLA Ops:
  7.2 7.2 %copy-start.6 = (f32[16,256]{1,0:T(8,128)S(1)}, f32[16,256]{1,0:T(8,128)}, u32[]{:S(2)}) copy-start(f32[16,256]{1,0:T(8,128)} %param.13) | copy-start | bytes 49156
  7.2 323.5 %all-gather.5.cloned.1.call-start = ((), (), s32[]{:S(2)}) async-start(), calls=%async_computation.1 | async-start | bytes 8519680 | tf_op jit(solution)/shard_map/all_gather | solution.py:80
  15.7 14.3 %copy-start.4 = (f32[2,128,8,128]{3,2,1,0:T(8,128)S(1)}, f32[2,128,8,128]{3,2,1,0:T(8,128)}, u32[]{:S(2)}) copy-start(f32[2,128,8,128]{3,2,1,0:T(8,128)} %get-tuple-element.334) | copy-start | bytes 3145732 | tf_op jit(solution)/shard_map/while
  43.2 8.1 %copy-start.5 = (f32[2,128,8,128]{3,2,1,0:T(8,128)}, f32[2,128,8,128]{3,2,1,0:T(8,128)S(1)}, u32[]{:S(2)}) copy-start(f32[2,128,8,128]{3,2,1,0:T(8,128)S(1)} %fusion.133) | copy-start | bytes 3145732 | tf_op jit(solution)/shard_map/while
  51.3 27.0 %copy-start.2 = (f32[2,8,16,128]{2,1,3,0:T(8,128)S(1)}, f32[2,8,16,128]{2,1,3,0:T(8,128)}, u32[]{:S(2)}) copy-start(f32[2,8,16,128]{2,1,3,0:T(8,128)} %get-tuple-element.337) | copy-start | bytes 393220 | tf_op jit(solution)/shard_map/while
  80.2 1.1 copy-start.3
  83.3 14.6 %copy-start.4 = (f32[2,128,8,128]{3,2,1,0:T(8,128)S(1)}, f32[2,128,8,128]{3,2,1,0:T(8,128)}, u32[]{:S(2)}) copy-start(f32[2,128,8,128]{3,2,1,0:T(8,128)} %get-tuple-element.334) | copy-start | bytes 3145732 | tf_op jit(solution)/shard_map/while
  111.0 8.1 %copy-start.5 = (f32[2,128,8,128]{3,2,1,0:T(8,128)}, f32[2,128,8,128]{3,2,1,0:T(8,128)S(1)}, u32[]{:S(2)}) copy-start(f32[2,128,8,128]{3,2,1,0:T(8,128)S(1)} %fusion.133) | copy-start | bytes 3145732 | tf_op jit(solution)/shard_map/while
  119.1 27.0 %copy-start.2 = (f32[2,8,16,128]{2,1,3,0:T(8,128)S(1)}, f32[2,8,16,128]{2,1,3,0:T(8,128)}, u32[]{:S(2)}) copy-start(f32[2,8,16,128]{2,1,3,0:T(8,128)} %get-tuple-element.337) | copy-start | bytes 393220 | tf_op jit(solution)/shard_map/while
  148.0 1.1 copy-start.3
  159.4 3.3 copy-start.7
  160.5 333.4 %all-gather.3.cloned.1.call-start = ((), (), s32[]{:S(2)}) async-start(), calls=%async_computation | async-start | bytes 8519680 | tf_op jit(solution)/shard_map/all_gather | solution.py:79
  501.9 118.3 %copy-start = (f32[2,128,4,256]{1,2,0,3:T(4,128)S(1)}, f32[2,128,4,256]{1,2,0,3:T(4,128)}, u32[]{:S(2)}) copy-start(f32[2,128,4,256]{1,2,0,3:T(4,128)} %copy.59) | copy-start | bytes 3145732
  504.3 115.9 %copy-start.1 = (f32[2,128,4,256]{1,2,0,3:T(4,128)S(1)}, f32[2,128,4,256]{1,2,0,3:T(4,128)}, u32[]{:S(2)}) copy-start(f32[2,128,4,256]{1,2,0,3:T(4,128)} %copy.61) | copy-start | bytes 3145732
  609.1 11.1 %copy-start.8 = (f32[128]{0:T(128)S(1)}, f32[128]{0:T(128)}, u32[]{:S(2)}) copy-start(f32[128]{0:T(128)} %iota_subtract_fusion.1) | copy-start | bytes 1540
Sparse Core Ops, SparseCore 0:
  160.6 170.0 all-gather.4
  334.6 159.2 all-gather.2
where the time goes:
time: 641 us; the launch traced here: 638 us
  waiting for transfers between devices  312 us (49%)
  matrix products  143 us (22%)
  blocking collectives  101 us (16%)
  local copies, waits for them, and re-layouts  42.6 us (7%)
  other arithmetic  15.4 us (2%)
  between operations  14.5 us (2%)
  loops' own time  9.43 us (1%)
    all_gather x1, waiting for transfers between devices, local(): lax.all_gather(send_up[None], 'context', axis=0, tiled=True)  163 us
    all_gather x1, waiting for transfers between devices, local(): lax.all_gather(send_down[None], 'context', axis=0, tiled=True)  149 us
    psum x1, blocking collectives, local(): summed = lax.psum(own_terms, ('context', 'tensor'))  101 us
    dot_general x2, matrix products, local_terms(): jnp.einsum('fna,fnb->fab', falling * residue_part[:, :, None], rising, pr...  28.7 us
    dot_general x2, matrix products, local_terms(): jnp.einsum('fka,fkb->fab', upstream_part, inputs_part, precision=highest)  27 us
    dot_general x2, matrix products, local_terms(): weighted = jnp.einsum('fab,fnb->fna', pair_sums, rising, precision=highest)  26.9 us
    dot_general x2, matrix products, local_terms(): jnp.einsum('fab,fkb->fka', toeplitz, inputs_part, precision=highest)  26.2 us
    dot_general x2, matrix products, local_terms(): jnp.einsum('fab,fka->fkb', toeplitz, upstream_part, precision=highest)  16.2 us
  transfers between devices with their start and end apart: 2, of which 2 were waited for; matrix products, arithmetic and copies ran while one was open for 3% of the time, Pallas kernels for 0%

commit v1 on v0

v1 whole, which is shorter than its diff:
```python
import functools

import jax
import jax.numpy as jnp
from jax import lax
from jax.experimental import pallas as pl
from jax.experimental.pallas import tpu as pltpu
from jax.sharding import Mesh, PartitionSpec as P

F32 = jnp.float32
LANES = 128
MODES = 16
ROWS = 9


def spread(row):
    return jnp.broadcast_to(row, (8, LANES))


def bottom():
    return lax.broadcasted_iota(jnp.int32, (8, LANES), 0) >= 4


def swap_halves(tile):
    return pltpu.roll(tile, 4, 0)


def lanes_of(half):
    return pl.ds(half * LANES, LANES)


def local_kernel(core, query, key, value, grad, residue, rate, near, back, keep, send, within, work_u, work_g):
    length = query.shape[1]
    repeat = query.shape[2] // (2 * LANES)
    first = core[0] == 0
    for half in range(2):
        for seq in range(2):
            for rep in range(repeat):
                cut = pl.ds(rep * 2 * LANES + half * LANES, LANES)
                rows = pl.ds(seq * repeat + rep, length, stride=8)
                work_u[rows, :] = key[seq, :, cut].astype(F32) * value[seq, :, cut].astype(F32)
                work_g[rows, :] = grad[seq, :, cut].astype(F32) * query[seq, :, cut].astype(F32)
        for group in range(0, MODES, 8):
            modes = range(group, group + 8)
            decay = [spread(jnp.exp(-rate[n : n + 1, lanes_of(half)])) for n in modes]
            weight = [spread(residue[n : n + 1, lanes_of(half)]) for n in modes]

            def step(i, carry, decay=decay, weight=weight, group=group, half=half):
                ups, downs, sums = (list(c) for c in carry)
                ahead = pl.ds(pl.multiple_of(i * 8, 8), 8)
                behind = pl.ds(pl.multiple_of((length - 1 - i) * 8, 8), 8)
                u, g, gr = work_u[ahead, :], work_g[ahead, :], work_g[behind, :]
                parts, parts_back = [], []
                for m in range(8):
                    ups[m] = decay[m] * ups[m] + u
                    downs[m] = decay[m] * downs[m] + gr
                    sums[m] = sums[m] + g * ups[m]
                    parts.append(weight[m] * ups[m])
                    parts_back.append(weight[m] * downs[m])
                z, dz = tree(parts), tree(parts_back)
                if group:
                    z, dz = z + near[half, ahead, :], dz + back[half, behind, :]
                near[half, ahead, :] = z
                back[half, behind, :] = dz
                return tuple(ups), tuple(downs), tuple(sums)

            zero = tuple(jnp.zeros((8, LANES), F32) for _ in range(8))
            ups, downs, sums = lax.fori_loop(0, length, step, (zero, zero, zero), unroll=2)
            low = bottom()
            for m in range(8):
                top_half = jnp.where(low, swap_halves(downs[m]), ups[m])
                end_half = jnp.where(low, downs[m], swap_halves(ups[m]))
                piece = half * MODES + group + m
                keep[piece] = jnp.where(first, top_half, end_half)
                send[piece] = jnp.where(first, end_half, top_half)
                within[piece : piece + 1, :] = jnp.sum(sums[m], axis=0, keepdims=True)


def tree(parts):
    while len(parts) > 1:
        parts = [parts[i] + parts[i + 1] for i in range(0, len(parts), 2)]
    return parts[0]


def order(first, own, other):
    return jnp.where(first, own, other), jnp.where(first, other, own)


def pair_kernel(core, own, other, within, rate, out, *, block):
    first = core[0] == 0
    low = bottom()
    for half in range(2):
        for n in range(MODES):
            piece = half * MODES + n
            pace = rate[n : n + 1, lanes_of(half)]
            decay = spread(jnp.exp(-pace * float(block)))
            left, right = order(first, own[piece], other[piece])
            joined = jnp.where(low, left + decay * right, decay * left + right)
            cross = jnp.where(low, 0.0, left * swap_halves(right))
            total = jnp.exp(-pace) * jnp.sum(cross, axis=0, keepdims=True)
            for row in range(8):
                out[piece * ROWS + row] = joined[row : row + 1, :]
            out[piece * ROWS + 8] = within[piece : piece + 1, :] + total


def scan_kernel(pieces, pace, out, *, block):
    count = pieces.shape[0] // ROWS
    decay = jnp.exp(-pace[...] * float(block))
    decay4 = jnp.broadcast_to(decay, (4, LANES))

    def load(index, base):
        return jnp.concatenate([pieces[index * ROWS + base + j] for j in range(4)], axis=0)

    ahead = jnp.zeros((4, LANES), F32)
    cross = jnp.zeros((4, LANES), F32)
    local = jnp.zeros((1, LANES), F32)
    for index in range(count):
        for j in range(4):
            out[index * ROWS + j] = ahead[j : j + 1, :]
        cross = cross + ahead * load(index, 4)
        local = local + pieces[index * ROWS + 8]
        ahead = decay4 * ahead + load(index, 0)
    behind = jnp.zeros((4, LANES), F32)
    for index in reversed(range(count)):
        for j in range(4):
            out[index * ROWS + 4 + j] = behind[j : j + 1, :]
        behind = decay4 * behind + load(index, 4)
    total = local + jnp.exp(-pace[...]) * jnp.sum(cross, axis=0, keepdims=True)
    for index in range(count):
        out[index * ROWS + 8] = total


def split_kernel(core, pieces, own, other, rate, keep, send, total, *, block):
    first = core[0] == 0
    low = bottom()
    for half in range(2):
        for n in range(MODES):
            piece = half * MODES + n
            pace = rate[n : n + 1, lanes_of(half)]
            decay = spread(jnp.exp(-pace * float(block)))
            left, right = order(first, own[piece], other[piece])
            outer = jnp.concatenate([pieces[piece * ROWS + row] for row in range(8)], axis=0)
            inner = decay * outer + jnp.where(low, right, left)
            for_left = jnp.where(low, inner, outer)
            for_right = jnp.where(low, outer, inner)
            mine, others = order(first, for_left, for_right)
            keep[piece] = mine
            send[piece] = others
            total[piece : piece + 1, :] = pieces[piece * ROWS + 8]


def final_kernel(
    core, query, key, value, grad, residue, rate, near, back, own, other, mixed, grad_query, grad_key, grad_value, work
):
    length = query.shape[1]
    repeat = query.shape[2] // (2 * LANES)
    first = core[0] == 0
    low = bottom()
    for half in range(2):
        decay, forward, backward = [], [], []
        for n in range(MODES):
            piece = half * MODES + n
            weight = spread(residue[n : n + 1, lanes_of(half)])
            decay.append(spread(jnp.exp(-rate[n : n + 1, lanes_of(half)])))
            one, two = order(first, own[piece], other[piece])
            forward.append(weight * jnp.where(low, swap_halves(two), one))
            backward.append(weight * jnp.where(low, two, swap_halves(one)))

        def step(i, carry, decay=decay, half=half, source=near):
            carry = [decay[n] * carry[n] for n in range(MODES)]
            rows = pl.ds(pl.multiple_of(i * 8, 8), 8)
            work[rows, :] = source[half, rows, :] + tree(carry)
            return tuple(carry)

        lax.fori_loop(0, length, step, tuple(forward), unroll=2)
        for seq in range(2):
            for rep in range(repeat):
                cut = pl.ds(rep * 2 * LANES + half * LANES, LANES)
                z = work[pl.ds(seq * repeat + rep, length, stride=8), :]
                mixed[seq, :, cut] = (query[seq, :, cut].astype(F32) * z).astype(jnp.bfloat16)
                grad_query[seq, :, cut] = (grad[seq, :, cut].astype(F32) * z).astype(jnp.bfloat16)

        def step_back(i, carry, decay=decay, half=half):
            return step(length - 1 - i, carry, decay, half, back)

        lax.fori_loop(0, length, step_back, tuple(backward), unroll=2)
        for seq in range(2):
            for rep in range(repeat):
                cut = pl.ds(rep * 2 * LANES + half * LANES, LANES)
                du = work[pl.ds(seq * repeat + rep, length, stride=8), :]
                grad_key[seq, :, cut] = (du * value[seq, :, cut].astype(F32)).astype(jnp.bfloat16)
                grad_value[seq, :, cut] = (du * key[seq, :, cut].astype(F32)).astype(jnp.bfloat16)


VMEM = pl.BlockSpec(memory_space=pltpu.VMEM)
SMEM = pl.BlockSpec(memory_space=pltpu.SMEM)


def struct(*shape, dtype=F32):
    return jax.ShapeDtypeStruct(shape, dtype)


def local(query, key, value, grad_out, residue, rate):
    seq_count, block, channels = query.shape
    pieces = 2 * MODES
    core_id = lax.axis_index("core")
    core = core_id.astype(jnp.int32).reshape(1)
    tile = struct(pieces, 8, LANES)
    rows = struct(pieces * ROWS, 1, LANES)
    works = struct(2, block * 8, LANES)
    near, back, keep, send, within = pl.pallas_call(
        local_kernel,
        name="local",
        out_shape=(works, works, tile, tile, struct(pieces, LANES)),
        in_specs=[SMEM] + [VMEM] * 6,
        out_specs=(VMEM,) * 5,
        scratch_shapes=[pltpu.VMEM((block * 8, LANES), F32)] * 2,
    )(core, query, key, value, grad_out, residue, rate)
    exchange = [(0, 1), (1, 0)]
    other = lax.ppermute(send, "core", exchange)
    joined = pl.pallas_call(
        functools.partial(pair_kernel, block=block),
        name="pair",
        out_shape=rows,
        in_specs=[SMEM] + [VMEM] * 4,
        out_specs=VMEM,
    )(core, keep, other, within, rate)
    gathered = lax.all_to_all(joined, ("xh", "z"), 0, 0, tiled=True)
    pace = lax.dynamic_slice(
        rate, (lax.axis_index("z"), lax.axis_index("xh") * LANES), (1, LANES)
    )
    scanned = pl.pallas_call(
        functools.partial(scan_kernel, block=2 * block),
        name="scan",
        out_shape=rows,
        in_specs=[VMEM] * 2,
        out_specs=VMEM,
    )(gathered, pace)
    returned = lax.all_to_all(scanned, ("xh", "z"), 0, 0, tiled=True)
    state, state_send, total = pl.pallas_call(
        functools.partial(split_kernel, block=block),
        name="split",
        out_shape=(tile, tile, struct(pieces, LANES)),
        in_specs=[SMEM] + [VMEM] * 4,
        out_specs=(VMEM,) * 3,
    )(core, returned, keep, other, rate)
    state_other = lax.ppermute(state_send, "core", exchange)
    group = lax.axis_size("core") * lax.axis_size("tensor")
    copies = jnp.broadcast_to(total[None], (group,) + total.shape)
    totals = lax.all_to_all(copies, ("core", "tensor"), 0, 0, tiled=True)
    summed = jnp.sum(totals, axis=0)
    summed = jnp.concatenate([summed[:MODES], summed[MODES:]], axis=1)
    length = block * lax.axis_size(("xh", "z", "core"))
    grad_residue = summed / float(seq_count * length)
    whole = struct(*query.shape, dtype=jnp.bfloat16)
    mixed, grad_query, grad_key, grad_value = pl.pallas_call(
        final_kernel,
        name="final",
        out_shape=(whole,) * 4,
        in_specs=[SMEM] + [VMEM] * 10,
        out_specs=(VMEM,) * 4,
        scratch_shapes=[pltpu.VMEM((block * 8, LANES), F32)],
    )(core, query, key, value, grad_out, residue, rate, near, back, state, state_other)
    return (mixed, grad_query, grad_key, grad_value, grad_residue)


def solution(mesh):
    shape = (2, 16, 2, mesh.shape["tensor"])
    split = Mesh(mesh.devices.reshape(shape), ("xh", "z", "core", "tensor"))
    spec = P(None, ("xh", "z", "core"), "tensor")
    specs = (spec, spec, spec, spec)
    return jax.shard_map(
        local, mesh=split, in_specs=specs + (P(), P()), out_specs=specs + (P(),), check_vma=False
    )
```

time: 641 us -> 101 us (0.16)
  waiting for transfers between devices: 312 us -> 18.3 us
  matrix products: 143 us -> 0 us
  blocking collectives: 101 us -> 20.7 us
  local copies, waits for them, and re-layouts: 42.6 us -> 4.68 us
  starting transfers between devices: 0.08 us -> 31.6 us
  Pallas kernels: 0 us -> 24.1 us
  other arithmetic: 15.4 us -> 0.63 us
  between operations: 14.5 us -> 0.69 us
  loops' own time: 9.43 us -> 0 us
    all_gather x2 -> x0, waiting for transfers between devices: 312 us -> none  [the longest x1 163 us: local(): lax.all_gather(send_up[None], 'context', axis=0, tiled=True)]
    dot_general x16 -> x0, matrix products: 143 us -> none  [the longest x2 28.7 us: local_terms(): jnp.einsum('fna,fnb->fab', falling * residue_part[:, :, None], rising, pr...]
    psum x1 -> x0, blocking collectives: 101 us -> none  [local(): summed = lax.psum(own_terms, ('context', 'tensor'))]
    pallas_call x0 -> x5, Pallas kernels: none -> 24.1 us  [the longest x1 11.1 us: local(): pl.pallas_call(local_kernel, name='local', out_shape=(works, works, tile,...]
    all_to_all x0 -> x2, starting transfers between devices: none -> 20.8 us  [the longest x1 12.3 us: local(): gathered = lax.all_to_all(joined, ('xh', 'z'), 0, 0, tiled=True)]
    all_to_all x0 -> x1, blocking collectives: none -> 20.7 us  [local(): returned = lax.all_to_all(scanned, ('xh', 'z'), 0, 0, tiled=True)]
    all_to_all x0 -> x2, waiting for transfers between devices: none -> 15.9 us  [the longest x1 15.9 us: local(): gathered = lax.all_to_all(joined, ('xh', 'z'), 0, 0, tiled=True)]
    convert_element_type x8 -> x0, local copies, waits for them, and re-layouts: 15.4 us -> none  [the longest x2 4.79 us: local(): query_work = to_work(query, filters).astype(jnp.float32)]
  transfers between devices with their start and end apart: 2 -> 4, of which waited for: 2 -> 3; matrix products, arithmetic and copies ran while one was open for 3% -> 1% of each run, Pallas kernels for 0% -> 8%
where the time goes in v1:
time: 101 us
  starting transfers between devices  31.6 us (31%)
  Pallas kernels  24.1 us (24%)
  blocking collectives  20.7 us (20%)
  waiting for transfers between devices  18.3 us (18%)
  local copies, waits for them, and re-layouts  4.68 us (5%)
    all_to_all x1, blocking collectives, local(): returned = lax.all_to_all(scanned, ('xh', 'z'), 0, 0, tiled=True)  20.7 us
    all_to_all x1, waiting for transfers between devices, local(): gathered = lax.all_to_all(joined, ('xh', 'z'), 0, 0, tiled=True)  15.9 us
    all_to_all x1, starting transfers between devices, local(): gathered = lax.all_to_all(joined, ('xh', 'z'), 0, 0, tiled=True)  12.3 us
    pallas_call x1, Pallas kernels, local(): pl.pallas_call(local_kernel, name='local', out_shape=(works, works, tile,...  11.1 us
    ppermute x1, starting transfers between devices, local(): other = lax.ppermute(send, 'core', exchange)  8.73 us
    all_to_all x1, starting transfers between devices, local(): totals = lax.all_to_all(copies, ('core', 'tensor'), 0, 0, tiled=True)  8.51 us
    pallas_call x1, Pallas kernels, local(): pl.pallas_call(final_kernel, name='final', out_shape=(whole,) * 4, in_spe...  7.68 us
  transfers between devices with their start and end apart: 4, of which 3 were waited for; matrix products, arithmetic and copies ran while one was open for 1% of the time, Pallas kernels for 8%

profile of v1, /device:TPU:1, one launch (start us, length us, event | category | flops | bytes accessed | tf_op | source)
XLA Modules:
  0.0 100.6 jit_solution(17493939094600120352)
XLA Ops:
  0.6 11.1 %local.1 = (f32[2,1024,128]{2,1,0:T(8,128)}, f32[2,1024,128]{2,1,0:T(8,128)}, f32[32,8,128]{2,1,0:T(8,128)}, f32[32,8,128]{2,1,0:T(8,128)}, f32[32,128]{1,0:T(8,128)}) custom-call(s32[1]{0:T(128)} %bitcast.core, bf16[2,128,1024]{2,1,0:T(8,128)(2,1)} %query.3, bf16[2,128,1024]{2,1,0:T(8,128)(2,1)} %key.3, bf16[2,128,1024]{2,1,0:T(8,128)(2,1)} %value.3, ...), custom_call_target="tpu_custom_call" | custom-call | tf_op jit(solution)/shard_map/local/pallas_call | solution.py:211
  11.8 8.7 %collective-permute-start = (f32[32,8,128]{2,1,0:T(8,128)}, f32[32,8,128]{2,1,0:T(8,128)S(1)}, u32[]{:S(2)}, u32[]{:S(2)}) collective-permute-start(f32[32,8,128]{2,1,0:T(8,128)} %get-tuple-element.20), channel_id=1, source_target_pairs={{0,8},{8,0},{1,9},{9,1},{2,10},{10,2},{3,11},{11,3},{4,12},{12,4},... | collective-permute-start | bytes 393224 | tf_op jit(solution)/shard_map/ppermute | solution.py:220
  20.5 1.2 %collective-permute-done.other = f32[32,8,128]{2,1,0:T(8,128)S(1)} collective-permute-done((f32[32,8,128]{2,1,0:T(8,128)}, f32[32,8,128]{2,1,0:T(8,128)S(1)}, u32[]{:S(2)}, u32[]{:S(2)}) %collective-permute-start) | collective-permute-done | bytes 131104 | tf_op jit(solution)/shard_map/ppermute | solution.py:220
  21.7 0.0 copy-start.1
  21.7 0.7 copy-done.1
  22.3 1.7 %pair.1 = f32[288,1,128]{2,1,0:T(1,128)} custom-call(s32[1]{0:T(128)} %bitcast.core, f32[32,8,128]{2,1,0:T(8,128)} %get-tuple-element.19.own, f32[32,8,128]{2,1,0:T(8,128)} %copy-done.1, f32[32,128]{1,0:T(8,128)} %get-tuple-element.21.within, f32[16,256]{1,0:T(8,128)} %rate.7), custom_call_target="tpu_custom_call" | custom-call | tf_op jit(solution)/shard_map/pair/pallas_call | solution.py:221
  24.1 12.3 %all-to-all-start = ((f32[288,1,128]{2,1,0:T(1,128)}), f32[288,1,128]{2,1,0:T(1,128)S(1)}, u32[]{:S(2)}, u32[]{:S(2)}) async-start(f32[288,1,128]{2,1,0:T(1,128)} %pair.1), calls=%async_computation | async-start | bytes 294912 | tf_op jit(solution)/shard_map/all_to_all | solution.py:228
  36.4 1.3 %dynamic_slice.3.pace = f32[1,128]{1,0:T(1,128)} dynamic-slice(f32[16,256]{1,0:T(8,128)} %rate.7, s32[]{:T(128)S(6)} %select_n.6, s32[]{:T(128)S(6)} %select_n.7), dynamic_slice_sizes={1,128} | dynamic-slice | bytes 1028 | tf_op jit(solution)/shard_map/dynamic_slice | solution.py:229
  37.7 15.9 %all-to-all-done.pieces = f32[288,1,128]{2,1,0:T(1,128)S(1)} async-done(((f32[288,1,128]{2,1,0:T(1,128)}), f32[288,1,128]{2,1,0:T(1,128)S(1)}, u32[]{:S(2)}, u32[]{:S(2)}) %all-to-all-start) | async-done | bytes 147488 | tf_op jit(solution)/shard_map/all_to_all | solution.py:228
  53.6 0.0 copy-start
  53.6 0.7 copy-done
  54.2 1.7 %scan.1 = f32[288,1,128]{2,1,0:T(1,128)} custom-call(f32[288,1,128]{2,1,0:T(1,128)} %copy-done, f32[1,128]{1,0:T(1,128)} %dynamic_slice.3.pace), custom_call_target="tpu_custom_call" | custom-call | tf_op jit(solution)/shard_map/scan/pallas_call | solution.py:232
  56.0 20.7 %all_to_all.15.pieces = f32[288,1,128]{2,1,0:T(1,128)} all-to-all(f32[288,1,128]{2,1,0:T(1,128)} %scan.1), channel_id=1, replica_groups=mesh['xh'=2,'z'=16,'core'=2,'tensor'=8] {'xh','z'}, dimensions={0} | all-to-all | bytes 294912 | tf_op jit(solution)/shard_map/all_to_all | solution.py:239
  76.6 1.8 %split.1 = (f32[32,8,128]{2,1,0:T(8,128)}, f32[32,8,128]{2,1,0:T(8,128)}, f32[32,128]{1,0:T(8,128)}) custom-call(s32[1]{0:T(128)} %bitcast.core, f32[288,1,128]{2,1,0:T(1,128)} %all_to_all.15.pieces, f32[32,8,128]{2,1,0:T(8,128)} %get-tuple-element.19.own, f32[32,8,128]{2,1,0:T(8,128)} %copy-done.1, f32[16,256]{1,0:T(8,128)} %rate.7), custom_call_target="tpu_custom_call" | custom-call | tf_op jit(solution)/shard_map/split/pallas_call | solution.py:240
  78.5 1.4 %broadcast_in_dim.2 = f32[16,32,128]{2,1,0:T(8,128)} broadcast(f32[32,128]{1,0:T(8,128)} %get-tuple-element.28), dimensions={1,2} | broadcast | bytes 278528 | tf_op jit(solution)/shard_map/broadcast_in_dim | solution.py:249
  79.9 0.0 copy-start.3
  79.9 8.5 %all-to-all-start.2 = ((f32[16,32,128]{2,1,0:T(8,128)}), f32[16,32,128]{2,1,0:T(8,128)S(1)}, u32[]{:S(2)}, u32[]{:S(2)}) async-start(f32[16,32,128]{2,1,0:T(8,128)} %broadcast_in_dim.2), calls=%async_computation.2 | async-start | bytes 524288 | tf_op jit(solution)/shard_map/all_to_all | solution.py:250
  88.4 0.0 copy-done.3
  88.4 2.0 %collective-permute-start.1 = (f32[32,8,128]{2,1,0:T(8,128)S(1)}, f32[32,8,128]{2,1,0:T(8,128)S(1)}, u32[]{:S(2)}, u32[]{:S(2)}) collective-permute-start(f32[32,8,128]{2,1,0:T(8,128)S(1)} %copy-done.3), channel_id=1, source_target_pairs={{0,8},{8,0},{1,9},{9,1},{2,10},{10,2},{3,11},{11,3},{4,12},{12,4},... | collective-permute-start | bytes 393224 | tf_op jit(solution)/shard_map/ppermute | solution.py:247
  90.4 1.2 %collective-permute-done.1.other = f32[32,8,128]{2,1,0:T(8,128)S(1)} collective-permute-done((f32[32,8,128]{2,1,0:T(8,128)S(1)}, f32[32,8,128]{2,1,0:T(8,128)S(1)}, u32[]{:S(2)}, u32[]{:S(2)}) %collective-permute-start.1) | collective-permute-done | bytes 131104 | tf_op jit(solution)/shard_map/ppermute | solution.py:247
  91.7 0.0 copy-start.2
  91.7 0.6 copy-done.2
  92.3 7.7 %final.1 = (bf16[2,128,1024]{2,1,0:T(8,128)(2,1)}, bf16[2,128,1024]{2,1,0:T(8,128)(2,1)}, bf16[2,128,1024]{2,1,0:T(8,128)(2,1)}, bf16[2,128,1024]{2,1,0:T(8,128)(2,1)}) custom-call(s32[1]{0:T(128)} %bitcast.core, bf16[2,128,1024]{2,1,0:T(8,128)(2,1)} %query.3, bf16[2,128,1024]{2,1,0:T(8,128)(2,1)} %key.3, bf16[2,128,1024]{2,1,0:T(8,128)(2,1)} %value.3, ...), custom_call_target="tpu_custom_call" | custom-call | tf_op jit(solution)/shard_map/final/pallas_call | solution.py:256
  100.0 0.0 all-to-all-done.2
  100.0 0.6 maximum_multiply_fusion
  (2 shorter events, 0.0 us)
Async XLA Ops:
  11.8 9.9 %collective-permute-start = (f32[32,8,128]{2,1,0:T(8,128)}, f32[32,8,128]{2,1,0:T(8,128)S(1)}, u32[]{:S(2)}, u32[]{:S(2)}) collective-permute-start(f32[32,8,128]{2,1,0:T(8,128)} %get-tuple-element.20), channel_id=1, source_target_pairs={{0,8},{8,0},{1,9},{9,1},{2,10},{10,2},{3,11},{11,3},{4,12},{12,4},... | collective-permute-start | bytes 393224 | tf_op jit(solution)/shard_map/ppermute | solution.py:220
  21.7 0.7 copy-start.1
  24.1 29.5 %all-to-all-start = ((f32[288,1,128]{2,1,0:T(1,128)}), f32[288,1,128]{2,1,0:T(1,128)S(1)}, u32[]{:S(2)}, u32[]{:S(2)}) async-start(f32[288,1,128]{2,1,0:T(1,128)} %pair.1), calls=%async_computation | async-start | bytes 294912 | tf_op jit(solution)/shard_map/all_to_all | solution.py:228
  53.6 0.7 copy-start
  79.9 8.5 %copy-start.3 = (f32[32,8,128]{2,1,0:T(8,128)S(1)}, f32[32,8,128]{2,1,0:T(8,128)}, u32[]{:S(2)}) copy-start(f32[32,8,128]{2,1,0:T(8,128)} %get-tuple-element.23) | copy-start | bytes 393220
  79.9 20.1 %all-to-all-start.2 = ((f32[16,32,128]{2,1,0:T(8,128)}), f32[16,32,128]{2,1,0:T(8,128)S(1)}, u32[]{:S(2)}, u32[]{:S(2)}) async-start(f32[16,32,128]{2,1,0:T(8,128)} %broadcast_in_dim.2), calls=%async_computation.2 | async-start | bytes 524288 | tf_op jit(solution)/shard_map/all_to_all | solution.py:250
  88.4 3.2 %collective-permute-start.1 = (f32[32,8,128]{2,1,0:T(8,128)S(1)}, f32[32,8,128]{2,1,0:T(8,128)S(1)}, u32[]{:S(2)}, u32[]{:S(2)}) collective-permute-start(f32[32,8,128]{2,1,0:T(8,128)S(1)} %copy-done.3), channel_id=1, source_target_pairs={{0,8},{8,0},{1,9},{9,1},{2,10},{10,2},{3,11},{11,3},{4,12},{12,4},... | collective-permute-start | bytes 393224 | tf_op jit(solution)/shard_map/ppermute | solution.py:247
  91.7 0.6 copy-start.2

commit v2 on v1

--- a/solution.py
+++ b/solution.py
@@ -29,43 +29,75 @@
     return pl.ds(half * LANES, LANES)
 
 
-def local_kernel(core, query, key, value, grad, residue, rate, near, back, keep, send, within, work_u, work_g):
+def columns(half, rep):
+    return pl.ds(rep * 2 * LANES + half * LANES, LANES)
+
+
+def slab_copy(source, target, sems, which, half, rep):
+    cut = columns(half, rep)
+    return pltpu.make_async_copy(source.at[:, :, cut], target.at[:, :, cut], sems.at[which, half, rep])
+
+
+def fetch(pairs, sems, half, repeat, wait):
+    for rep in range(repeat):
+        for which, (source, target) in enumerate(pairs):
+            copy = slab_copy(source, target, sems, which, half, rep)
+            copy.wait() if wait else copy.start()
+
+
+def products_of(half, first, second, work, repeat):
+    length = first.shape[1]
+    for seq in range(2):
+        for rep in range(repeat):
+            cut = columns(half, rep)
+            rows = pl.ds(seq * repeat + rep, length, stride=8)
+            work[half, rows, :] = first[seq, :, cut].astype(F32) * second[seq, :, cut].astype(F32)
+
+
+def sums_kernel(
+    core,
+    query_in,
+    key_in,
+    value_in,
+    grad_in,
+    rate,
+    keep,
+    send,
+    within,
+    query,
+    key,
+    value,
+    grad,
+    work_u,
+    work_g,
+    sems,
+):
     length = query.shape[1]
     repeat = query.shape[2] // (2 * LANES)
     first = core[0] == 0
-    for half in range(2):
-        for seq in range(2):
-            for rep in range(repeat):
-                cut = pl.ds(rep * 2 * LANES + half * LANES, LANES)
-                rows = pl.ds(seq * repeat + rep, length, stride=8)
-                work_u[rows, :] = key[seq, :, cut].astype(F32) * value[seq, :, cut].astype(F32)
-                work_g[rows, :] = grad[seq, :, cut].astype(F32) * query[seq, :, cut].astype(F32)
+    pairs = ((key_in, key), (value_in, value), (grad_in, grad), (query_in, query))
+    for half in range(2):
+        fetch(pairs, sems, half, repeat, False)
+    for half in range(2):
+        fetch(pairs, sems, half, repeat, True)
+        products_of(half, key, value, work_u, repeat)
+        products_of(half, grad, query, work_g, repeat)
         for group in range(0, MODES, 8):
-            modes = range(group, group + 8)
-            decay = [spread(jnp.exp(-rate[n : n + 1, lanes_of(half)])) for n in modes]
-            weight = [spread(residue[n : n + 1, lanes_of(half)]) for n in modes]
-
-            def step(i, carry, decay=decay, weight=weight, group=group, half=half):
+            decay = [spread(jnp.exp(-rate[n : n + 1, lanes_of(half)])) for n in range(group, group + 8)]
+
+            def step(i, carry, decay=decay, half=half):
                 ups, downs, sums = (list(c) for c in carry)
                 ahead = pl.ds(pl.multiple_of(i * 8, 8), 8)
                 behind = pl.ds(pl.multiple_of((length - 1 - i) * 8, 8), 8)
-                u, g, gr = work_u[ahead, :], work_g[ahead, :], work_g[behind, :]
-                parts, parts_back = [], []
+                u, g, gr = work_u[half, ahead, :], work_g[half, ahead, :], work_g[half, behind, :]
                 for m in range(8):
                     ups[m] = decay[m] * ups[m] + u
                     downs[m] = decay[m] * downs[m] + gr
                     sums[m] = sums[m] + g * ups[m]
-                    parts.append(weight[m] * ups[m])
-                    parts_back.append(weight[m] * downs[m])
-                z, dz = tree(parts), tree(parts_back)
-                if group:
-                    z, dz = z + near[half, ahead, :], dz + back[half, behind, :]
-                near[half, ahead, :] = z
-                back[half, behind, :] = dz
                 return tuple(ups), tuple(downs), tuple(sums)
 
             zero = tuple(jnp.zeros((8, LANES), F32) for _ in range(8))
-            ups, downs, sums = lax.fori_loop(0, length, step, (zero, zero, zero), unroll=2)
+            ups, downs, sums = lax.fori_loop(0, length, step, (zero, zero, zero), unroll=4)
             low = bottom()
             for m in range(8):
                 top_half = jnp.where(low, swap_halves(downs[m]), ups[m])
@@ -74,6 +106,43 @@
                 keep[piece] = jnp.where(first, top_half, end_half)
                 send[piece] = jnp.where(first, end_half, top_half)
                 within[piece : piece + 1, :] = jnp.sum(sums[m], axis=0, keepdims=True)
+
+
+def near_kernel(
+    query_in, key_in, value_in, grad_in, residue, rate, near, back, query, key, value, grad, work_u, work_g, sems
+):
+    length = query.shape[1]
+    repeat = query.shape[2] // (2 * LANES)
+    pairs = ((key_in, key), (value_in, value), (grad_in, grad), (query_in, query))
+    for half in range(2):
+        fetch(pairs, sems, half, repeat, False)
+    for half in range(2):
+        fetch(pairs, sems, half, repeat, True)
+        products_of(half, key, value, work_u, repeat)
+        products_of(half, grad, query, work_g, repeat)
+        for group in range(0, MODES, 8):
+            modes = range(group, group + 8)
+            decay = [spread(jnp.exp(-rate[n : n + 1, lanes_of(half)])) for n in modes]
+            weight = [spread(residue[n : n + 1, lanes_of(half)]) for n in modes]
+
+            def step(i, carry, decay=decay, weight=weight, group=group, half=half):
+                ups, downs = (list(c) for c in carry)
+                ahead = pl.ds(pl.multiple_of(i * 8, 8), 8)
+                behind = pl.ds(pl.multiple_of((length - 1 - i) * 8, 8), 8)
+                u, g = work_u[half, ahead, :], work_g[half, behind, :]
+                for m in range(8):
+                    ups[m] = decay[m] * ups[m] + u
+                    downs[m] = decay[m] * downs[m] + g
+                z = tree([weight[m] * ups[m] for m in range(8)])
+                dz = tree([weight[m] * downs[m] for m in range(8)])
+                if group:
+                    z, dz = z + near[half, ahead, :], dz + back[half, behind, :]
+                near[half, ahead, :] = z
+                back[half, behind, :] = dz
+                return tuple(ups), tuple(downs)
+
+            zero = tuple(jnp.zeros((8, LANES), F32) for _ in range(8))
+            lax.fori_loop(0, length, step, (zero, zero), unroll=2)
 
 
 def tree(parts):
@@ -146,16 +215,60 @@
             mine, others = order(first, for_left, for_right)
             keep[piece] = mine
             send[piece] = others
-            total[piece : piece + 1, :] = pieces[piece * ROWS + 8]
+            row = pieces[piece * ROWS + 8]
+            for copy in range(total.shape[0]):
+                total[copy, piece : piece + 1, :] = row
 
 
 def final_kernel(
-    core, query, key, value, grad, residue, rate, near, back, own, other, mixed, grad_query, grad_key, grad_value, work
+    core,
+    query_in,
+    key_in,
+    value_in,
+    grad_in,
+    residue,
+    rate,
+    near,
+    back,
+    own,
+    other,
+    mixed_out,
+    grad_query_out,
+    grad_key_out,
+    grad_value_out,
+    work,
+    query,
+    key,
+    value,
+    grad,
+    mixed,
+    grad_query,
+    grad_key,
+    grad_value,
+    in_sems,
+    sems,
 ):
     length = query.shape[1]
     repeat = query.shape[2] // (2 * LANES)
     first = core[0] == 0
     low = bottom()
+    outs = ((mixed, mixed_out), (grad_query, grad_query_out), (grad_key, grad_key_out), (grad_value, grad_value_out))
+
+    pairs = ((query_in, query), (grad_in, grad), (value_in, value), (key_in, key))
+    for half in range(2):
+        fetch(pairs, in_sems, half, repeat, False)
+
+    def products(half, source_a, source_b, base):
+        target_a, target_b = outs[base][0], outs[base + 1][0]
+        for rep in range(repeat):
+            cut = columns(half, rep)
+            for seq in range(2):
+                shared = work[pl.ds(seq * repeat + rep, length, stride=8), :]
+                target_a[seq, :, cut] = (source_a[seq, :, cut].astype(F32) * shared).astype(jnp.bfloat16)
+                target_b[seq, :, cut] = (source_b[seq, :, cut].astype(F32) * shared).astype(jnp.bfloat16)
+            for which in (base, base + 1):
+                slab_copy(*outs[which], sems, which, half, rep).start()
+
     for half in range(2):
         decay, forward, backward = [], [], []
         for n in range(MODES):
@@ -172,28 +285,27 @@
             work[rows, :] = source[half, rows, :] + tree(carry)
             return tuple(carry)
 
+        def step_back(i, carry, step=step):
+            return step(length - 1 - i, carry, source=back)
+
         lax.fori_loop(0, length, step, tuple(forward), unroll=2)
-        for seq in range(2):
+        fetch(pairs, in_sems, half, repeat, True)
+        products(half, query, grad, 0)
+        lax.fori_loop(0, length, step_back, tuple(backward), unroll=2)
+        products(half, value, key, 2)
+    for which in range(4):
+        for half in range(2):
             for rep in range(repeat):
-                cut = pl.ds(rep * 2 * LANES + half * LANES, LANES)
-                z = work[pl.ds(seq * repeat + rep, length, stride=8), :]
-                mixed[seq, :, cut] = (query[seq, :, cut].astype(F32) * z).astype(jnp.bfloat16)
-                grad_query[seq, :, cut] = (grad[seq, :, cut].astype(F32) * z).astype(jnp.bfloat16)
-
-        def step_back(i, carry, decay=decay, half=half):
-            return step(length - 1 - i, carry, decay, half, back)
-
-        lax.fori_loop(0, length, step_back, tuple(backward), unroll=2)
-        for seq in range(2):
-            for rep in range(repeat):
-                cut = pl.ds(rep * 2 * LANES + half * LANES, LANES)
-                du = work[pl.ds(seq * repeat + rep, length, stride=8), :]
-                grad_key[seq, :, cut] = (du * value[seq, :, cut].astype(F32)).astype(jnp.bfloat16)
-                grad_value[seq, :, cut] = (du * key[seq, :, cut].astype(F32)).astype(jnp.bfloat16)
+                slab_copy(*outs[which], sems, which, half, rep).wait()
 
 
 VMEM = pl.BlockSpec(memory_space=pltpu.VMEM)
 SMEM = pl.BlockSpec(memory_space=pltpu.SMEM)
+HBM = pl.BlockSpec(memory_space=pltpu.HBM)
+
+
+def room(mebibytes):
+    return pltpu.CompilerParams(vmem_limit_bytes=int(mebibytes * 2**20))
 
 
 def struct(*shape, dtype=F32):
@@ -208,14 +320,30 @@
     tile = struct(pieces, 8, LANES)
     rows = struct(pieces * ROWS, 1, LANES)
     works = struct(2, block * 8, LANES)
-    near, back, keep, send, within = pl.pallas_call(
-        local_kernel,
-        name="local",
-        out_shape=(works, works, tile, tile, struct(pieces, LANES)),
-        in_specs=[SMEM] + [VMEM] * 6,
-        out_specs=(VMEM,) * 5,
-        scratch_shapes=[pltpu.VMEM((block * 8, LANES), F32)] * 2,
-    )(core, query, key, value, grad_out, residue, rate)
+    whole = struct(*query.shape, dtype=jnp.bfloat16)
+    repeat = channels // (2 * LANES)
+    inputs = tuple(pltpu.with_memory_space_constraint(x, pltpu.HBM) for x in (query, key, value, grad_out))
+    buffers = [pltpu.VMEM(query.shape, jnp.bfloat16)] * 4
+    arrivals = [pltpu.SemaphoreType.DMA((4, 2, repeat))]
+    keep, send, within = pl.pallas_call(
+        sums_kernel,
+        name="sums",
+        out_shape=(tile, tile, struct(pieces, LANES)),
+        in_specs=[SMEM] + [HBM] * 4 + [VMEM],
+        out_specs=(VMEM,) * 3,
+        scratch_shapes=buffers + [pltpu.VMEM(works.shape, F32)] * 2 + arrivals,
+        compiler_params=room(12),
+    )(core, *inputs, rate)
+    near, back = pl.pallas_call(
+        near_kernel,
+        name="near",
+        out_shape=(works, works),
+        in_specs=[HBM] * 4 + [VMEM] * 2,
+        out_specs=(VMEM,) * 2,
+        scratch_shapes=buffers + [pltpu.VMEM(works.shape, F32)] * 2 + arrivals,
+        compiler_params=room(12),
+        cost_estimate=pl.CostEstimate(flops=2**26, transcendentals=0, bytes_accessed=2**22),
+    )(*inputs, residue, rate)
     exchange = [(0, 1), (1, 0)]
     other = lax.ppermute(send, "core", exchange)
     joined = pl.pallas_call(
@@ -224,43 +352,46 @@
         out_shape=rows,
         in_specs=[SMEM] + [VMEM] * 4,
         out_specs=VMEM,
+        compiler_params=room(4),
     )(core, keep, other, within, rate)
     gathered = lax.all_to_all(joined, ("xh", "z"), 0, 0, tiled=True)
+    gathered, near, back = lax.optimization_barrier((gathered, near, back))
     pace = lax.dynamic_slice(
         rate, (lax.axis_index("z"), lax.axis_index("xh") * LANES), (1, LANES)
     )
     scanned = pl.pallas_call(
         functools.partial(scan_kernel, block=2 * block),
         name="scan",
-        out_shape=rows,
+        out_shape=pltpu.VMEM(rows.shape, F32),
         in_specs=[VMEM] * 2,
         out_specs=VMEM,
+        compiler_params=room(4),
     )(gathered, pace)
     returned = lax.all_to_all(scanned, ("xh", "z"), 0, 0, tiled=True)
+    group = lax.axis_size("core") * lax.axis_size("tensor")
     state, state_send, total = pl.pallas_call(
         functools.partial(split_kernel, block=block),
         name="split",
-        out_shape=(tile, tile, struct(pieces, LANES)),
+        out_shape=(tile, tile, struct(group, pieces, LANES)),
         in_specs=[SMEM] + [VMEM] * 4,
         out_specs=(VMEM,) * 3,
+        compiler_params=room(4),
     )(core, returned, keep, other, rate)
     state_other = lax.ppermute(state_send, "core", exchange)
-    group = lax.axis_size("core") * lax.axis_size("tensor")
-    copies = jnp.broadcast_to(total[None], (group,) + total.shape)
-    totals = lax.all_to_all(copies, ("core", "tensor"), 0, 0, tiled=True)
+    totals = lax.all_to_all(total, ("core", "tensor"), 0, 0, tiled=True)
     summed = jnp.sum(totals, axis=0)
     summed = jnp.concatenate([summed[:MODES], summed[MODES:]], axis=1)
     length = block * lax.axis_size(("xh", "z", "core"))
     grad_residue = summed / float(seq_count * length)
-    whole = struct(*query.shape, dtype=jnp.bfloat16)
     mixed, grad_query, grad_key, grad_value = pl.pallas_call(
         final_kernel,
         name="final",
         out_shape=(whole,) * 4,
-        in_specs=[SMEM] + [VMEM] * 10,
-        out_specs=(VMEM,) * 4,
-        scratch_shapes=[pltpu.VMEM((block * 8, LANES), F32)],
-    )(core, query, key, value, grad_out, residue, rate, near, back, state, state_other)
+        in_specs=[SMEM] + [HBM] * 4 + [VMEM] * 6,
+        out_specs=(HBM,) * 4,
+        scratch_shapes=[pltpu.VMEM((block * 8, LANES), F32)] + buffers * 2 + arrivals * 2,
+        compiler_params=room(12),
+    )(core, *inputs, residue, rate, near, back, state, state_other)
     return (mixed, grad_query, grad_key, grad_value, grad_residue)
 
 

time: 101 us -> 89.2 us (0.88)
  waiting for transfers between devices: 18.3 us -> 11 us
  local copies, waits for them, and re-layouts: 4.68 us -> 1.5 us
  Pallas kernels: 24.1 us -> 21.9 us
    all_to_all x1, waiting for transfers between devices: 15.9 us -> 8.84 us  [local(): gathered = lax.all_to_all(joined, ('xh', 'z'), 0, 0, tiled=True)]
    pallas_call x1 -> x2, Pallas kernels: 11.1 us -> 13.8 us  [the longest x1 7.54 us: local(): pl.pallas_call(near_kernel, name='near', out_shape=(works, works), in_spe...]
    pallas_call x1, Pallas kernels: 1.71 us -> 0.14 us  [local(): pl.pallas_call(functools.partial(scan_kernel, block=2 * block), name='sca...]
    broadcast_in_dim x1 -> x0, local copies, waits for them, and re-layouts: 1.44 us -> none  [local(): copies = jnp.broadcast_to(total[None], (group,) + total.shape)]
    pallas_call x1, Pallas kernels: 7.68 us -> 6.24 us  [local(): pl.pallas_call(final_kernel, name='final', out_shape=(whole,) * 4, in_spe...]
    dynamic_slice x1, local copies, waits for them, and re-layouts: 1.28 us -> 0.07 us  [local(): lax.dynamic_slice(rate, (lax.axis_index('z'), lax.axis_index('xh') * LANE...]
    all_to_all x1, blocking collectives: 20.7 us -> 21.7 us  [local(): returned = lax.all_to_all(scanned, ('xh', 'z'), 0, 0, tiled=True)]
  transfers between devices with their start and end apart: 4 -> 4, of which waited for: 3 -> 3; matrix products, arithmetic and copies ran while one was open for 1% -> 0% of each run, Pallas kernels for 8% -> 16%
where the time goes in v2:
time: 89.2 us; the launch traced here: 88.5 us
  starting transfers between devices  31 us (35%)
  Pallas kernels  21.9 us (25%)
  blocking collectives  21.7 us (24%)
  waiting for transfers between devices  11 us (12%)
  local copies, waits for them, and re-layouts  1.5 us (2%)
    all_to_all x1, blocking collectives, local(): returned = lax.all_to_all(scanned, ('xh', 'z'), 0, 0, tiled=True)  21.7 us
    all_to_all x1, starting transfers between devices, local(): gathered = lax.all_to_all(joined, ('xh', 'z'), 0, 0, tiled=True)  12.4 us
    all_to_all x1, waiting for transfers between devices, local(): gathered = lax.all_to_all(joined, ('xh', 'z'), 0, 0, tiled=True)  8.84 us
    ppermute x1, starting transfers between devices, local(): other = lax.ppermute(send, 'core', exchange)  8.75 us
    all_to_all x1, starting transfers between devices, local(): totals = lax.all_to_all(total, ('core', 'tensor'), 0, 0, tiled=True)  7.81 us
    pallas_call x1, Pallas kernels, local(): pl.pallas_call(near_kernel, name='near', out_shape=(works, works), in_spe...  7.54 us
    pallas_call x1, Pallas kernels, local(): pl.pallas_call(sums_kernel, name='sums', out_shape=(tile, tile, struct(pi...  6.26 us
    pallas_call x1, Pallas kernels, local(): pl.pallas_call(final_kernel, name='final', out_shape=(whole,) * 4, in_spe...  6.24 us
  transfers between devices with their start and end apart: 4, of which 3 were waited for; matrix products, arithmetic and copies ran while one was open for 0% of the time, Pallas kernels for 16%

profile of v2, /device:TPU:1, one launch (start us, length us, event | category | flops | bytes accessed | tf_op | source)
XLA Modules:
  0.0 88.5 jit_solution(12473692515662936690)
XLA Ops:
  0.6 0.0 copy-start
  0.6 0.7 copy-done
  1.4 6.3 %sums.1 = (f32[32,8,128]{2,1,0:T(8,128)S(1)}, f32[32,8,128]{2,1,0:T(8,128)S(1)}, f32[32,128]{1,0:T(8,128)S(1)}) custom-call(s32[1]{0:T(128)} %bitcast.core, bf16[2,128,1024]{2,1,0:T(8,128)(2,1)} %query_in.5, bf16[2,128,1024]{2,1,0:T(8,128)(2,1)} %key_in.5, bf16[2,128,1024]{2,1,0:T(8,128)(2,1)} %value_in.5, bf16[2,128,1024]{2,1,0:T(8,128)(2,1)} %grad_in.5, ...), custom_call_target="tpu_custom_call" | custom-call | tf_op jit(solution)/shard_map/sums/pallas_call | solution.py:328
  7.6 8.7 %collective-permute-start = (f32[32,8,128]{2,1,0:T(8,128)S(1)}, f32[32,8,128]{2,1,0:T(8,128)S(1)}, u32[]{:S(2)}, u32[]{:S(2)}) collective-permute-start(f32[32,8,128]{2,1,0:T(8,128)S(1)} %get-tuple-element.21), channel_id=1, source_target_pairs={{0,8},{8,0},{1,9},{9,1},{2,10},{10,2},{3,11},{11,3},{4,12},{12,4},... | collective-permute-start | bytes 393224 | tf_op jit(solution)/shard_map/ppermute | solution.py:348
  16.4 1.0 %collective-permute-done.other = f32[32,8,128]{2,1,0:T(8,128)S(1)} collective-permute-done((f32[32,8,128]{2,1,0:T(8,128)S(1)}, f32[32,8,128]{2,1,0:T(8,128)S(1)}, u32[]{:S(2)}, u32[]{:S(2)}) %collective-permute-start) | collective-permute-done | bytes 131104 | tf_op jit(solution)/shard_map/ppermute | solution.py:348
  17.3 0.8 pair.1
  18.1 0.0 copy-start.2
  18.1 12.4 %all-to-all-start = ((f32[288,1,128]{2,1,0:T(1,128)}), f32[288,1,128]{2,1,0:T(1,128)S(1)}, u32[]{:S(2)}, u32[]{:S(2)}) async-start(f32[288,1,128]{2,1,0:T(1,128)} %pair.1), calls=%async_computation | async-start | bytes 294912 | tf_op jit(solution)/shard_map/all_to_all | solution.py:357
  30.6 0.0 copy-start.1
  30.6 0.7 copy-done.1
  31.3 0.1 dynamic_slice.3.pace
  31.4 0.0 copy-done.2
  31.4 7.5 %near.1 = (f32[2,1024,128]{2,1,0:T(8,128)S(1)}, f32[2,1024,128]{2,1,0:T(8,128)S(1)}) custom-call(bf16[2,128,1024]{2,1,0:T(8,128)(2,1)} %query_in.5, bf16[2,128,1024]{2,1,0:T(8,128)(2,1)} %key_in.5, bf16[2,128,1024]{2,1,0:T(8,128)(2,1)} %value_in.5, bf16[2,128,1024]{2,1,0:T(8,128)(2,1)} %grad_in.5, f32[16,256]{1,0:T(8,128)S(1)} %copy-done.2, ...), custom_call_target="tpu_custom_call" | custom-call | flops 67108864 | bytes 4194304 | tf_op jit(solution)/shard_map/near/pallas_call | solution.py:337
  38.9 8.8 %all-to-all-done.pieces = f32[288,1,128]{2,1,0:T(1,128)S(1)} async-done(((f32[288,1,128]{2,1,0:T(1,128)}), f32[288,1,128]{2,1,0:T(1,128)S(1)}, u32[]{:S(2)}, u32[]{:S(2)}) %all-to-all-start) | async-done | bytes 147488 | tf_op jit(solution)/shard_map/all_to_all | solution.py:357
  47.8 0.1 scan.1
  47.9 21.7 %all_to_all.15.pieces = f32[288,1,128]{2,1,0:T(1,128)S(1)} all-to-all(f32[288,1,128]{2,1,0:T(1,128)S(1)} %scan.1), channel_id=1, replica_groups=mesh['xh'=2,'z'=16,'core'=2,'tensor'=8] {'xh','z'}, dimensions={0} | all-to-all | bytes 294912 | tf_op jit(solution)/shard_map/all_to_all | solution.py:370
  69.6 1.0 %split.1 = (f32[32,8,128]{2,1,0:T(8,128)S(1)}, f32[32,8,128]{2,1,0:T(8,128)S(1)}, f32[16,32,128]{2,1,0:T(8,128)}) custom-call(s32[1]{0:T(128)} %bitcast.core, f32[288,1,128]{2,1,0:T(1,128)S(1)} %all_to_all.15.pieces, f32[32,8,128]{2,1,0:T(8,128)S(1)} %get-tuple-element.20.own, f32[32,8,128]{2,1,0:T(8,128)S(1)} %collective-permute-done.other, ...), custom_call_target="tpu_custom_call" | custom-call | tf_op jit(solution)/shard_map/split/pallas_call | solution.py:372
  70.6 7.8 %all-to-all-start.2 = ((f32[16,32,128]{2,1,0:T(8,128)}), f32[16,32,128]{2,1,0:T(8,128)S(1)}, u32[]{:S(2)}, u32[]{:S(2)}) async-start(f32[16,32,128]{2,1,0:T(8,128)} %get-tuple-element.34), calls=%async_computation.2 | async-start | bytes 524288 | tf_op jit(solution)/shard_map/all_to_all | solution.py:381
  78.4 2.0 %collective-permute-start.1 = (f32[32,8,128]{2,1,0:T(8,128)S(1)}, f32[32,8,128]{2,1,0:T(8,128)S(1)}, u32[]{:S(2)}, u32[]{:S(2)}) collective-permute-start(f32[32,8,128]{2,1,0:T(8,128)S(1)} %get-tuple-element.29), channel_id=1, source_target_pairs={{0,8},{8,0},{1,9},{9,1},{2,10},{10,2},{3,11},{11,3},{4,12},{12,4},... | collective-permute-start | bytes 393224 | tf_op jit(solution)/shard_map/ppermute | solution.py:380
  80.4 1.2 %collective-permute-done.1.other = f32[32,8,128]{2,1,0:T(8,128)S(1)} collective-permute-done((f32[32,8,128]{2,1,0:T(8,128)S(1)}, f32[32,8,128]{2,1,0:T(8,128)S(1)}, u32[]{:S(2)}, u32[]{:S(2)}) %collective-permute-start.1) | collective-permute-done | bytes 131104 | tf_op jit(solution)/shard_map/ppermute | solution.py:380
  81.6 6.2 %final.1 = (bf16[2,128,1024]{2,1,0:T(8,128)(2,1)}, bf16[2,128,1024]{2,1,0:T(8,128)(2,1)}, bf16[2,128,1024]{2,1,0:T(8,128)(2,1)}, bf16[2,128,1024]{2,1,0:T(8,128)(2,1)}) custom-call(s32[1]{0:T(128)} %bitcast.core, bf16[2,128,1024]{2,1,0:T(8,128)(2,1)} %query_in.5, bf16[2,128,1024]{2,1,0:T(8,128)(2,1)} %key_in.5, bf16[2,128,1024]{2,1,0:T(8,128)(2,1)} %value_in.5, ...), custom_call_target="tpu_custom_call" | custom-call | tf_op jit(solution)/shard_map/final/pallas_call | solution.py:386
  87.9 0.0 all-to-all-done.2
  87.9 0.6 maximum_multiply_fusion
  (2 shorter events, 0.0 us)
Async XLA Ops:
  0.6 0.7 copy-start
  7.6 9.7 %collective-permute-start = (f32[32,8,128]{2,1,0:T(8,128)S(1)}, f32[32,8,128]{2,1,0:T(8,128)S(1)}, u32[]{:S(2)}, u32[]{:S(2)}) collective-permute-start(f32[32,8,128]{2,1,0:T(8,128)S(1)} %get-tuple-element.21), channel_id=1, source_target_pairs={{0,8},{8,0},{1,9},{9,1},{2,10},{10,2},{3,11},{11,3},{4,12},{12,4},... | collective-permute-start | bytes 393224 | tf_op jit(solution)/shard_map/ppermute | solution.py:348
  18.1 13.3 %copy-start.2 = (f32[16,256]{1,0:T(8,128)S(1)}, f32[16,256]{1,0:T(8,128)}, u32[]{:S(2)}) copy-start(f32[16,256]{1,0:T(8,128)} %residue.3) | copy-start | bytes 49156
  18.1 29.6 %all-to-all-start = ((f32[288,1,128]{2,1,0:T(1,128)}), f32[288,1,128]{2,1,0:T(1,128)S(1)}, u32[]{:S(2)}, u32[]{:S(2)}) async-start(f32[288,1,128]{2,1,0:T(1,128)} %pair.1), calls=%async_computation | async-start | bytes 294912 | tf_op jit(solution)/shard_map/all_to_all | solution.py:357
  30.6 0.7 copy-start.1
  70.6 17.3 %all-to-all-start.2 = ((f32[16,32,128]{2,1,0:T(8,128)}), f32[16,32,128]{2,1,0:T(8,128)S(1)}, u32[]{:S(2)}, u32[]{:S(2)}) async-start(f32[16,32,128]{2,1,0:T(8,128)} %get-tuple-element.34), calls=%async_computation.2 | async-start | bytes 524288 | tf_op jit(solution)/shard_map/all_to_all | solution.py:381
  78.4 3.2 %collective-permute-start.1 = (f32[32,8,128]{2,1,0:T(8,128)S(1)}, f32[32,8,128]{2,1,0:T(8,128)S(1)}, u32[]{:S(2)}, u32[]{:S(2)}) collective-permute-start(f32[32,8,128]{2,1,0:T(8,128)S(1)} %get-tuple-element.29), channel_id=1, source_target_pairs={{0,8},{8,0},{1,9},{9,1},{2,10},{10,2},{3,11},{11,3},{4,12},{12,4},... | collective-permute-start | bytes 393224 | tf_op jit(solution)/shard_map/ppermute | solution.py:380

commit v3 on v2

--- a/solution.py
+++ b/solution.py
@@ -60,7 +60,9 @@
     key_in,
     value_in,
     grad_in,
-    rate,
+    rate_in,
+    work_u,
+    work_g,
     keep,
     send,
     within,
@@ -68,17 +70,21 @@
     key,
     value,
     grad,
-    work_u,
-    work_g,
+    rate,
     sems,
+    rate_sem,
 ):
     length = query.shape[1]
     repeat = query.shape[2] // (2 * LANES)
     first = core[0] == 0
     pairs = ((key_in, key), (value_in, value), (grad_in, grad), (query_in, query))
-    for half in range(2):
-        fetch(pairs, sems, half, repeat, False)
-    for half in range(2):
+    fetch(pairs, sems, 0, repeat, False)
+    rates = pltpu.make_async_copy(rate_in, rate, rate_sem)
+    rates.start()
+    fetch(pairs, sems, 1, repeat, False)
+    for half in range(2):
+        if half == 0:
+            rates.wait()
         fetch(pairs, sems, half, repeat, True)
         products_of(half, key, value, work_u, repeat)
         products_of(half, grad, query, work_g, repeat)
@@ -102,47 +108,28 @@
             for m in range(8):
                 top_half = jnp.where(low, swap_halves(downs[m]), ups[m])
                 end_half = jnp.where(low, downs[m], swap_halves(ups[m]))
-                piece = half * MODES + group + m
+                piece = 2 * (group + m) + half
                 keep[piece] = jnp.where(first, top_half, end_half)
                 send[piece] = jnp.where(first, end_half, top_half)
                 within[piece : piece + 1, :] = jnp.sum(sums[m], axis=0, keepdims=True)
 
 
-def near_kernel(
-    query_in, key_in, value_in, grad_in, residue, rate, near, back, query, key, value, grad, work_u, work_g, sems
-):
-    length = query.shape[1]
-    repeat = query.shape[2] // (2 * LANES)
-    pairs = ((key_in, key), (value_in, value), (grad_in, grad), (query_in, query))
-    for half in range(2):
-        fetch(pairs, sems, half, repeat, False)
-    for half in range(2):
-        fetch(pairs, sems, half, repeat, True)
-        products_of(half, key, value, work_u, repeat)
-        products_of(half, grad, query, work_g, repeat)
-        for group in range(0, MODES, 8):
-            modes = range(group, group + 8)
-            decay = [spread(jnp.exp(-rate[n : n + 1, lanes_of(half)])) for n in modes]
-            weight = [spread(residue[n : n + 1, lanes_of(half)]) for n in modes]
-
-            def step(i, carry, decay=decay, weight=weight, group=group, half=half):
-                ups, downs = (list(c) for c in carry)
-                ahead = pl.ds(pl.multiple_of(i * 8, 8), 8)
-                behind = pl.ds(pl.multiple_of((length - 1 - i) * 8, 8), 8)
-                u, g = work_u[half, ahead, :], work_g[half, behind, :]
-                for m in range(8):
-                    ups[m] = decay[m] * ups[m] + u
-                    downs[m] = decay[m] * downs[m] + g
-                z = tree([weight[m] * ups[m] for m in range(8)])
-                dz = tree([weight[m] * downs[m] for m in range(8)])
-                if group:
-                    z, dz = z + near[half, ahead, :], dz + back[half, behind, :]
-                near[half, ahead, :] = z
-                back[half, behind, :] = dz
-                return tuple(ups), tuple(downs)
-
-            zero = tuple(jnp.zeros((8, LANES), F32) for _ in range(8))
-            lax.fori_loop(0, length, step, (zero, zero), unroll=2)
+def near_kernel(work_u, work_g, residue, rate, near, back):
+    length = near.shape[1] // 8
+    for half in range(2):
+        decay = [spread(jnp.exp(-rate[n : n + 1, lanes_of(half)])) for n in range(MODES)]
+        weight = [spread(residue[n : n + 1, lanes_of(half)]) for n in range(MODES)]
+        for source, target, reverse in ((work_u, near, False), (work_g, back, True)):
+
+            def step(i, states, half=half, source=source, target=target, reverse=reverse, decay=decay, weight=weight):
+                index = length - 1 - i if reverse else i
+                rows = pl.ds(pl.multiple_of(index * 8, 8), 8)
+                value = source[half, rows, :]
+                states = tuple(decay[n] * states[n] + value for n in range(MODES))
+                target[half, rows, :] = tree([weight[n] * states[n] for n in range(MODES)])
+                return states
+
+            lax.fori_loop(0, length, step, tuple(jnp.zeros((8, LANES), F32) for _ in range(MODES)), unroll=2)
 
 
 def tree(parts):
@@ -160,7 +147,7 @@
     low = bottom()
     for half in range(2):
         for n in range(MODES):
-            piece = half * MODES + n
+            piece = 2 * n + half
             pace = rate[n : n + 1, lanes_of(half)]
             decay = spread(jnp.exp(-pace * float(block)))
             left, right = order(first, own[piece], other[piece])
@@ -172,31 +159,52 @@
             out[piece * ROWS + 8] = within[piece : piece + 1, :] + total
 
 
-def scan_kernel(pieces, pace, out, *, block):
-    count = pieces.shape[0] // ROWS
-    decay = jnp.exp(-pace[...] * float(block))
-    decay4 = jnp.broadcast_to(decay, (4, LANES))
-
-    def load(index, base):
-        return jnp.concatenate([pieces[index * ROWS + base + j] for j in range(4)], axis=0)
-
-    ahead = jnp.zeros((4, LANES), F32)
-    cross = jnp.zeros((4, LANES), F32)
-    local = jnp.zeros((1, LANES), F32)
-    for index in range(count):
-        for j in range(4):
-            out[index * ROWS + j] = ahead[j : j + 1, :]
-        cross = cross + ahead * load(index, 4)
-        local = local + pieces[index * ROWS + 8]
-        ahead = decay4 * ahead + load(index, 0)
-    behind = jnp.zeros((4, LANES), F32)
-    for index in reversed(range(count)):
-        for j in range(4):
-            out[index * ROWS + 4 + j] = behind[j : j + 1, :]
-        behind = decay4 * behind + load(index, 4)
-    total = local + jnp.exp(-pace[...]) * jnp.sum(cross, axis=0, keepdims=True)
-    for index in range(count):
-        out[index * ROWS + 8] = total
+def rows_of(pieces, chip, half, base):
+    start = (2 * chip + half) * ROWS + base
+    return jnp.concatenate([pieces[start + j] for j in range(4)], axis=0)
+
+
+def totals_kernel(part, pieces, pace, out, *, block):
+    count = pieces.shape[0] // (2 * ROWS)
+    early = part[0] == 0
+    for half in range(2):
+        rates = pace[:, lanes_of(half)]
+        decay = jnp.broadcast_to(jnp.exp(-rates * float(block)), (4, LANES))
+        ahead, cross, behind = (jnp.zeros((4, LANES), F32) for _ in range(3))
+        local = jnp.zeros((1, LANES), F32)
+        for chip in range(count):
+            cross = cross + ahead * rows_of(pieces, chip, half, 4)
+            local = local + pieces[(2 * chip + half) * ROWS + 8]
+            ahead = decay * ahead + rows_of(pieces, chip, half, 0)
+        for chip in reversed(range(count)):
+            behind = decay * behind + rows_of(pieces, chip, half, 4)
+        total = local + jnp.exp(-rates) * jnp.sum(cross, axis=0, keepdims=True)
+        out[half, 0:4, :] = jnp.where(early, ahead, behind)
+        out[half, 4:8, :] = jnp.broadcast_to(total, (4, LANES))
+
+
+def scan_kernel(part, pieces, pace, own, other, out, *, block):
+    count = pieces.shape[0] // (2 * ROWS)
+    early = part[0] == 0
+    for half in range(2):
+        rates = pace[:, lanes_of(half)]
+        decay = jnp.broadcast_to(jnp.exp(-rates * float(block)), (4, LANES))
+        given = other[half, 0:4, :]
+        ahead = jnp.where(early, 0.0, given)
+        behind = jnp.where(early, given, 0.0)
+        cross = jnp.sum(own[half, 0:4, :] * given, axis=0, keepdims=True)
+        total = own[half, 4:5, :] + other[half, 4:5, :] + jnp.exp(-rates) * cross
+        for chip in range(count):
+            start = (2 * chip + half) * ROWS
+            for j in range(4):
+                out[start + j] = ahead[j : j + 1, :]
+            out[start + 8] = total
+            ahead = decay * ahead + rows_of(pieces, chip, half, 0)
+        for chip in reversed(range(count)):
+            start = (2 * chip + half) * ROWS + 4
+            for j in range(4):
+                out[start + j] = behind[j : j + 1, :]
+            behind = decay * behind + rows_of(pieces, chip, half, 4)
 
 
 def split_kernel(core, pieces, own, other, rate, keep, send, total, *, block):
@@ -204,7 +212,7 @@
     low = bottom()
     for half in range(2):
         for n in range(MODES):
-            piece = half * MODES + n
+            piece = 2 * n + half
             pace = rate[n : n + 1, lanes_of(half)]
             decay = spread(jnp.exp(-pace * float(block)))
             left, right = order(first, own[piece], other[piece])
@@ -217,7 +225,7 @@
             send[piece] = others
             row = pieces[piece * ROWS + 8]
             for copy in range(total.shape[0]):
-                total[copy, piece : piece + 1, :] = row
+                total[copy, half * MODES + n : half * MODES + n + 1, :] = row
 
 
 def final_kernel(
@@ -272,7 +280,7 @@
     for half in range(2):
         decay, forward, backward = [], [], []
         for n in range(MODES):
-            piece = half * MODES + n
+            piece = 2 * n + half
             weight = spread(residue[n : n + 1, lanes_of(half)])
             decay.append(spread(jnp.exp(-rate[n : n + 1, lanes_of(half)])))
             one, two = order(first, own[piece], other[piece])
@@ -312,11 +320,11 @@
     return jax.ShapeDtypeStruct(shape, dtype)
 
 
-def local(query, key, value, grad_out, residue, rate):
+def staged(query, key, value, grad_out, residue, rate):
     seq_count, block, channels = query.shape
     pieces = 2 * MODES
-    core_id = lax.axis_index("core")
-    core = core_id.astype(jnp.int32).reshape(1)
+    core = lax.axis_index("core").astype(jnp.int32).reshape(1)
+    part = lax.axis_index("xh").astype(jnp.int32).reshape(1)
     tile = struct(pieces, 8, LANES)
     rows = struct(pieces * ROWS, 1, LANES)
     works = struct(2, block * 8, LANES)
@@ -325,25 +333,25 @@
     inputs = tuple(pltpu.with_memory_space_constraint(x, pltpu.HBM) for x in (query, key, value, grad_out))
     buffers = [pltpu.VMEM(query.shape, jnp.bfloat16)] * 4
     arrivals = [pltpu.SemaphoreType.DMA((4, 2, repeat))]
-    keep, send, within = pl.pallas_call(
+    work_u, work_g, keep, send, within = pl.pallas_call(
         sums_kernel,
         name="sums",
-        out_shape=(tile, tile, struct(pieces, LANES)),
-        in_specs=[SMEM] + [HBM] * 4 + [VMEM],
-        out_specs=(VMEM,) * 3,
-        scratch_shapes=buffers + [pltpu.VMEM(works.shape, F32)] * 2 + arrivals,
+        out_shape=(works, works, tile, tile, struct(pieces, LANES)),
+        in_specs=[SMEM] + [HBM] * 5,
+        out_specs=(VMEM,) * 5,
+        scratch_shapes=buffers + [pltpu.VMEM(rate.shape, F32)] + arrivals + [pltpu.SemaphoreType.DMA],
         compiler_params=room(12),
-    )(core, *inputs, rate)
+    )(core, *inputs, pltpu.with_memory_space_constraint(rate, pltpu.HBM))
     near, back = pl.pallas_call(
         near_kernel,
         name="near",
         out_shape=(works, works),
-        in_specs=[HBM] * 4 + [VMEM] * 2,
+        in_specs=[VMEM] * 4,
         out_specs=(VMEM,) * 2,
-        scratch_shapes=buffers + [pltpu.VMEM(works.shape, F32)] * 2 + arrivals,
+        input_output_aliases={0: 0, 1: 1},
         compiler_params=room(12),
         cost_estimate=pl.CostEstimate(flops=2**26, transcendentals=0, bytes_accessed=2**22),
-    )(*inputs, residue, rate)
+    )(work_u, work_g, residue, rate)
     exchange = [(0, 1), (1, 0)]
     other = lax.ppermute(send, "core", exchange)
     joined = pl.pallas_call(
@@ -354,20 +362,27 @@
         out_specs=VMEM,
         compiler_params=room(4),
     )(core, keep, other, within, rate)
-    gathered = lax.all_to_all(joined, ("xh", "z"), 0, 0, tiled=True)
+    gathered = lax.all_to_all(joined, "z", 0, 0, tiled=True)
     gathered, near, back = lax.optimization_barrier((gathered, near, back))
-    pace = lax.dynamic_slice(
-        rate, (lax.axis_index("z"), lax.axis_index("xh") * LANES), (1, LANES)
-    )
+    pace = lax.dynamic_slice(rate, (lax.axis_index("z"), 0), (1, rate.shape[1]))
+    totals = pl.pallas_call(
+        functools.partial(totals_kernel, block=2 * block),
+        name="totals",
+        out_shape=struct(2, 8, LANES),
+        in_specs=[SMEM] + [VMEM] * 2,
+        out_specs=VMEM,
+        compiler_params=room(4),
+    )(part, gathered, pace)
+    totals_other = lax.ppermute(totals, "xh", exchange)
     scanned = pl.pallas_call(
         functools.partial(scan_kernel, block=2 * block),
         name="scan",
         out_shape=pltpu.VMEM(rows.shape, F32),
-        in_specs=[VMEM] * 2,
+        in_specs=[SMEM] + [VMEM] * 4,
         out_specs=VMEM,
         compiler_params=room(4),
-    )(gathered, pace)
-    returned = lax.all_to_all(scanned, ("xh", "z"), 0, 0, tiled=True)
+    )(part, gathered, pace, totals, totals_other)
+    returned = lax.all_to_all(scanned, "z", 0, 0, tiled=True)
     group = lax.axis_size("core") * lax.axis_size("tensor")
     state, state_send, total = pl.pallas_call(
         functools.partial(split_kernel, block=block),
@@ -378,10 +393,10 @@
         compiler_params=room(4),
     )(core, returned, keep, other, rate)
     state_other = lax.ppermute(state_send, "core", exchange)
-    totals = lax.all_to_all(total, ("core", "tensor"), 0, 0, tiled=True)
-    summed = jnp.sum(totals, axis=0)
+    shares = lax.all_to_all(total, ("core", "tensor"), 0, 0, tiled=True)
+    summed = jnp.sum(shares, axis=0)
+    length = block * lax.axis_size(("xh", "z", "core"))
     summed = jnp.concatenate([summed[:MODES], summed[MODES:]], axis=1)
-    length = block * lax.axis_size(("xh", "z", "core"))
     grad_residue = summed / float(seq_count * length)
     mixed, grad_query, grad_key, grad_value = pl.pallas_call(
         final_kernel,
@@ -400,6 +415,4 @@
     split = Mesh(mesh.devices.reshape(shape), ("xh", "z", "core", "tensor"))
     spec = P(None, ("xh", "z", "core"), "tensor")
     specs = (spec, spec, spec, spec)
-    return jax.shard_map(
-        local, mesh=split, in_specs=specs + (P(), P()), out_specs=specs + (P(),), check_vma=False
-    )
+    return jax.shard_map(staged, mesh=split, in_specs=specs + (P(), P()), out_specs=specs + (P(),), check_vma=False)

time: 89.2 us -> 85.9 us (0.963)
  starting transfers between devices: 31 us -> 34.7 us
  blocking collectives: 21.7 us -> 18.9 us
  waiting for transfers between devices: 11 us -> 9.26 us
  Pallas kernels: 21.9 us -> 20.3 us
    ppermute x2 -> x3, starting transfers between devices: 10.8 us -> 15.4 us  [the longest x1 8.75 us: staged(): other = lax.ppermute(send, 'core', exchange)]
    all_to_all x2, waiting for transfers between devices: 8.85 us -> 5.84 us  [the longest x1 5.84 us: staged(): gathered = lax.all_to_all(joined, 'z', 0, 0, tiled=True)]
    all_to_all x1, blocking collectives: 21.7 us -> 18.9 us  [staged(): returned = lax.all_to_all(scanned, 'z', 0, 0, tiled=True)]
    pallas_call x6 -> x7, Pallas kernels: 21.9 us -> 20.3 us  [the longest x1 6.53 us: staged(): pl.pallas_call(sums_kernel, name='sums', out_shape=(works, works, tile, t...]
    ppermute x2 -> x3, waiting for transfers between devices: 2.18 us -> 3.42 us  [the longest x1 1.24 us: staged(): totals_other = lax.ppermute(totals, 'xh', exchange)]
    all_to_all x2, starting transfers between devices: 20.3 us -> 19.3 us  [the longest x1 9.68 us: staged(): shares = lax.all_to_all(total, ('core', 'tensor'), 0, 0, tiled=True)]
  transfers between devices with their start and end apart: 4 -> 5, of which waited for: 3 -> 4; matrix products, arithmetic and copies ran while one was open for 0% -> 0% of each run, Pallas kernels for 16% -> 14%
where the time goes in v3:
time: 85.9 us; the launch traced here: 85.3 us
  starting transfers between devices  34.7 us (40%)
  Pallas kernels  20.3 us (24%)
  blocking collectives  18.9 us (22%)
  waiting for transfers between devices  9.26 us (11%)
    all_to_all x1, blocking collectives, staged(): returned = lax.all_to_all(scanned, 'z', 0, 0, tiled=True)  18.9 us
    all_to_all x1, starting transfers between devices, staged(): shares = lax.all_to_all(total, ('core', 'tensor'), 0, 0, tiled=True)  9.68 us
    all_to_all x1, starting transfers between devices, staged(): gathered = lax.all_to_all(joined, 'z', 0, 0, tiled=True)  9.57 us
    ppermute x1, starting transfers between devices, staged(): other = lax.ppermute(send, 'core', exchange)  8.75 us
    pallas_call x1, Pallas kernels, staged(): pl.pallas_call(sums_kernel, name='sums', out_shape=(works, works, tile, t...  6.53 us
    pallas_call x1, Pallas kernels, staged(): pl.pallas_call(final_kernel, name='final', out_shape=(whole,) * 4, in_spe...  6.24 us
    all_to_all x1, waiting for transfers between devices, staged(): gathered = lax.all_to_all(joined, 'z', 0, 0, tiled=True)  5.84 us
    pallas_call x1, Pallas kernels, staged(): pl.pallas_call(near_kernel, name='near', out_shape=(works, works), in_spe...  5.62 us
  transfers between devices with their start and end apart: 5, of which 4 were waited for; matrix products, arithmetic and copies ran while one was open for 0% of the time, Pallas kernels for 14%

profile of v3, /device:TPU:1, one launch (start us, length us, event | category | flops | bytes accessed | tf_op | source)
XLA Modules:
  0.0 85.3 jit_solution(10388404761101394033)
XLA Ops:
  0.6 0.0 copy-start
  0.6 6.5 %sums.1 = (f32[2,1024,128]{2,1,0:T(8,128)S(1)}, f32[2,1024,128]{2,1,0:T(8,128)S(1)}, f32[32,8,128]{2,1,0:T(8,128)S(1)}, f32[32,8,128]{2,1,0:T(8,128)S(1)}, f32[32,128]{1,0:T(8,128)S(1)}) custom-call(s32[1]{0:T(128)} %bitcast.core, bf16[2,128,1024]{2,1,0:T(8,128)(2,1)} %query_in.3, bf16[2,128,1024]{2,1,0:T(8,128)(2,1)} %key_in.3, ...), custom_call_target="tpu_custom_call" | custom-call | tf_op jit(solution)/shard_map/sums/pallas_call | solution.py:336
  7.2 8.7 %collective-permute-start = (f32[32,8,128]{2,1,0:T(8,128)S(1)}, f32[32,8,128]{2,1,0:T(8,128)S(1)}, u32[]{:S(2)}, u32[]{:S(2)}) collective-permute-start(f32[32,8,128]{2,1,0:T(8,128)S(1)} %get-tuple-element.23), channel_id=1, source_target_pairs={{0,8},{8,0},{1,9},{9,1},{2,10},{10,2},{3,11},{11,3},{4,12},{12,4},... | collective-permute-start | bytes 393224 | tf_op jit(solution)/shard_map/ppermute | solution.py:356
  15.9 1.0 %collective-permute-done.other = f32[32,8,128]{2,1,0:T(8,128)S(1)} collective-permute-done((f32[32,8,128]{2,1,0:T(8,128)S(1)}, f32[32,8,128]{2,1,0:T(8,128)S(1)}, u32[]{:S(2)}, u32[]{:S(2)}) %collective-permute-start) | collective-permute-done | bytes 131104 | tf_op jit(solution)/shard_map/ppermute | solution.py:356
  16.9 0.0 copy-done
  16.9 0.8 pair.1
  17.7 9.6 %all-to-all-start = ((f32[288,1,128]{2,1,0:T(1,128)}), f32[288,1,128]{2,1,0:T(1,128)S(1)}, u32[]{:S(2)}, u32[]{:S(2)}) async-start(f32[288,1,128]{2,1,0:T(1,128)} %pair.1), calls=%async_computation | async-start | bytes 294912 | tf_op jit(solution)/shard_map/all_to_all | solution.py:365
  27.3 0.0 copy-start.1
  27.3 0.7 copy-done.1
  28.0 5.6 %near.1 = (f32[2,1024,128]{2,1,0:T(8,128)S(1)}, f32[2,1024,128]{2,1,0:T(8,128)S(1)}) custom-call(f32[2,1024,128]{2,1,0:T(8,128)S(1)} %get-tuple-element.25.work_u, f32[2,1024,128]{2,1,0:T(8,128)S(1)} %get-tuple-element.26.work_g, f32[16,256]{1,0:T(8,128)S(1)} %copy-done.1, f32[16,256]{1,0:T(8,128)S(1)} %copy-done), custom_call_target="tpu_custom_call", output_to_operand_aliasing={{0}: (0, {}), {1}: (1, {})} | custom-call | flops 67108864 | bytes 4194304 | tf_op jit(solution)/shard_map/near/pallas_call | solution.py:345
  33.6 5.8 %all-to-all-done.pieces = f32[288,1,128]{2,1,0:T(1,128)S(1)} async-done(((f32[288,1,128]{2,1,0:T(1,128)}), f32[288,1,128]{2,1,0:T(1,128)S(1)}, u32[]{:S(2)}, u32[]{:S(2)}) %all-to-all-start) | async-done | bytes 147488 | tf_op jit(solution)/shard_map/all_to_all | solution.py:365
  39.5 0.1 totals.1.own
  39.6 4.6 %collective-permute-start.1 = (f32[2,8,128]{2,1,0:T(8,128)S(1)}, f32[2,8,128]{2,1,0:T(8,128)S(1)}, u32[]{:S(2)}, u32[]{:S(2)}) collective-permute-start(f32[2,8,128]{2,1,0:T(8,128)S(1)} %totals.1.own), channel_id=1, source_target_pairs={{0,256},{256,0},{1,257},{257,1},{2,258},{258,2},{3,259},{259,3},{4... | collective-permute-start | bytes 24584 | tf_op jit(solution)/shard_map/ppermute | solution.py:376
  44.2 1.2 %collective-permute-done.1.other = f32[2,8,128]{2,1,0:T(8,128)S(1)} collective-permute-done((f32[2,8,128]{2,1,0:T(8,128)S(1)}, f32[2,8,128]{2,1,0:T(8,128)S(1)}, u32[]{:S(2)}, u32[]{:S(2)}) %collective-permute-start.1) | collective-permute-done | bytes 8224 | tf_op jit(solution)/shard_map/ppermute | solution.py:376
  45.5 0.1 scan.1
  45.5 18.9 %all_to_all.15.pieces = f32[288,1,128]{2,1,0:T(1,128)S(1)} all-to-all(f32[288,1,128]{2,1,0:T(1,128)S(1)} %scan.1), channel_id=1, replica_groups=mesh['xh'=2,'z'=16,'core'=2,'tensor'=8] {'z'}, dimensions={0} | all-to-all | bytes 294912 | tf_op jit(solution)/shard_map/all_to_all | solution.py:385
  64.5 1.0 %split.1 = (f32[32,8,128]{2,1,0:T(8,128)S(1)}, f32[32,8,128]{2,1,0:T(8,128)S(1)}, f32[16,32,128]{2,1,0:T(8,128)}) custom-call(s32[1]{0:T(128)} %bitcast.core, f32[288,1,128]{2,1,0:T(1,128)S(1)} %all_to_all.15.pieces, f32[32,8,128]{2,1,0:T(8,128)S(1)} %get-tuple-element.22.own, f32[32,8,128]{2,1,0:T(8,128)S(1)} %collective-permute-done.other, ...), custom_call_target="tpu_custom_call" | custom-call | tf_op jit(solution)/shard_map/split/pallas_call | solution.py:387
  65.5 9.7 %all-to-all-start.2 = ((f32[16,32,128]{2,1,0:T(8,128)}), f32[16,32,128]{2,1,0:T(8,128)S(1)}, u32[]{:S(2)}, u32[]{:S(2)}) async-start(f32[16,32,128]{2,1,0:T(8,128)} %get-tuple-element.38), calls=%async_computation.2 | async-start | bytes 524288 | tf_op jit(solution)/shard_map/all_to_all | solution.py:396
  75.2 2.0 %collective-permute-start.2 = (f32[32,8,128]{2,1,0:T(8,128)S(1)}, f32[32,8,128]{2,1,0:T(8,128)S(1)}, u32[]{:S(2)}, u32[]{:S(2)}) collective-permute-start(f32[32,8,128]{2,1,0:T(8,128)S(1)} %get-tuple-element.33), channel_id=1, source_target_pairs={{0,8},{8,0},{1,9},{9,1},{2,10},{10,2},{3,11},{11,3},{4,12},{12,4},... | collective-permute-start | bytes 393224 | tf_op jit(solution)/shard_map/ppermute | solution.py:395
  77.2 1.2 %collective-permute-done.2.other = f32[32,8,128]{2,1,0:T(8,128)S(1)} collective-permute-done((f32[32,8,128]{2,1,0:T(8,128)S(1)}, f32[32,8,128]{2,1,0:T(8,128)S(1)}, u32[]{:S(2)}, u32[]{:S(2)}) %collective-permute-start.2) | collective-permute-done | bytes 131104 | tf_op jit(solution)/shard_map/ppermute | solution.py:395
  78.4 6.2 %final.1 = (bf16[2,128,1024]{2,1,0:T(8,128)(2,1)}, bf16[2,128,1024]{2,1,0:T(8,128)(2,1)}, bf16[2,128,1024]{2,1,0:T(8,128)(2,1)}, bf16[2,128,1024]{2,1,0:T(8,128)(2,1)}) custom-call(s32[1]{0:T(128)} %bitcast.core, bf16[2,128,1024]{2,1,0:T(8,128)(2,1)} %query_in.3, bf16[2,128,1024]{2,1,0:T(8,128)(2,1)} %key_in.3, bf16[2,128,1024]{2,1,0:T(8,128)(2,1)} %value_in.3, ...), custom_call_target="tpu_custom_call" | custom-call | tf_op jit(solution)/shard_map/final/pallas_call | solution.py:401
  84.6 0.0 all-to-all-done.2
  84.7 0.6 maximum_multiply_fusion
  (3 shorter events, 0.0 us)
Async XLA Ops:
  0.6 16.3 %copy-start = (f32[16,256]{1,0:T(8,128)S(1)}, f32[16,256]{1,0:T(8,128)}, u32[]{:S(2)}) copy-start(f32[16,256]{1,0:T(8,128)} %rate.7) | copy-start | bytes 49156
  7.2 9.7 %collective-permute-start = (f32[32,8,128]{2,1,0:T(8,128)S(1)}, f32[32,8,128]{2,1,0:T(8,128)S(1)}, u32[]{:S(2)}, u32[]{:S(2)}) collective-permute-start(f32[32,8,128]{2,1,0:T(8,128)S(1)} %get-tuple-element.23), channel_id=1, source_target_pairs={{0,8},{8,0},{1,9},{9,1},{2,10},{10,2},{3,11},{11,3},{4,12},{12,4},... | collective-permute-start | bytes 393224 | tf_op jit(solution)/shard_map/ppermute | solution.py:356
  17.7 21.8 %all-to-all-start = ((f32[288,1,128]{2,1,0:T(1,128)}), f32[288,1,128]{2,1,0:T(1,128)S(1)}, u32[]{:S(2)}, u32[]{:S(2)}) async-start(f32[288,1,128]{2,1,0:T(1,128)} %pair.1), calls=%async_computation | async-start | bytes 294912 | tf_op jit(solution)/shard_map/all_to_all | solution.py:365
  27.3 0.7 copy-start.1
  39.6 5.9 %collective-permute-start.1 = (f32[2,8,128]{2,1,0:T(8,128)S(1)}, f32[2,8,128]{2,1,0:T(8,128)S(1)}, u32[]{:S(2)}, u32[]{:S(2)}) collective-permute-start(f32[2,8,128]{2,1,0:T(8,128)S(1)} %totals.1.own), channel_id=1, source_target_pairs={{0,256},{256,0},{1,257},{257,1},{2,258},{258,2},{3,259},{259,3},{4... | collective-permute-start | bytes 24584 | tf_op jit(solution)/shard_map/ppermute | solution.py:376
  65.5 19.2 %all-to-all-start.2 = ((f32[16,32,128]{2,1,0:T(8,128)}), f32[16,32,128]{2,1,0:T(8,128)S(1)}, u32[]{:S(2)}, u32[]{:S(2)}) async-start(f32[16,32,128]{2,1,0:T(8,128)} %get-tuple-element.38), calls=%async_computation.2 | async-start | bytes 524288 | tf_op jit(solution)/shard_map/all_to_all | solution.py:396
  75.2 3.2 %collective-permute-start.2 = (f32[32,8,128]{2,1,0:T(8,128)S(1)}, f32[32,8,128]{2,1,0:T(8,128)S(1)}, u32[]{:S(2)}, u32[]{:S(2)}) collective-permute-start(f32[32,8,128]{2,1,0:T(8,128)S(1)} %get-tuple-element.33), channel_id=1, source_target_pairs={{0,8},{8,0},{1,9},{9,1},{2,10},{10,2},{3,11},{11,3},{4,12},{12,4},... | collective-permute-start | bytes 393224 | tf_op jit(solution)/shard_map/ppermute | solution.py:395

commit v4 on v3

--- a/solution.py
+++ b/solution.py
@@ -10,11 +10,18 @@
 F32 = jnp.float32
 LANES = 128
 MODES = 16
+STEP = 4
+WAVE = 4
+SHARE = 10
 ROWS = 9
 
 
 def spread(row):
     return jnp.broadcast_to(row, (8, LANES))
+
+
+def first_core(seat, members):
+    return lax.rem(seat[0], members // 2) < members // 4
 
 
 def bottom():
@@ -55,7 +62,7 @@
 
 
 def sums_kernel(
-    core,
+    seat,
     query_in,
     key_in,
     value_in,
@@ -73,10 +80,12 @@
     rate,
     sems,
     rate_sem,
+    *,
+    members,
 ):
     length = query.shape[1]
     repeat = query.shape[2] // (2 * LANES)
-    first = core[0] == 0
+    first = first_core(seat, members)
     pairs = ((key_in, key), (value_in, value), (grad_in, grad), (query_in, query))
     fetch(pairs, sems, 0, repeat, False)
     rates = pltpu.make_async_copy(rate_in, rate, rate_sem)
@@ -88,30 +97,51 @@
         fetch(pairs, sems, half, repeat, True)
         products_of(half, key, value, work_u, repeat)
         products_of(half, grad, query, work_g, repeat)
-        for group in range(0, MODES, 8):
-            decay = [spread(jnp.exp(-rate[n : n + 1, lanes_of(half)])) for n in range(group, group + 8)]
-
-            def step(i, carry, decay=decay, half=half):
-                ups, downs, sums = (list(c) for c in carry)
-                ahead = pl.ds(pl.multiple_of(i * 8, 8), 8)
-                behind = pl.ds(pl.multiple_of((length - 1 - i) * 8, 8), 8)
-                u, g, gr = work_u[half, ahead, :], work_g[half, ahead, :], work_g[half, behind, :]
-                for m in range(8):
-                    ups[m] = decay[m] * ups[m] + u
-                    downs[m] = decay[m] * downs[m] + gr
-                    sums[m] = sums[m] + g * ups[m]
-                return tuple(ups), tuple(downs), tuple(sums)
-
-            zero = tuple(jnp.zeros((8, LANES), F32) for _ in range(8))
-            ups, downs, sums = lax.fori_loop(0, length, step, (zero, zero, zero), unroll=4)
+        lags = None
+        for group in range(0, MODES, WAVE):
+            modes = range(group, group + WAVE)
+            decay = [spread(jnp.exp(-rate[n : n + 1, lanes_of(half)])) for n in modes]
+            jump = [spread(jnp.exp(-rate[n : n + 1, lanes_of(half)] * float(STEP))) for n in modes]
+
+            def step(i, carry, decay=decay, jump=jump, half=half):
+                ups, downs, powers, sums, pairs = (list(c) for c in carry)
+                base = i * (8 * STEP)
+                rows = [pl.ds(pl.multiple_of(base + 8 * j, 8), 8) for j in range(STEP)]
+                us = [work_u[half, row, :] for row in rows]
+                gs = [work_g[half, row, :] for row in rows]
+                for lag in range(len(pairs)):
+                    for j in range(lag, STEP):
+                        pairs[lag] = pairs[lag] + gs[j] * us[j - lag]
+                for m in range(WAVE):
+                    risen, fallen = us[0], gs[-1]
+                    for j in range(1, STEP):
+                        risen = decay[m] * risen + us[j]
+                        fallen = decay[m] * fallen + gs[STEP - 1 - j]
+                    sums[m] = sums[m] + fallen * ups[m]
+                    ups[m] = jump[m] * ups[m] + risen
+                    downs[m] = downs[m] + powers[m] * fallen
+                    powers[m] = powers[m] * jump[m]
+                return tuple(ups), tuple(downs), tuple(powers), tuple(sums), tuple(pairs)
+
+            zero = tuple(jnp.zeros((8, LANES), F32) for _ in range(WAVE))
+            ones = tuple(jnp.ones((8, LANES), F32) for _ in range(WAVE))
+            none = () if lags else tuple(jnp.zeros((8, LANES), F32) for _ in range(STEP))
+            ups, downs, _, sums, pairs_of = lax.fori_loop(
+                0, length // STEP, step, (zero, zero, ones, zero, none), unroll=2
+            )
+            lags = lags or pairs_of
             low = bottom()
-            for m in range(8):
+            for m in range(WAVE):
                 top_half = jnp.where(low, swap_halves(downs[m]), ups[m])
                 end_half = jnp.where(low, downs[m], swap_halves(ups[m]))
                 piece = 2 * (group + m) + half
                 keep[piece] = jnp.where(first, top_half, end_half)
                 send[piece] = jnp.where(first, end_half, top_half)
-                within[piece : piece + 1, :] = jnp.sum(sums[m], axis=0, keepdims=True)
+                inner = lags[-1]
+                for lag in reversed(range(STEP - 1)):
+                    inner = decay[m] * inner + lags[lag]
+                inner = inner + decay[m] * sums[m]
+                within[piece : piece + 1, :] = jnp.sum(inner, axis=0, keepdims=True)
 
 
 def near_kernel(work_u, work_g, residue, rate, near, back):
@@ -142,8 +172,8 @@
     return jnp.where(first, own, other), jnp.where(first, other, own)
 
 
-def pair_kernel(core, own, other, within, rate, out, *, block):
-    first = core[0] == 0
+def pair_kernel(seat, own, other, within, rate, out, *, block, members):
+    first = first_core(seat, members)
     low = bottom()
     for half in range(2):
         for n in range(MODES):
@@ -164,9 +194,9 @@
     return jnp.concatenate([pieces[start + j] for j in range(4)], axis=0)
 
 
-def totals_kernel(part, pieces, pace, out, *, block):
+def totals_kernel(seat, pieces, pace, out, *, block, members):
     count = pieces.shape[0] // (2 * ROWS)
-    early = part[0] == 0
+    early = seat[0] < members // 2
     for half in range(2):
         rates = pace[:, lanes_of(half)]
         decay = jnp.broadcast_to(jnp.exp(-rates * float(block)), (4, LANES))
@@ -179,21 +209,32 @@
         for chip in reversed(range(count)):
             behind = decay * behind + rows_of(pieces, chip, half, 4)
         total = local + jnp.exp(-rates) * jnp.sum(cross, axis=0, keepdims=True)
-        out[half, 0:4, :] = jnp.where(early, ahead, behind)
-        out[half, 4:8, :] = jnp.broadcast_to(total, (4, LANES))
-
-
-def scan_kernel(part, pieces, pace, own, other, out, *, block):
+        shown = jnp.where(early, ahead, behind)
+        for copy in range(out.shape[0] // SHARE):
+            for j in range(4):
+                out[copy * SHARE + 4 * half + j] = shown[j : j + 1, :]
+            out[copy * SHARE + 8 + half] = total
+
+
+def scan_kernel(seat, pieces, pace, shares, out, *, block, members):
     count = pieces.shape[0] // (2 * ROWS)
-    early = part[0] == 0
+    pairs = shares.shape[0] // (2 * SHARE)
+    early = seat[0] < members // 2
+    source = lax.rem(seat[0] + members // 2, members) * SHARE
     for half in range(2):
         rates = pace[:, lanes_of(half)]
         decay = jnp.broadcast_to(jnp.exp(-rates * float(block)), (4, LANES))
-        given = other[half, 0:4, :]
+        given = jnp.concatenate([shares[source + 4 * half + j] for j in range(4)], axis=0)
         ahead = jnp.where(early, 0.0, given)
         behind = jnp.where(early, given, 0.0)
-        cross = jnp.sum(own[half, 0:4, :] * given, axis=0, keepdims=True)
-        total = own[half, 4:5, :] + other[half, 4:5, :] + jnp.exp(-rates) * cross
+        cross = jnp.zeros((1, LANES), F32)
+        total = jnp.zeros((1, LANES), F32)
+        for one in range(pairs):
+            two = one + pairs
+            total = total + (shares[one * SHARE + 8 + half] + shares[two * SHARE + 8 + half])
+            for j in range(4 * half, 4 * half + 4):
+                cross = cross + shares[one * SHARE + j] * shares[two * SHARE + j]
+        total = total + jnp.exp(-rates) * cross
         for chip in range(count):
             start = (2 * chip + half) * ROWS
             for j in range(4):
@@ -207,8 +248,8 @@
             behind = decay * behind + rows_of(pieces, chip, half, 4)
 
 
-def split_kernel(core, pieces, own, other, rate, keep, send, total, *, block):
-    first = core[0] == 0
+def split_kernel(seat, pieces, own, other, rate, keep, send, *, block, members):
+    first = first_core(seat, members)
     low = bottom()
     for half in range(2):
         for n in range(MODES):
@@ -223,48 +264,49 @@
             mine, others = order(first, for_left, for_right)
             keep[piece] = mine
             send[piece] = others
-            row = pieces[piece * ROWS + 8]
-            for copy in range(total.shape[0]):
-                total[copy, half * MODES + n : half * MODES + n + 1, :] = row
 
 
 def final_kernel(
-    core,
-    query_in,
-    key_in,
-    value_in,
-    grad_in,
+    seat,
+    query,
+    key,
+    value,
+    grad,
     residue,
     rate,
     near,
     back,
     own,
     other,
+    pieces,
     mixed_out,
     grad_query_out,
     grad_key_out,
     grad_value_out,
+    grad_residue_out,
     work,
-    query,
-    key,
-    value,
-    grad,
     mixed,
     grad_query,
     grad_key,
     grad_value,
-    in_sems,
+    grad_residue,
     sems,
+    residue_sem,
+    *,
+    scale,
+    members,
 ):
     length = query.shape[1]
     repeat = query.shape[2] // (2 * LANES)
-    first = core[0] == 0
+    first = first_core(seat, members)
     low = bottom()
     outs = ((mixed, mixed_out), (grad_query, grad_query_out), (grad_key, grad_key_out), (grad_value, grad_value_out))
 
-    pairs = ((query_in, query), (grad_in, grad), (value_in, value), (key_in, key))
-    for half in range(2):
-        fetch(pairs, in_sems, half, repeat, False)
+    for half in range(2):
+        for n in range(MODES):
+            grad_residue[n : n + 1, lanes_of(half)] = pieces[(2 * n + half) * ROWS + 8] * scale
+    residue_copy = pltpu.make_async_copy(grad_residue, grad_residue_out, residue_sem)
+    residue_copy.start()
 
     def products(half, source_a, source_b, base):
         target_a, target_b = outs[base][0], outs[base + 1][0]
@@ -297,7 +339,6 @@
             return step(length - 1 - i, carry, source=back)
 
         lax.fori_loop(0, length, step, tuple(forward), unroll=2)
-        fetch(pairs, in_sems, half, repeat, True)
         products(half, query, grad, 0)
         lax.fori_loop(0, length, step_back, tuple(backward), unroll=2)
         products(half, value, key, 2)
@@ -305,6 +346,7 @@
         for half in range(2):
             for rep in range(repeat):
                 slab_copy(*outs[which], sems, which, half, rep).wait()
+    residue_copy.wait()
 
 
 VMEM = pl.BlockSpec(memory_space=pltpu.VMEM)
@@ -320,11 +362,12 @@
     return jax.ShapeDtypeStruct(shape, dtype)
 
 
-def staged(query, key, value, grad_out, residue, rate):
+def local(query, key, value, grad_out, residue, rate):
     seq_count, block, channels = query.shape
     pieces = 2 * MODES
-    core = lax.axis_index("core").astype(jnp.int32).reshape(1)
-    part = lax.axis_index("xh").astype(jnp.int32).reshape(1)
+    owners = ("xh", "core", "tensor")
+    members = lax.axis_size(owners)
+    seat = lax.axis_index(owners).astype(jnp.int32).reshape(1)
     tile = struct(pieces, 8, LANES)
     rows = struct(pieces * ROWS, 1, LANES)
     works = struct(2, block * 8, LANES)
@@ -334,14 +377,14 @@
     buffers = [pltpu.VMEM(query.shape, jnp.bfloat16)] * 4
     arrivals = [pltpu.SemaphoreType.DMA((4, 2, repeat))]
     work_u, work_g, keep, send, within = pl.pallas_call(
-        sums_kernel,
+        functools.partial(sums_kernel, members=members),
         name="sums",
         out_shape=(works, works, tile, tile, struct(pieces, LANES)),
         in_specs=[SMEM] + [HBM] * 5,
         out_specs=(VMEM,) * 5,
         scratch_shapes=buffers + [pltpu.VMEM(rate.shape, F32)] + arrivals + [pltpu.SemaphoreType.DMA],
         compiler_params=room(12),
-    )(core, *inputs, pltpu.with_memory_space_constraint(rate, pltpu.HBM))
+    )(seat, *inputs, pltpu.with_memory_space_constraint(rate, pltpu.HBM))
     near, back = pl.pallas_call(
         near_kernel,
         name="near",
@@ -355,59 +398,57 @@
     exchange = [(0, 1), (1, 0)]
     other = lax.ppermute(send, "core", exchange)
     joined = pl.pallas_call(
-        functools.partial(pair_kernel, block=block),
+        functools.partial(pair_kernel, block=block, members=members),
         name="pair",
         out_shape=rows,
         in_specs=[SMEM] + [VMEM] * 4,
         out_specs=VMEM,
         compiler_params=room(4),
-    )(core, keep, other, within, rate)
+    )(seat, keep, other, within, rate)
     gathered = lax.all_to_all(joined, "z", 0, 0, tiled=True)
     gathered, near, back = lax.optimization_barrier((gathered, near, back))
     pace = lax.dynamic_slice(rate, (lax.axis_index("z"), 0), (1, rate.shape[1]))
-    totals = pl.pallas_call(
-        functools.partial(totals_kernel, block=2 * block),
+    shown = pl.pallas_call(
+        functools.partial(totals_kernel, block=2 * block, members=members),
         name="totals",
-        out_shape=struct(2, 8, LANES),
+        out_shape=pltpu.VMEM((members * SHARE, 1, LANES), F32),
         in_specs=[SMEM] + [VMEM] * 2,
         out_specs=VMEM,
         compiler_params=room(4),
-    )(part, gathered, pace)
-    totals_other = lax.ppermute(totals, "xh", exchange)
+    )(seat, gathered, pace)
+    shares = lax.all_to_all(shown, owners, 0, 0, tiled=True)
     scanned = pl.pallas_call(
-        functools.partial(scan_kernel, block=2 * block),
+        functools.partial(scan_kernel, block=2 * block, members=members),
         name="scan",
         out_shape=pltpu.VMEM(rows.shape, F32),
-        in_specs=[SMEM] + [VMEM] * 4,
+        in_specs=[SMEM] + [VMEM] * 3,
         out_specs=VMEM,
         compiler_params=room(4),
-    )(part, gathered, pace, totals, totals_other)
+    )(seat, gathered, pace, shares)
     returned = lax.all_to_all(scanned, "z", 0, 0, tiled=True)
-    group = lax.axis_size("core") * lax.axis_size("tensor")
-    state, state_send, total = pl.pallas_call(
-        functools.partial(split_kernel, block=block),
+    state, state_send = pl.pallas_call(
+        functools.partial(split_kernel, block=block, members=members),
         name="split",
-        out_shape=(tile, tile, struct(group, pieces, LANES)),
+        out_shape=(tile, tile),
         in_specs=[SMEM] + [VMEM] * 4,
-        out_specs=(VMEM,) * 3,
+        out_specs=(VMEM,) * 2,
         compiler_params=room(4),
-    )(core, returned, keep, other, rate)
+    )(seat, returned, keep, other, rate)
     state_other = lax.ppermute(state_send, "core", exchange)
-    shares = lax.all_to_all(total, ("core", "tensor"), 0, 0, tiled=True)
-    summed = jnp.sum(shares, axis=0)
     length = block * lax.axis_size(("xh", "z", "core"))
-    summed = jnp.concatenate([summed[:MODES], summed[MODES:]], axis=1)
-    grad_residue = summed / float(seq_count * length)
-    mixed, grad_query, grad_key, grad_value = pl.pallas_call(
-        final_kernel,
+    return pl.pallas_call(
+        functools.partial(final_kernel, scale=1.0 / float(seq_count * length), members=members),
         name="final",
-        out_shape=(whole,) * 4,
-        in_specs=[SMEM] + [HBM] * 4 + [VMEM] * 6,
-        out_specs=(HBM,) * 4,
-        scratch_shapes=[pltpu.VMEM((block * 8, LANES), F32)] + buffers * 2 + arrivals * 2,
+        out_shape=(whole,) * 4 + (struct(*residue.shape),),
+        in_specs=[SMEM] + [VMEM] * 11,
+        out_specs=(HBM,) * 5,
+        scratch_shapes=[pltpu.VMEM((block * 8, LANES), F32)]
+        + buffers
+        + [pltpu.VMEM(residue.shape, F32)]
+        + arrivals
+        + [pltpu.SemaphoreType.DMA],
         compiler_params=room(12),
-    )(core, *inputs, residue, rate, near, back, state, state_other)
-    return (mixed, grad_query, grad_key, grad_value, grad_residue)
+    )(seat, query, key, value, grad_out, residue, rate, near, back, state, state_other, returned)
 
 
 def solution(mesh):
@@ -415,4 +456,6 @@
     split = Mesh(mesh.devices.reshape(shape), ("xh", "z", "core", "tensor"))
     spec = P(None, ("xh", "z", "core"), "tensor")
     specs = (spec, spec, spec, spec)
-    return jax.shard_map(staged, mesh=split, in_specs=specs + (P(), P()), out_specs=specs + (P(),), check_vma=False)
+    return jax.shard_map(
+        local, mesh=split, in_specs=specs + (P(), P()), out_specs=specs + (P(),), check_vma=False
+    )

time: 85.9 us -> 87.2 us (1.015)
  blocking collectives: 18.9 us -> 34.8 us
  starting transfers between devices: 34.7 us -> 24.3 us
  Pallas kernels: 20.3 us -> 18.4 us
    all_to_all x1 -> x2, blocking collectives: 18.9 us -> 34.8 us  [the longest x1 18.7 us: local(): shares = lax.all_to_all(shown, owners, 0, 0, tiled=True)]
    all_to_all x2 -> x1, starting transfers between devices: 19.3 us -> 9.7 us  [local(): gathered = lax.all_to_all(joined, 'z', 0, 0, tiled=True)]
    pallas_call x7, Pallas kernels: 20.3 us -> 18.4 us  [the longest x1 5.94 us: local(): pl.pallas_call(functools.partial(sums_kernel, members=members), name='sum...]
    ppermute x3 -> x2, waiting for transfers between devices: 3.42 us -> 1.93 us  [the longest x1 0.96 us: local(): other = lax.ppermute(send, 'core', exchange)]
    ppermute x3 -> x2, starting transfers between devices: 15.4 us -> 14.6 us  [the longest x1 8.75 us: local(): other = lax.ppermute(send, 'core', exchange)]
    all_to_all x2 -> x1, waiting for transfers between devices: 5.84 us -> 6.53 us  [local(): gathered = lax.all_to_all(joined, 'z', 0, 0, tiled=True)]
  transfers between devices with their start and end apart: 5 -> 3, of which waited for: 4 -> 3; matrix products, arithmetic and copies ran while one was open for 0% -> 0% of each run, Pallas kernels for 14% -> 6%
where the time goes in v4:
time: 87.2 us; the launch traced here: 86.8 us
  blocking collectives  34.8 us (40%)
  starting transfers between devices  24.3 us (28%)
  Pallas kernels  18.4 us (21%)
  waiting for transfers between devices  8.46 us (10%)
    all_to_all x1, blocking collectives, local(): shares = lax.all_to_all(shown, owners, 0, 0, tiled=True)  18.7 us
    all_to_all x1, blocking collectives, local(): returned = lax.all_to_all(scanned, 'z', 0, 0, tiled=True)  16.1 us
    all_to_all x1, starting transfers between devices, local(): gathered = lax.all_to_all(joined, 'z', 0, 0, tiled=True)  9.7 us
    ppermute x1, starting transfers between devices, local(): other = lax.ppermute(send, 'core', exchange)  8.75 us
    all_to_all x1, waiting for transfers between devices, local(): gathered = lax.all_to_all(joined, 'z', 0, 0, tiled=True)  6.53 us
    pallas_call x1, Pallas kernels, local(): pl.pallas_call(functools.partial(sums_kernel, members=members), name='sum...  5.94 us
    ppermute x1, starting transfers between devices, local(): state_other = lax.ppermute(state_send, 'core', exchange)  5.85 us
    pallas_call x1, Pallas kernels, local(): pl.pallas_call(functools.partial(final_kernel, scale=1.0 / float(seq_coun...  5.68 us
  transfers between devices with their start and end apart: 3, of which 3 were waited for; matrix products, arithmetic and copies ran while one was open for 0% of the time, Pallas kernels for 6%

profile of v4, /device:TPU:1, one launch (start us, length us, event | category | flops | bytes accessed | tf_op | source)
XLA Modules:
  0.0 86.8 jit_solution(18423087611925977090)
XLA Ops:
  0.6 0.0 copy-start.4
  0.7 5.9 %sums.1 = (f32[2,1024,128]{2,1,0:T(8,128)S(1)}, f32[2,1024,128]{2,1,0:T(8,128)S(1)}, f32[32,8,128]{2,1,0:T(8,128)S(1)}, f32[32,8,128]{2,1,0:T(8,128)S(1)}, f32[32,128]{1,0:T(8,128)S(1)}) custom-call(s32[1]{0:T(128)} %bitcast.seat, bf16[2,128,1024]{2,1,0:T(8,128)(2,1)} %query.1, bf16[2,128,1024]{2,1,0:T(8,128)(2,1)} %key.1, bf16[2,128,1024]{2,1,0:T(8,128)(2,1)} %value.1, ...), custom_call_target="tpu_custom_call" | custom-call | tf_op jit(solution)/shard_map/sums/pallas_call | solution.py:379
  6.6 8.7 %collective-permute-start = (f32[32,8,128]{2,1,0:T(8,128)S(1)}, f32[32,8,128]{2,1,0:T(8,128)S(1)}, u32[]{:S(2)}, u32[]{:S(2)}) collective-permute-start(f32[32,8,128]{2,1,0:T(8,128)S(1)} %get-tuple-element.18), channel_id=1, source_target_pairs={{0,8},{8,0},{1,9},{9,1},{2,10},{10,2},{3,11},{11,3},{4,12},{12,4},... | collective-permute-start | bytes 393224 | tf_op jit(solution)/shard_map/ppermute | solution.py:399
  15.4 1.0 %collective-permute-done.other = f32[32,8,128]{2,1,0:T(8,128)S(1)} collective-permute-done((f32[32,8,128]{2,1,0:T(8,128)S(1)}, f32[32,8,128]{2,1,0:T(8,128)S(1)}, u32[]{:S(2)}, u32[]{:S(2)}) %collective-permute-start) | collective-permute-done | bytes 131104 | tf_op jit(solution)/shard_map/ppermute | solution.py:399
  16.3 0.0 copy-done.4
  16.3 0.8 pair.1
  17.1 0.0 copy-start.5
  17.1 9.7 %all-to-all-start = ((f32[288,1,128]{2,1,0:T(1,128)}), f32[288,1,128]{2,1,0:T(1,128)S(1)}, u32[]{:S(2)}, u32[]{:S(2)}) async-start(f32[288,1,128]{2,1,0:T(1,128)} %pair.1), calls=%async_computation | async-start | bytes 294912 | tf_op jit(solution)/shard_map/all_to_all | solution.py:408
  26.8 0.0 copy-done.5
  26.8 0.0 copy-start.3
  26.8 5.6 %near.1 = (f32[2,1024,128]{2,1,0:T(8,128)S(1)}, f32[2,1024,128]{2,1,0:T(8,128)S(1)}) custom-call(f32[2,1024,128]{2,1,0:T(8,128)S(1)} %get-tuple-element.20.work_u, f32[2,1024,128]{2,1,0:T(8,128)S(1)} %get-tuple-element.21.work_g, f32[16,256]{1,0:T(8,128)S(1)} %copy-done.5, f32[16,256]{1,0:T(8,128)S(1)} %copy-done.4), custom_call_target="tpu_custom_call", output_to_operand_aliasing={{0}: (0, {}), {1}: (1, {})} | custom-call | flops 67108864 | bytes 4194304 | tf_op jit(solution)/shard_map/near/pallas_call | solution.py:388
  32.5 6.5 %all-to-all-done.pieces = f32[288,1,128]{2,1,0:T(1,128)S(1)} async-done(((f32[288,1,128]{2,1,0:T(1,128)}), f32[288,1,128]{2,1,0:T(1,128)S(1)}, u32[]{:S(2)}, u32[]{:S(2)}) %all-to-all-start) | async-done | bytes 147488 | tf_op jit(solution)/shard_map/all_to_all | solution.py:408
  39.0 0.0 copy-start.2
  39.0 0.1 totals.1
  39.1 18.7 %all_to_all.15.shares = f32[320,1,128]{2,1,0:T(1,128)S(1)} all-to-all(f32[320,1,128]{2,1,0:T(1,128)S(1)} %totals.1), channel_id=1, replica_groups=mesh['xh'=2,'z'=16,'core'=2,'tensor'=8] {'xh','core','tensor'}, dimensions={0} | all-to-all | bytes 327680 | tf_op jit(solution)/shard_map/all_to_all | solution.py:419
  57.8 0.0 copy-start
  57.8 0.0 copy-start.1
  57.8 0.1 scan.1
  58.0 16.1 %all_to_all.16.pieces = f32[288,1,128]{2,1,0:T(1,128)S(1)} all-to-all(f32[288,1,128]{2,1,0:T(1,128)S(1)} %scan.1), channel_id=1, replica_groups=mesh['xh'=2,'z'=16,'core'=2,'tensor'=8] {'z'}, dimensions={0} | all-to-all | bytes 294912 | tf_op jit(solution)/shard_map/all_to_all | solution.py:428
  74.1 0.1 split.1
  74.2 5.8 %collective-permute-start.1 = (f32[32,8,128]{2,1,0:T(8,128)S(1)}, f32[32,8,128]{2,1,0:T(8,128)S(1)}, u32[]{:S(2)}, u32[]{:S(2)}) collective-permute-start(f32[32,8,128]{2,1,0:T(8,128)S(1)} %get-tuple-element.28), channel_id=1, source_target_pairs={{0,8},{8,0},{1,9},{9,1},{2,10},{10,2},{3,11},{11,3},{4,12},{12,4},... | collective-permute-start | bytes 393224 | tf_op jit(solution)/shard_map/ppermute | solution.py:437
  80.1 1.0 %collective-permute-done.1.other = f32[32,8,128]{2,1,0:T(8,128)S(1)} collective-permute-done((f32[32,8,128]{2,1,0:T(8,128)S(1)}, f32[32,8,128]{2,1,0:T(8,128)S(1)}, u32[]{:S(2)}, u32[]{:S(2)}) %collective-permute-start.1) | collective-permute-done | bytes 131104 | tf_op jit(solution)/shard_map/ppermute | solution.py:437
  81.1 0.0 copy-done.3
  81.1 0.0 copy-done.2
  81.1 0.0 copy-done
  81.1 0.0 copy-done.1
  81.1 5.7 %final.1 = (bf16[2,128,1024]{2,1,0:T(8,128)(2,1)}, bf16[2,128,1024]{2,1,0:T(8,128)(2,1)}, bf16[2,128,1024]{2,1,0:T(8,128)(2,1)}, bf16[2,128,1024]{2,1,0:T(8,128)(2,1)}, f32[16,256]{1,0:T(8,128)}) custom-call(s32[1]{0:T(128)} %bitcast.seat, bf16[2,128,1024]{2,1,0:T(8,128)(2,1)S(1)} %copy-done, bf16[2,128,1024]{2,1,0:T(8,128)(2,1)S(1)} %copy-done.1, ...), custom_call_target="tpu_custom_call" | custom-call | tf_op jit(solution)/shard_map/final/pallas_call | solution.py:439
  (1 shorter events, 0.0 us)
Async XLA Ops:
  0.6 15.7 %copy-start.4 = (f32[16,256]{1,0:T(8,128)S(1)}, f32[16,256]{1,0:T(8,128)}, u32[]{:S(2)}) copy-start(f32[16,256]{1,0:T(8,128)} %rate.7) | copy-start | bytes 49156
  6.6 9.7 %collective-permute-start = (f32[32,8,128]{2,1,0:T(8,128)S(1)}, f32[32,8,128]{2,1,0:T(8,128)S(1)}, u32[]{:S(2)}, u32[]{:S(2)}) collective-permute-start(f32[32,8,128]{2,1,0:T(8,128)S(1)} %get-tuple-element.18), channel_id=1, source_target_pairs={{0,8},{8,0},{1,9},{9,1},{2,10},{10,2},{3,11},{11,3},{4,12},{12,4},... | collective-permute-start | bytes 393224 | tf_op jit(solution)/shard_map/ppermute | solution.py:399
  17.1 9.7 %copy-start.5 = (f32[16,256]{1,0:T(8,128)S(1)}, f32[16,256]{1,0:T(8,128)}, u32[]{:S(2)}) copy-start(f32[16,256]{1,0:T(8,128)} %residue.3) | copy-start | bytes 49156
  17.1 21.9 %all-to-all-start = ((f32[288,1,128]{2,1,0:T(1,128)}), f32[288,1,128]{2,1,0:T(1,128)S(1)}, u32[]{:S(2)}, u32[]{:S(2)}) async-start(f32[288,1,128]{2,1,0:T(1,128)} %pair.1), calls=%async_computation | async-start | bytes 294912 | tf_op jit(solution)/shard_map/all_to_all | solution.py:408
  26.8 54.2 %copy-start.3 = (bf16[2,128,1024]{2,1,0:T(8,128)(2,1)S(1)}, bf16[2,128,1024]{2,1,0:T(8,128)(2,1)}, u32[]{:S(2)}) copy-start(bf16[2,128,1024]{2,1,0:T(8,128)(2,1)} %grad.1) | copy-start | bytes 1572868
  39.0 42.1 %copy-start.2 = (bf16[2,128,1024]{2,1,0:T(8,128)(2,1)S(1)}, bf16[2,128,1024]{2,1,0:T(8,128)(2,1)}, u32[]{:S(2)}) copy-start(bf16[2,128,1024]{2,1,0:T(8,128)(2,1)} %value.1) | copy-start | bytes 1572868
  57.8 23.2 %copy-start = (bf16[2,128,1024]{2,1,0:T(8,128)(2,1)S(1)}, bf16[2,128,1024]{2,1,0:T(8,128)(2,1)}, u32[]{:S(2)}) copy-start(bf16[2,128,1024]{2,1,0:T(8,128)(2,1)} %query.1) | copy-start | bytes 1572868
  57.8 23.2 %copy-start.1 = (bf16[2,128,1024]{2,1,0:T(8,128)(2,1)S(1)}, bf16[2,128,1024]{2,1,0:T(8,128)(2,1)}, u32[]{:S(2)}) copy-start(bf16[2,128,1024]{2,1,0:T(8,128)(2,1)} %key.1) | copy-start | bytes 1572868
  74.2 6.8 %collective-permute-start.1 = (f32[32,8,128]{2,1,0:T(8,128)S(1)}, f32[32,8,128]{2,1,0:T(8,128)S(1)}, u32[]{:S(2)}, u32[]{:S(2)}) collective-permute-start(f32[32,8,128]{2,1,0:T(8,128)S(1)} %get-tuple-element.28), channel_id=1, source_target_pairs={{0,8},{8,0},{1,9},{9,1},{2,10},{10,2},{3,11},{11,3},{4,12},{12,4},... | collective-permute-start | bytes 393224 | tf_op jit(solution)/shard_map/ppermute | solution.py:437

commit v5 on v3

--- a/solution.py
+++ b/solution.py
@@ -10,6 +10,8 @@
 F32 = jnp.float32
 LANES = 128
 MODES = 16
+STEP = 4
+WAVE = 4
 ROWS = 9
 
 
@@ -38,10 +40,10 @@
     return pltpu.make_async_copy(source.at[:, :, cut], target.at[:, :, cut], sems.at[which, half, rep])
 
 
-def fetch(pairs, sems, half, repeat, wait):
+def fetch(pairs, sems, half, repeat, wait, base=0):
     for rep in range(repeat):
         for which, (source, target) in enumerate(pairs):
-            copy = slab_copy(source, target, sems, which, half, rep)
+            copy = slab_copy(source, target, sems, base + which, half, rep)
             copy.wait() if wait else copy.start()
 
 
@@ -88,30 +90,51 @@
         fetch(pairs, sems, half, repeat, True)
         products_of(half, key, value, work_u, repeat)
         products_of(half, grad, query, work_g, repeat)
-        for group in range(0, MODES, 8):
-            decay = [spread(jnp.exp(-rate[n : n + 1, lanes_of(half)])) for n in range(group, group + 8)]
-
-            def step(i, carry, decay=decay, half=half):
-                ups, downs, sums = (list(c) for c in carry)
-                ahead = pl.ds(pl.multiple_of(i * 8, 8), 8)
-                behind = pl.ds(pl.multiple_of((length - 1 - i) * 8, 8), 8)
-                u, g, gr = work_u[half, ahead, :], work_g[half, ahead, :], work_g[half, behind, :]
-                for m in range(8):
-                    ups[m] = decay[m] * ups[m] + u
-                    downs[m] = decay[m] * downs[m] + gr
-                    sums[m] = sums[m] + g * ups[m]
-                return tuple(ups), tuple(downs), tuple(sums)
-
-            zero = tuple(jnp.zeros((8, LANES), F32) for _ in range(8))
-            ups, downs, sums = lax.fori_loop(0, length, step, (zero, zero, zero), unroll=4)
+        lags = None
+        for group in range(0, MODES, WAVE):
+            modes = range(group, group + WAVE)
+            decay = [spread(jnp.exp(-rate[n : n + 1, lanes_of(half)])) for n in modes]
+            jump = [spread(jnp.exp(-rate[n : n + 1, lanes_of(half)] * float(STEP))) for n in modes]
+
+            def step(i, carry, decay=decay, jump=jump, half=half):
+                ups, downs, powers, sums, pairs = (list(c) for c in carry)
+                base = i * (8 * STEP)
+                rows = [pl.ds(pl.multiple_of(base + 8 * j, 8), 8) for j in range(STEP)]
+                us = [work_u[half, row, :] for row in rows]
+                gs = [work_g[half, row, :] for row in rows]
+                for lag in range(len(pairs)):
+                    for j in range(lag, STEP):
+                        pairs[lag] = pairs[lag] + gs[j] * us[j - lag]
+                for m in range(WAVE):
+                    risen, fallen = us[0], gs[-1]
+                    for j in range(1, STEP):
+                        risen = decay[m] * risen + us[j]
+                        fallen = decay[m] * fallen + gs[STEP - 1 - j]
+                    sums[m] = sums[m] + fallen * ups[m]
+                    ups[m] = jump[m] * ups[m] + risen
+                    downs[m] = downs[m] + powers[m] * fallen
+                    powers[m] = powers[m] * jump[m]
+                return tuple(ups), tuple(downs), tuple(powers), tuple(sums), tuple(pairs)
+
+            zero = tuple(jnp.zeros((8, LANES), F32) for _ in range(WAVE))
+            ones = tuple(jnp.ones((8, LANES), F32) for _ in range(WAVE))
+            none = () if lags else tuple(jnp.zeros((8, LANES), F32) for _ in range(STEP))
+            ups, downs, _, sums, pairs_of = lax.fori_loop(
+                0, length // STEP, step, (zero, zero, ones, zero, none), unroll=4
+            )
+            lags = lags or pairs_of
             low = bottom()
-            for m in range(8):
+            for m in range(WAVE):
                 top_half = jnp.where(low, swap_halves(downs[m]), ups[m])
                 end_half = jnp.where(low, downs[m], swap_halves(ups[m]))
-                piece = 2 * (group + m) + half
+                piece = half * MODES + group + m
                 keep[piece] = jnp.where(first, top_half, end_half)
                 send[piece] = jnp.where(first, end_half, top_half)
-                within[piece : piece + 1, :] = jnp.sum(sums[m], axis=0, keepdims=True)
+                inner = lags[-1]
+                for lag in reversed(range(STEP - 1)):
+                    inner = decay[m] * inner + lags[lag]
+                inner = inner + decay[m] * sums[m]
+                within[piece : piece + 1, :] = jnp.sum(inner, axis=0, keepdims=True)
 
 
 def near_kernel(work_u, work_g, residue, rate, near, back):
@@ -147,7 +170,7 @@
     low = bottom()
     for half in range(2):
         for n in range(MODES):
-            piece = 2 * n + half
+            piece = half * MODES + n
             pace = rate[n : n + 1, lanes_of(half)]
             decay = spread(jnp.exp(-pace * float(block)))
             left, right = order(first, own[piece], other[piece])
@@ -159,60 +182,44 @@
             out[piece * ROWS + 8] = within[piece : piece + 1, :] + total
 
 
-def rows_of(pieces, chip, half, base):
-    start = (2 * chip + half) * ROWS + base
-    return jnp.concatenate([pieces[start + j] for j in range(4)], axis=0)
-
-
-def totals_kernel(part, pieces, pace, out, *, block):
-    count = pieces.shape[0] // (2 * ROWS)
-    early = part[0] == 0
-    for half in range(2):
-        rates = pace[:, lanes_of(half)]
-        decay = jnp.broadcast_to(jnp.exp(-rates * float(block)), (4, LANES))
-        ahead, cross, behind = (jnp.zeros((4, LANES), F32) for _ in range(3))
-        local = jnp.zeros((1, LANES), F32)
-        for chip in range(count):
-            cross = cross + ahead * rows_of(pieces, chip, half, 4)
-            local = local + pieces[(2 * chip + half) * ROWS + 8]
-            ahead = decay * ahead + rows_of(pieces, chip, half, 0)
-        for chip in reversed(range(count)):
-            behind = decay * behind + rows_of(pieces, chip, half, 4)
-        total = local + jnp.exp(-rates) * jnp.sum(cross, axis=0, keepdims=True)
-        out[half, 0:4, :] = jnp.where(early, ahead, behind)
-        out[half, 4:8, :] = jnp.broadcast_to(total, (4, LANES))
-
-
-def scan_kernel(part, pieces, pace, own, other, out, *, block):
-    count = pieces.shape[0] // (2 * ROWS)
-    early = part[0] == 0
-    for half in range(2):
-        rates = pace[:, lanes_of(half)]
-        decay = jnp.broadcast_to(jnp.exp(-rates * float(block)), (4, LANES))
-        given = other[half, 0:4, :]
-        ahead = jnp.where(early, 0.0, given)
-        behind = jnp.where(early, given, 0.0)
-        cross = jnp.sum(own[half, 0:4, :] * given, axis=0, keepdims=True)
-        total = own[half, 4:5, :] + other[half, 4:5, :] + jnp.exp(-rates) * cross
-        for chip in range(count):
-            start = (2 * chip + half) * ROWS
-            for j in range(4):
-                out[start + j] = ahead[j : j + 1, :]
-            out[start + 8] = total
-            ahead = decay * ahead + rows_of(pieces, chip, half, 0)
-        for chip in reversed(range(count)):
-            start = (2 * chip + half) * ROWS + 4
-            for j in range(4):
-                out[start + j] = behind[j : j + 1, :]
-            behind = decay * behind + rows_of(pieces, chip, half, 4)
-
-
-def split_kernel(core, pieces, own, other, rate, keep, send, total, *, block):
+def scan_kernel(pieces, pace, out, *, block):
+    count = pieces.shape[0] // ROWS
+    decay = jnp.exp(-pace[...] * float(block))
+    decay4 = jnp.broadcast_to(decay, (4, LANES))
+
+    def load(index, base):
+        return jnp.concatenate([pieces[index * ROWS + base + j] for j in range(4)], axis=0)
+
+    ahead = jnp.zeros((4, LANES), F32)
+    cross = jnp.zeros((4, LANES), F32)
+    local = jnp.zeros((1, LANES), F32)
+    for index in range(count):
+        for j in range(4):
+            out[index * ROWS + j] = ahead[j : j + 1, :]
+        cross = cross + ahead * load(index, 4)
+        local = local + pieces[index * ROWS + 8]
+        ahead = decay4 * ahead + load(index, 0)
+    behind = jnp.zeros((4, LANES), F32)
+    for index in reversed(range(count)):
+        for j in range(4):
+            out[index * ROWS + 4 + j] = behind[j : j + 1, :]
+        behind = decay4 * behind + load(index, 4)
+    total = local + jnp.exp(-pace[...]) * jnp.sum(cross, axis=0, keepdims=True)
+    for index in range(count):
+        out[index * ROWS + 8] = total
+
+
+def split_kernel(core, pieces, own, other, rate, keep, send, total, share, sems, *, block):
     first = core[0] == 0
     low = bottom()
+    for piece in range(2 * MODES):
+        share[piece : piece + 1, :] = pieces[piece * ROWS + 8]
+    copies = [pltpu.make_async_copy(share, total.at[i], sems.at[i]) for i in range(total.shape[0])]
+    for copy in copies:
+        copy.start()
     for half in range(2):
         for n in range(MODES):
-            piece = 2 * n + half
+            piece = half * MODES + n
             pace = rate[n : n + 1, lanes_of(half)]
             decay = spread(jnp.exp(-pace * float(block)))
             left, right = order(first, own[piece], other[piece])
@@ -223,9 +230,8 @@
             mine, others = order(first, for_left, for_right)
             keep[piece] = mine
             send[piece] = others
-            row = pieces[piece * ROWS + 8]
-            for copy in range(total.shape[0]):
-                total[copy, half * MODES + n : half * MODES + n + 1, :] = row
+    for copy in copies:
+        copy.wait()
 
 
 def final_kernel(
@@ -262,9 +268,10 @@
     low = bottom()
     outs = ((mixed, mixed_out), (grad_query, grad_query_out), (grad_key, grad_key_out), (grad_value, grad_value_out))
 
-    pairs = ((query_in, query), (grad_in, grad), (value_in, value), (key_in, key))
-    for half in range(2):
-        fetch(pairs, in_sems, half, repeat, False)
+    fore, aft = ((query_in, query), (grad_in, grad)), ((value_in, value), (key_in, key))
+    for half in range(2):
+        fetch(fore, in_sems, half, repeat, False)
+        fetch(aft, in_sems, half, repeat, False, 2)
 
     def products(half, source_a, source_b, base):
         target_a, target_b = outs[base][0], outs[base + 1][0]
@@ -280,7 +287,7 @@
     for half in range(2):
         decay, forward, backward = [], [], []
         for n in range(MODES):
-            piece = 2 * n + half
+            piece = half * MODES + n
             weight = spread(residue[n : n + 1, lanes_of(half)])
             decay.append(spread(jnp.exp(-rate[n : n + 1, lanes_of(half)])))
             one, two = order(first, own[piece], other[piece])
@@ -297,9 +304,10 @@
             return step(length - 1 - i, carry, source=back)
 
         lax.fori_loop(0, length, step, tuple(forward), unroll=2)
-        fetch(pairs, in_sems, half, repeat, True)
+        fetch(fore, in_sems, half, repeat, True)
         products(half, query, grad, 0)
         lax.fori_loop(0, length, step_back, tuple(backward), unroll=2)
+        fetch(aft, in_sems, half, repeat, True, 2)
         products(half, value, key, 2)
     for which in range(4):
         for half in range(2):
@@ -324,7 +332,6 @@
     seq_count, block, channels = query.shape
     pieces = 2 * MODES
     core = lax.axis_index("core").astype(jnp.int32).reshape(1)
-    part = lax.axis_index("xh").astype(jnp.int32).reshape(1)
     tile = struct(pieces, 8, LANES)
     rows = struct(pieces * ROWS, 1, LANES)
     works = struct(2, block * 8, LANES)
@@ -362,34 +369,26 @@
         out_specs=VMEM,
         compiler_params=room(4),
     )(core, keep, other, within, rate)
-    gathered = lax.all_to_all(joined, "z", 0, 0, tiled=True)
+    gathered = lax.all_to_all(joined, ("xh", "z"), 0, 0, tiled=True)
     gathered, near, back = lax.optimization_barrier((gathered, near, back))
-    pace = lax.dynamic_slice(rate, (lax.axis_index("z"), 0), (1, rate.shape[1]))
-    totals = pl.pallas_call(
-        functools.partial(totals_kernel, block=2 * block),
-        name="totals",
-        out_shape=struct(2, 8, LANES),
-        in_specs=[SMEM] + [VMEM] * 2,
-        out_specs=VMEM,
-        compiler_params=room(4),
-    )(part, gathered, pace)
-    totals_other = lax.ppermute(totals, "xh", exchange)
+    pace = lax.dynamic_slice(rate, (lax.axis_index("z"), lax.axis_index("xh") * LANES), (1, LANES))
     scanned = pl.pallas_call(
         functools.partial(scan_kernel, block=2 * block),
         name="scan",
         out_shape=pltpu.VMEM(rows.shape, F32),
-        in_specs=[SMEM] + [VMEM] * 4,
+        in_specs=[VMEM] * 2,
         out_specs=VMEM,
         compiler_params=room(4),
-    )(part, gathered, pace, totals, totals_other)
-    returned = lax.all_to_all(scanned, "z", 0, 0, tiled=True)
+    )(gathered, pace)
+    returned = lax.all_to_all(scanned, ("xh", "z"), 0, 0, tiled=True)
     group = lax.axis_size("core") * lax.axis_size("tensor")
     state, state_send, total = pl.pallas_call(
         functools.partial(split_kernel, block=block),
         name="split",
         out_shape=(tile, tile, struct(group, pieces, LANES)),
         in_specs=[SMEM] + [VMEM] * 4,
-        out_specs=(VMEM,) * 3,
+        out_specs=(VMEM, VMEM, HBM),
+        scratch_shapes=[pltpu.VMEM((pieces, LANES), F32), pltpu.SemaphoreType.DMA((group,))],
         compiler_params=room(4),
     )(core, returned, keep, other, rate)
     state_other = lax.ppermute(state_send, "core", exchange)

time: 85.9 us -> 86.4 us (level)
  starting transfers between devices: 34.7 us -> 30.2 us
  waiting for transfers between devices: 9.26 us -> 13 us
  blocking collectives: 18.9 us -> 21.6 us
  Pallas kernels: 20.3 us -> 18.9 us
    all_to_all x1, waiting for transfers between devices: 5.84 us -> 10.8 us  [staged(): gathered = lax.all_to_all(joined, ('xh', 'z'), 0, 0, tiled=True)]
    ppermute x1 -> x0, starting transfers between devices: 4.65 us -> none  [staged(): totals_other = lax.ppermute(totals, 'xh', exchange)]
    all_to_all x1, starting transfers between devices: 9.57 us -> 12.3 us  [staged(): gathered = lax.all_to_all(joined, ('xh', 'z'), 0, 0, tiled=True)]
    all_to_all x1, blocking collectives: 18.9 us -> 21.6 us  [staged(): returned = lax.all_to_all(scanned, ('xh', 'z'), 0, 0, tiled=True)]
    all_to_all x1, starting transfers between devices: 9.68 us -> 7.18 us  [staged(): shares = lax.all_to_all(total, ('core', 'tensor'), 0, 0, tiled=True)]
    ppermute x1 -> x0, waiting for transfers between devices: 1.24 us -> none  [staged(): totals_other = lax.ppermute(totals, 'xh', exchange)]
    pallas_call x1, Pallas kernels: 6.53 us -> 5.59 us  [staged(): pl.pallas_call(sums_kernel, name='sums', out_shape=(works, works, tile, t...]
  transfers between devices with their start and end apart: 5 -> 4, of which waited for: 4 -> 3; matrix products, arithmetic and copies ran while one was open for 0% -> 0% of each run, Pallas kernels for 14% -> 13%
where the time goes in v5:
time: 86.4 us; the launch traced here: 85.9 us
  starting transfers between devices  30.2 us (35%)
  blocking collectives  21.6 us (25%)
  Pallas kernels  18.9 us (22%)
  waiting for transfers between devices  13 us (15%)
    all_to_all x1, blocking collectives, staged(): returned = lax.all_to_all(scanned, ('xh', 'z'), 0, 0, tiled=True)  21.6 us
    all_to_all x1, starting transfers between devices, staged(): gathered = lax.all_to_all(joined, ('xh', 'z'), 0, 0, tiled=True)  12.3 us
    all_to_all x1, waiting for transfers between devices, staged(): gathered = lax.all_to_all(joined, ('xh', 'z'), 0, 0, tiled=True)  10.8 us
    ppermute x1, starting transfers between devices, staged(): other = lax.ppermute(send, 'core', exchange)  8.75 us
    all_to_all x1, starting transfers between devices, staged(): shares = lax.all_to_all(total, ('core', 'tensor'), 0, 0, tiled=True)  7.18 us
    pallas_call x1, Pallas kernels, staged(): pl.pallas_call(final_kernel, name='final', out_shape=(whole,) * 4, in_spe...  5.95 us
    pallas_call x1, Pallas kernels, staged(): pl.pallas_call(near_kernel, name='near', out_shape=(works, works), in_spe...  5.62 us
    pallas_call x1, Pallas kernels, staged(): pl.pallas_call(sums_kernel, name='sums', out_shape=(works, works, tile, t...  5.59 us
  transfers between devices with their start and end apart: 4, of which 3 were waited for; matrix products, arithmetic and copies ran while one was open for 0% of the time, Pallas kernels for 13%

profile of v5, /device:TPU:1, one launch (start us, length us, event | category | flops | bytes accessed | tf_op | source)
XLA Modules:
  0.0 85.9 jit_solution(12655630730648357495)
XLA Ops:
  0.6 0.0 copy-start
  0.6 5.6 %sums.1 = (f32[2,1024,128]{2,1,0:T(8,128)S(1)}, f32[2,1024,128]{2,1,0:T(8,128)S(1)}, f32[32,8,128]{2,1,0:T(8,128)S(1)}, f32[32,8,128]{2,1,0:T(8,128)S(1)}, f32[32,128]{1,0:T(8,128)S(1)}) custom-call(s32[1]{0:T(128)} %bitcast.core, bf16[2,128,1024]{2,1,0:T(8,128)(2,1)} %query_in.3, bf16[2,128,1024]{2,1,0:T(8,128)(2,1)} %key_in.3, ...), custom_call_target="tpu_custom_call" | custom-call | tf_op jit(solution)/shard_map/sums/pallas_call | solution.py:343
  6.2 8.7 %collective-permute-start = (f32[32,8,128]{2,1,0:T(8,128)S(1)}, f32[32,8,128]{2,1,0:T(8,128)S(1)}, u32[]{:S(2)}, u32[]{:S(2)}) collective-permute-start(f32[32,8,128]{2,1,0:T(8,128)S(1)} %get-tuple-element.23), channel_id=1, source_target_pairs={{0,8},{8,0},{1,9},{9,1},{2,10},{10,2},{3,11},{11,3},{4,12},{12,4},... | collective-permute-start | bytes 393224 | tf_op jit(solution)/shard_map/ppermute | solution.py:363
  15.0 1.0 %collective-permute-done.other = f32[32,8,128]{2,1,0:T(8,128)S(1)} collective-permute-done((f32[32,8,128]{2,1,0:T(8,128)S(1)}, f32[32,8,128]{2,1,0:T(8,128)S(1)}, u32[]{:S(2)}, u32[]{:S(2)}) %collective-permute-start) | collective-permute-done | bytes 131104 | tf_op jit(solution)/shard_map/ppermute | solution.py:363
  16.0 0.0 copy-done
  16.0 0.8 pair.1
  16.7 12.3 %all-to-all-start = ((f32[288,1,128]{2,1,0:T(1,128)}), f32[288,1,128]{2,1,0:T(1,128)S(1)}, u32[]{:S(2)}, u32[]{:S(2)}) async-start(f32[288,1,128]{2,1,0:T(1,128)} %pair.1), calls=%async_computation | async-start | bytes 294912 | tf_op jit(solution)/shard_map/all_to_all | solution.py:372
  29.1 0.0 copy-start.1
  29.1 0.1 dynamic_slice.3.pace
  29.2 0.6 copy-done.1
  29.8 5.6 %near.1 = (f32[2,1024,128]{2,1,0:T(8,128)S(1)}, f32[2,1024,128]{2,1,0:T(8,128)S(1)}) custom-call(f32[2,1024,128]{2,1,0:T(8,128)S(1)} %get-tuple-element.25.work_u, f32[2,1024,128]{2,1,0:T(8,128)S(1)} %get-tuple-element.26.work_g, f32[16,256]{1,0:T(8,128)S(1)} %copy-done.1, f32[16,256]{1,0:T(8,128)S(1)} %copy-done), custom_call_target="tpu_custom_call", output_to_operand_aliasing={{0}: (0, {}), {1}: (1, {})} | custom-call | flops 67108864 | bytes 4194304 | tf_op jit(solution)/shard_map/near/pallas_call | solution.py:352
  35.4 10.8 %all-to-all-done.pieces = f32[288,1,128]{2,1,0:T(1,128)S(1)} async-done(((f32[288,1,128]{2,1,0:T(1,128)}), f32[288,1,128]{2,1,0:T(1,128)S(1)}, u32[]{:S(2)}, u32[]{:S(2)}) %all-to-all-start) | async-done | bytes 147488 | tf_op jit(solution)/shard_map/all_to_all | solution.py:372
  46.3 0.1 scan.1
  46.4 21.6 %all_to_all.15.pieces = f32[288,1,128]{2,1,0:T(1,128)S(1)} all-to-all(f32[288,1,128]{2,1,0:T(1,128)S(1)} %scan.1), channel_id=1, replica_groups=mesh['xh'=2,'z'=16,'core'=2,'tensor'=8] {'xh','z'}, dimensions={0} | all-to-all | bytes 294912 | tf_op jit(solution)/shard_map/all_to_all | solution.py:383
  68.0 0.9 %split.1 = (f32[32,8,128]{2,1,0:T(8,128)S(1)}, f32[32,8,128]{2,1,0:T(8,128)S(1)}, f32[16,32,128]{2,1,0:T(8,128)}) custom-call(s32[1]{0:T(128)} %bitcast.core, f32[288,1,128]{2,1,0:T(1,128)S(1)} %all_to_all.15.pieces, f32[32,8,128]{2,1,0:T(8,128)S(1)} %get-tuple-element.22.own, f32[32,8,128]{2,1,0:T(8,128)S(1)} %collective-permute-done.other, ...), custom_call_target="tpu_custom_call" | custom-call | tf_op jit(solution)/shard_map/split/pallas_call | solution.py:385
  68.8 7.2 %all-to-all-start.2 = ((f32[16,32,128]{2,1,0:T(8,128)}), f32[16,32,128]{2,1,0:T(8,128)S(1)}, u32[]{:S(2)}, u32[]{:S(2)}) async-start(f32[16,32,128]{2,1,0:T(8,128)} %get-tuple-element.38), calls=%async_computation.2 | async-start | bytes 524288 | tf_op jit(solution)/shard_map/all_to_all | solution.py:395
  76.0 2.0 %collective-permute-start.1 = (f32[32,8,128]{2,1,0:T(8,128)S(1)}, f32[32,8,128]{2,1,0:T(8,128)S(1)}, u32[]{:S(2)}, u32[]{:S(2)}) collective-permute-start(f32[32,8,128]{2,1,0:T(8,128)S(1)} %get-tuple-element.33), channel_id=1, source_target_pairs={{0,8},{8,0},{1,9},{9,1},{2,10},{10,2},{3,11},{11,3},{4,12},{12,4},... | collective-permute-start | bytes 393224 | tf_op jit(solution)/shard_map/ppermute | solution.py:394
  78.0 1.2 %collective-permute-done.1.other = f32[32,8,128]{2,1,0:T(8,128)S(1)} collective-permute-done((f32[32,8,128]{2,1,0:T(8,128)S(1)}, f32[32,8,128]{2,1,0:T(8,128)S(1)}, u32[]{:S(2)}, u32[]{:S(2)}) %collective-permute-start.1) | collective-permute-done | bytes 131104 | tf_op jit(solution)/shard_map/ppermute | solution.py:394
  79.3 5.9 %final.1 = (bf16[2,128,1024]{2,1,0:T(8,128)(2,1)}, bf16[2,128,1024]{2,1,0:T(8,128)(2,1)}, bf16[2,128,1024]{2,1,0:T(8,128)(2,1)}, bf16[2,128,1024]{2,1,0:T(8,128)(2,1)}) custom-call(s32[1]{0:T(128)} %bitcast.core, bf16[2,128,1024]{2,1,0:T(8,128)(2,1)} %query_in.3, bf16[2,128,1024]{2,1,0:T(8,128)(2,1)} %key_in.3, bf16[2,128,1024]{2,1,0:T(8,128)(2,1)} %value_in.3, ...), custom_call_target="tpu_custom_call" | custom-call | tf_op jit(solution)/shard_map/final/pallas_call | solution.py:400
  85.2 0.0 all-to-all-done.2
  85.3 0.6 maximum_multiply_fusion
  (2 shorter events, 0.0 us)
Async XLA Ops:
  0.6 15.3 %copy-start = (f32[16,256]{1,0:T(8,128)S(1)}, f32[16,256]{1,0:T(8,128)}, u32[]{:S(2)}) copy-start(f32[16,256]{1,0:T(8,128)} %rate.7) | copy-start | bytes 49156
  6.2 9.7 %collective-permute-start = (f32[32,8,128]{2,1,0:T(8,128)S(1)}, f32[32,8,128]{2,1,0:T(8,128)S(1)}, u32[]{:S(2)}, u32[]{:S(2)}) collective-permute-start(f32[32,8,128]{2,1,0:T(8,128)S(1)} %get-tuple-element.23), channel_id=1, source_target_pairs={{0,8},{8,0},{1,9},{9,1},{2,10},{10,2},{3,11},{11,3},{4,12},{12,4},... | collective-permute-start | bytes 393224 | tf_op jit(solution)/shard_map/ppermute | solution.py:363
  16.7 29.5 %all-to-all-start = ((f32[288,1,128]{2,1,0:T(1,128)}), f32[288,1,128]{2,1,0:T(1,128)S(1)}, u32[]{:S(2)}, u32[]{:S(2)}) async-start(f32[288,1,128]{2,1,0:T(1,128)} %pair.1), calls=%async_computation | async-start | bytes 294912 | tf_op jit(solution)/shard_map/all_to_all | solution.py:372
  29.1 0.7 copy-start.1
  68.8 16.4 %all-to-all-start.2 = ((f32[16,32,128]{2,1,0:T(8,128)}), f32[16,32,128]{2,1,0:T(8,128)S(1)}, u32[]{:S(2)}, u32[]{:S(2)}) async-start(f32[16,32,128]{2,1,0:T(8,128)} %get-tuple-element.38), calls=%async_computation.2 | async-start | bytes 524288 | tf_op jit(solution)/shard_map/all_to_all | solution.py:395
  76.0 3.2 %collective-permute-start.1 = (f32[32,8,128]{2,1,0:T(8,128)S(1)}, f32[32,8,128]{2,1,0:T(8,128)S(1)}, u32[]{:S(2)}, u32[]{:S(2)}) collective-permute-start(f32[32,8,128]{2,1,0:T(8,128)S(1)} %get-tuple-element.33), channel_id=1, source_target_pairs={{0,8},{8,0},{1,9},{9,1},{2,10},{10,2},{3,11},{11,3},{4,12},{12,4},... | collective-permute-start | bytes 393224 | tf_op jit(solution)/shard_map/ppermute | solution.py:394

commit v6 on v5

--- a/solution.py
+++ b/solution.py
@@ -47,13 +47,12 @@
             copy.wait() if wait else copy.start()
 
 
-def products_of(half, first, second, work, repeat):
+def products_of(half, rep, first, second, work, repeat):
     length = first.shape[1]
+    cut = columns(half, rep)
     for seq in range(2):
-        for rep in range(repeat):
-            cut = columns(half, rep)
-            rows = pl.ds(seq * repeat + rep, length, stride=8)
-            work[half, rows, :] = first[seq, :, cut].astype(F32) * second[seq, :, cut].astype(F32)
+        rows = pl.ds(seq * repeat + rep, length, stride=8)
+        work[half, rows, :] = first[seq, :, cut].astype(F32) * second[seq, :, cut].astype(F32)
 
 
 def sums_kernel(
@@ -87,9 +86,15 @@
     for half in range(2):
         if half == 0:
             rates.wait()
-        fetch(pairs, sems, half, repeat, True)
-        products_of(half, key, value, work_u, repeat)
-        products_of(half, grad, query, work_g, repeat)
+        batch = repeat if half else max(repeat // 2, 1)
+        for start in range(0, repeat, batch):
+            reps = range(start, start + batch)
+            for rep in reps:
+                for which, (source, target) in enumerate(pairs):
+                    slab_copy(source, target, sems, which, half, rep).wait()
+            for rep in reps:
+                products_of(half, rep, key, value, work_u, repeat)
+                products_of(half, rep, grad, query, work_g, repeat)
         lags = None
         for group in range(0, MODES, WAVE):
             modes = range(group, group + WAVE)
@@ -120,7 +125,7 @@
             ones = tuple(jnp.ones((8, LANES), F32) for _ in range(WAVE))
             none = () if lags else tuple(jnp.zeros((8, LANES), F32) for _ in range(STEP))
             ups, downs, _, sums, pairs_of = lax.fori_loop(
-                0, length // STEP, step, (zero, zero, ones, zero, none), unroll=4
+                0, length // STEP, step, (zero, zero, ones, zero, none), unroll=8
             )
             lags = lags or pairs_of
             low = bottom()
@@ -303,10 +308,10 @@
         def step_back(i, carry, step=step):
             return step(length - 1 - i, carry, source=back)
 
-        lax.fori_loop(0, length, step, tuple(forward), unroll=2)
+        lax.fori_loop(0, length, step, tuple(forward), unroll=4)
         fetch(fore, in_sems, half, repeat, True)
         products(half, query, grad, 0)
-        lax.fori_loop(0, length, step_back, tuple(backward), unroll=2)
+        lax.fori_loop(0, length, step_back, tuple(backward), unroll=4)
         fetch(aft, in_sems, half, repeat, True, 2)
         products(half, value, key, 2)
     for which in range(4):

time: 86.4 us -> 85.7 us (level)
  no operation moved by 1% of the time
where the time goes in v6:
time: 85.7 us; the launch traced here: 85.2 us
  starting transfers between devices  30.2 us (35%)
  blocking collectives  21.6 us (25%)
  Pallas kernels  18.2 us (21%)
  waiting for transfers between devices  13 us (15%)
    all_to_all x1, blocking collectives, staged(): returned = lax.all_to_all(scanned, ('xh', 'z'), 0, 0, tiled=True)  21.6 us
    all_to_all x1, starting transfers between devices, staged(): gathered = lax.all_to_all(joined, ('xh', 'z'), 0, 0, tiled=True)  12.3 us
    all_to_all x1, waiting for transfers between devices, staged(): gathered = lax.all_to_all(joined, ('xh', 'z'), 0, 0, tiled=True)  10.8 us
    ppermute x1, starting transfers between devices, staged(): other = lax.ppermute(send, 'core', exchange)  8.75 us
    all_to_all x1, starting transfers between devices, staged(): shares = lax.all_to_all(total, ('core', 'tensor'), 0, 0, tiled=True)  7.18 us
    pallas_call x1, Pallas kernels, staged(): pl.pallas_call(near_kernel, name='near', out_shape=(works, works), in_spe...  5.62 us
    pallas_call x1, Pallas kernels, staged(): pl.pallas_call(sums_kernel, name='sums', out_shape=(works, works, tile, t...  5.49 us
    pallas_call x1, Pallas kernels, staged(): pl.pallas_call(final_kernel, name='final', out_shape=(whole,) * 4, in_spe...  5.34 us
  transfers between devices with their start and end apart: 4, of which 3 were waited for; matrix products, arithmetic and copies ran while one was open for 0% of the time, Pallas kernels for 13%

profile of v6, /device:TPU:1, one launch (start us, length us, event | category | flops | bytes accessed | tf_op | source)
XLA Modules:
  0.0 85.2 jit_solution(973508917989424152)
XLA Ops:
  0.6 0.0 copy-start
  0.6 5.5 %sums.1 = (f32[2,1024,128]{2,1,0:T(8,128)S(1)}, f32[2,1024,128]{2,1,0:T(8,128)S(1)}, f32[32,8,128]{2,1,0:T(8,128)S(1)}, f32[32,8,128]{2,1,0:T(8,128)S(1)}, f32[32,128]{1,0:T(8,128)S(1)}) custom-call(s32[1]{0:T(128)} %bitcast.core, bf16[2,128,1024]{2,1,0:T(8,128)(2,1)} %query_in.3, bf16[2,128,1024]{2,1,0:T(8,128)(2,1)} %key_in.3, ...), custom_call_target="tpu_custom_call" | custom-call | tf_op jit(solution)/shard_map/sums/pallas_call | solution.py:348
  6.1 8.7 %collective-permute-start = (f32[32,8,128]{2,1,0:T(8,128)S(1)}, f32[32,8,128]{2,1,0:T(8,128)S(1)}, u32[]{:S(2)}, u32[]{:S(2)}) collective-permute-start(f32[32,8,128]{2,1,0:T(8,128)S(1)} %get-tuple-element.23), channel_id=1, source_target_pairs={{0,8},{8,0},{1,9},{9,1},{2,10},{10,2},{3,11},{11,3},{4,12},{12,4},... | collective-permute-start | bytes 393224 | tf_op jit(solution)/shard_map/ppermute | solution.py:368
  14.9 1.0 %collective-permute-done.other = f32[32,8,128]{2,1,0:T(8,128)S(1)} collective-permute-done((f32[32,8,128]{2,1,0:T(8,128)S(1)}, f32[32,8,128]{2,1,0:T(8,128)S(1)}, u32[]{:S(2)}, u32[]{:S(2)}) %collective-permute-start) | collective-permute-done | bytes 131104 | tf_op jit(solution)/shard_map/ppermute | solution.py:368
  15.9 0.0 copy-done
  15.9 0.8 pair.1
  16.6 12.3 %all-to-all-start = ((f32[288,1,128]{2,1,0:T(1,128)}), f32[288,1,128]{2,1,0:T(1,128)S(1)}, u32[]{:S(2)}, u32[]{:S(2)}) async-start(f32[288,1,128]{2,1,0:T(1,128)} %pair.1), calls=%async_computation | async-start | bytes 294912 | tf_op jit(solution)/shard_map/all_to_all | solution.py:377
  29.0 0.0 copy-start.1
  29.0 0.1 dynamic_slice.3.pace
  29.1 0.6 copy-done.1
  29.7 5.6 %near.1 = (f32[2,1024,128]{2,1,0:T(8,128)S(1)}, f32[2,1024,128]{2,1,0:T(8,128)S(1)}) custom-call(f32[2,1024,128]{2,1,0:T(8,128)S(1)} %get-tuple-element.25.work_u, f32[2,1024,128]{2,1,0:T(8,128)S(1)} %get-tuple-element.26.work_g, f32[16,256]{1,0:T(8,128)S(1)} %copy-done.1, f32[16,256]{1,0:T(8,128)S(1)} %copy-done), custom_call_target="tpu_custom_call", output_to_operand_aliasing={{0}: (0, {}), {1}: (1, {})} | custom-call | flops 67108864 | bytes 4194304 | tf_op jit(solution)/shard_map/near/pallas_call | solution.py:357
  35.3 10.8 %all-to-all-done.pieces = f32[288,1,128]{2,1,0:T(1,128)S(1)} async-done(((f32[288,1,128]{2,1,0:T(1,128)}), f32[288,1,128]{2,1,0:T(1,128)S(1)}, u32[]{:S(2)}, u32[]{:S(2)}) %all-to-all-start) | async-done | bytes 147488 | tf_op jit(solution)/shard_map/all_to_all | solution.py:377
  46.1 0.1 scan.1
  46.3 21.6 %all_to_all.15.pieces = f32[288,1,128]{2,1,0:T(1,128)S(1)} all-to-all(f32[288,1,128]{2,1,0:T(1,128)S(1)} %scan.1), channel_id=1, replica_groups=mesh['xh'=2,'z'=16,'core'=2,'tensor'=8] {'xh','z'}, dimensions={0} | all-to-all | bytes 294912 | tf_op jit(solution)/shard_map/all_to_all | solution.py:388
  67.9 0.9 %split.1 = (f32[32,8,128]{2,1,0:T(8,128)S(1)}, f32[32,8,128]{2,1,0:T(8,128)S(1)}, f32[16,32,128]{2,1,0:T(8,128)}) custom-call(s32[1]{0:T(128)} %bitcast.core, f32[288,1,128]{2,1,0:T(1,128)S(1)} %all_to_all.15.pieces, f32[32,8,128]{2,1,0:T(8,128)S(1)} %get-tuple-element.22.own, f32[32,8,128]{2,1,0:T(8,128)S(1)} %collective-permute-done.other, ...), custom_call_target="tpu_custom_call" | custom-call | tf_op jit(solution)/shard_map/split/pallas_call | solution.py:390
  68.7 7.2 %all-to-all-start.2 = ((f32[16,32,128]{2,1,0:T(8,128)}), f32[16,32,128]{2,1,0:T(8,128)S(1)}, u32[]{:S(2)}, u32[]{:S(2)}) async-start(f32[16,32,128]{2,1,0:T(8,128)} %get-tuple-element.38), calls=%async_computation.2 | async-start | bytes 524288 | tf_op jit(solution)/shard_map/all_to_all | solution.py:400
  75.9 2.0 %collective-permute-start.1 = (f32[32,8,128]{2,1,0:T(8,128)S(1)}, f32[32,8,128]{2,1,0:T(8,128)S(1)}, u32[]{:S(2)}, u32[]{:S(2)}) collective-permute-start(f32[32,8,128]{2,1,0:T(8,128)S(1)} %get-tuple-element.33), channel_id=1, source_target_pairs={{0,8},{8,0},{1,9},{9,1},{2,10},{10,2},{3,11},{11,3},{4,12},{12,4},... | collective-permute-start | bytes 393224 | tf_op jit(solution)/shard_map/ppermute | solution.py:399
  77.9 1.2 %collective-permute-done.1.other = f32[32,8,128]{2,1,0:T(8,128)S(1)} collective-permute-done((f32[32,8,128]{2,1,0:T(8,128)S(1)}, f32[32,8,128]{2,1,0:T(8,128)S(1)}, u32[]{:S(2)}, u32[]{:S(2)}) %collective-permute-start.1) | collective-permute-done | bytes 131104 | tf_op jit(solution)/shard_map/ppermute | solution.py:399
  79.1 5.3 %final.1 = (bf16[2,128,1024]{2,1,0:T(8,128)(2,1)}, bf16[2,128,1024]{2,1,0:T(8,128)(2,1)}, bf16[2,128,1024]{2,1,0:T(8,128)(2,1)}, bf16[2,128,1024]{2,1,0:T(8,128)(2,1)}) custom-call(s32[1]{0:T(128)} %bitcast.core, bf16[2,128,1024]{2,1,0:T(8,128)(2,1)} %query_in.3, bf16[2,128,1024]{2,1,0:T(8,128)(2,1)} %key_in.3, bf16[2,128,1024]{2,1,0:T(8,128)(2,1)} %value_in.3, ...), custom_call_target="tpu_custom_call" | custom-call | tf_op jit(solution)/shard_map/final/pallas_call | solution.py:405
  84.5 0.0 all-to-all-done.2
  84.5 0.6 maximum_multiply_fusion
  (2 shorter events, 0.0 us)
Async XLA Ops:
  0.6 15.2 %copy-start = (f32[16,256]{1,0:T(8,128)S(1)}, f32[16,256]{1,0:T(8,128)}, u32[]{:S(2)}) copy-start(f32[16,256]{1,0:T(8,128)} %rate.7) | copy-start | bytes 49156
  6.1 9.7 %collective-permute-start = (f32[32,8,128]{2,1,0:T(8,128)S(1)}, f32[32,8,128]{2,1,0:T(8,128)S(1)}, u32[]{:S(2)}, u32[]{:S(2)}) collective-permute-start(f32[32,8,128]{2,1,0:T(8,128)S(1)} %get-tuple-element.23), channel_id=1, source_target_pairs={{0,8},{8,0},{1,9},{9,1},{2,10},{10,2},{3,11},{11,3},{4,12},{12,4},... | collective-permute-start | bytes 393224 | tf_op jit(solution)/shard_map/ppermute | solution.py:368
  16.6 29.5 %all-to-all-start = ((f32[288,1,128]{2,1,0:T(1,128)}), f32[288,1,128]{2,1,0:T(1,128)S(1)}, u32[]{:S(2)}, u32[]{:S(2)}) async-start(f32[288,1,128]{2,1,0:T(1,128)} %pair.1), calls=%async_computation | async-start | bytes 294912 | tf_op jit(solution)/shard_map/all_to_all | solution.py:377
  29.0 0.7 copy-start.1
  68.7 15.8 %all-to-all-start.2 = ((f32[16,32,128]{2,1,0:T(8,128)}), f32[16,32,128]{2,1,0:T(8,128)S(1)}, u32[]{:S(2)}, u32[]{:S(2)}) async-start(f32[16,32,128]{2,1,0:T(8,128)} %get-tuple-element.38), calls=%async_computation.2 | async-start | bytes 524288 | tf_op jit(solution)/shard_map/all_to_all | solution.py:400
  75.9 3.2 %collective-permute-start.1 = (f32[32,8,128]{2,1,0:T(8,128)S(1)}, f32[32,8,128]{2,1,0:T(8,128)S(1)}, u32[]{:S(2)}, u32[]{:S(2)}) collective-permute-start(f32[32,8,128]{2,1,0:T(8,128)S(1)} %get-tuple-element.33), channel_id=1, source_target_pairs={{0,8},{8,0},{1,9},{9,1},{2,10},{10,2},{3,11},{11,3},{4,12},{12,4},... | collective-permute-start | bytes 393224 | tf_op jit(solution)/shard_map/ppermute | solution.py:399

commit v7 on v6

--- a/solution.py
+++ b/solution.py
@@ -17,14 +17,6 @@
 
 def spread(row):
     return jnp.broadcast_to(row, (8, LANES))
-
-
-def bottom():
-    return lax.broadcasted_iota(jnp.int32, (8, LANES), 0) >= 4
-
-
-def swap_halves(tile):
-    return pltpu.roll(tile, 4, 0)
 
 
 def lanes_of(half):
@@ -66,12 +58,14 @@
     work_g,
     keep,
     send,
-    within,
     query,
     key,
     value,
     grad,
     rate,
+    raw_u,
+    raw_g,
+    shares,
     sems,
     rate_sem,
 ):
@@ -128,18 +122,25 @@
                 0, length // STEP, step, (zero, zero, ones, zero, none), unroll=8
             )
             lags = lags or pairs_of
-            low = bottom()
             for m in range(WAVE):
-                top_half = jnp.where(low, swap_halves(downs[m]), ups[m])
-                end_half = jnp.where(low, downs[m], swap_halves(ups[m]))
                 piece = half * MODES + group + m
-                keep[piece] = jnp.where(first, top_half, end_half)
-                send[piece] = jnp.where(first, end_half, top_half)
+                raw_u[piece] = ups[m]
+                raw_g[piece] = downs[m]
                 inner = lags[-1]
                 for lag in reversed(range(STEP - 1)):
                     inner = decay[m] * inner + lags[lag]
                 inner = inner + decay[m] * sums[m]
-                within[piece : piece + 1, :] = jnp.sum(inner, axis=0, keepdims=True)
+                shares[piece : piece + 1, :] = jnp.sum(inner, axis=0, keepdims=True)
+        for m in range(MODES // 2):
+            one, two = half * MODES + m, half * MODES + MODES // 2 + m
+            spot = half * (MODES // 2) + m
+            for which, raw in enumerate((raw_u, raw_g)):
+                keep[2 * spot + which] = jnp.where(first, raw[one], raw[two])
+                send[2 * spot + which] = jnp.where(first, raw[two], raw[one])
+        one = shares[half * MODES : half * MODES + MODES // 2, :]
+        two = shares[half * MODES + MODES // 2 : (half + 1) * MODES, :]
+        keep[2 * MODES + half] = jnp.where(first, one, two)
+        send[2 * MODES + half] = jnp.where(first, two, one)
 
 
 def near_kernel(work_u, work_g, residue, rate, near, back):
@@ -170,21 +171,32 @@
     return jnp.where(first, own, other), jnp.where(first, other, own)
 
 
-def pair_kernel(core, own, other, within, rate, out, *, block):
+def own_rate(first, rate, m, half):
+    one = rate[m : m + 1, lanes_of(half)]
+    two = rate[MODES // 2 + m : MODES // 2 + m + 1, lanes_of(half)]
+    return jnp.where(first, one, two)
+
+
+def pair_kernel(core, own, other, rate, out, *, block):
     first = core[0] == 0
-    low = bottom()
-    for half in range(2):
-        for n in range(MODES):
-            piece = half * MODES + n
-            pace = rate[n : n + 1, lanes_of(half)]
+    for half in range(2):
+        within = own[2 * MODES + half] + other[2 * MODES + half]
+        for m in range(MODES // 2):
+            spot = half * (MODES // 2) + m
+            pace = own_rate(first, rate, m, half)
             decay = spread(jnp.exp(-pace * float(block)))
-            left, right = order(first, own[piece], other[piece])
-            joined = jnp.where(low, left + decay * right, decay * left + right)
-            cross = jnp.where(low, 0.0, left * swap_halves(right))
-            total = jnp.exp(-pace) * jnp.sum(cross, axis=0, keepdims=True)
-            for row in range(8):
-                out[piece * ROWS + row] = joined[row : row + 1, :]
-            out[piece * ROWS + 8] = within[piece : piece + 1, :] + total
+            left_u, right_u = order(first, own[2 * spot], other[2 * spot])
+            left_g, right_g = order(first, own[2 * spot + 1], other[2 * spot + 1])
+            rising = decay * left_u + right_u
+            falling = left_g + decay * right_g
+            cross = jnp.exp(-pace) * jnp.sum(left_u * right_g, axis=0, keepdims=True)
+            for seq in range(2):
+                start = (2 * spot + seq) * ROWS
+                for j in range(4):
+                    out[start + j] = rising[4 * seq + j : 4 * seq + j + 1, :]
+                    out[start + 4 + j] = falling[4 * seq + j : 4 * seq + j + 1, :]
+            out[2 * spot * ROWS + 8] = within[m : m + 1, :] + cross
+            out[(2 * spot + 1) * ROWS + 8] = jnp.zeros((1, LANES), F32)
 
 
 def scan_kernel(pieces, pace, out, *, block):
@@ -216,25 +228,25 @@
 
 def split_kernel(core, pieces, own, other, rate, keep, send, total, share, sems, *, block):
     first = core[0] == 0
-    low = bottom()
-    for piece in range(2 * MODES):
-        share[piece : piece + 1, :] = pieces[piece * ROWS + 8]
+    for spot in range(MODES):
+        share[spot : spot + 1, :] = pieces[2 * spot * ROWS + 8] + pieces[(2 * spot + 1) * ROWS + 8]
     copies = [pltpu.make_async_copy(share, total.at[i], sems.at[i]) for i in range(total.shape[0])]
     for copy in copies:
         copy.start()
     for half in range(2):
-        for n in range(MODES):
-            piece = half * MODES + n
-            pace = rate[n : n + 1, lanes_of(half)]
-            decay = spread(jnp.exp(-pace * float(block)))
-            left, right = order(first, own[piece], other[piece])
-            outer = jnp.concatenate([pieces[piece * ROWS + row] for row in range(8)], axis=0)
-            inner = decay * outer + jnp.where(low, right, left)
-            for_left = jnp.where(low, inner, outer)
-            for_right = jnp.where(low, outer, inner)
-            mine, others = order(first, for_left, for_right)
-            keep[piece] = mine
-            send[piece] = others
+        for m in range(MODES // 2):
+            spot = half * (MODES // 2) + m
+            decay = spread(jnp.exp(-own_rate(first, rate, m, half) * float(block)))
+            left_u, _ = order(first, own[2 * spot], other[2 * spot])
+            _, right_g = order(first, own[2 * spot + 1], other[2 * spot + 1])
+            rows = [[pieces[(2 * spot + seq) * ROWS + base + j] for seq in range(2) for j in range(4)] for base in (0, 4)]
+            ahead, behind = (jnp.concatenate(r, axis=0) for r in rows)
+            ahead_right = decay * ahead + left_u
+            behind_left = decay * behind + right_g
+            keep[2 * spot] = jnp.where(first, ahead, ahead_right)
+            send[2 * spot] = jnp.where(first, ahead_right, ahead)
+            keep[2 * spot + 1] = jnp.where(first, behind_left, behind)
+            send[2 * spot + 1] = jnp.where(first, behind, behind_left)
     for copy in copies:
         copy.wait()
 
@@ -270,7 +282,6 @@
     length = query.shape[1]
     repeat = query.shape[2] // (2 * LANES)
     first = core[0] == 0
-    low = bottom()
     outs = ((mixed, mixed_out), (grad_query, grad_query_out), (grad_key, grad_key_out), (grad_value, grad_value_out))
 
     fore, aft = ((query_in, query), (grad_in, grad)), ((value_in, value), (key_in, key))
@@ -292,12 +303,12 @@
     for half in range(2):
         decay, forward, backward = [], [], []
         for n in range(MODES):
-            piece = half * MODES + n
+            spot = half * (MODES // 2) + n % (MODES // 2)
             weight = spread(residue[n : n + 1, lanes_of(half)])
             decay.append(spread(jnp.exp(-rate[n : n + 1, lanes_of(half)])))
-            one, two = order(first, own[piece], other[piece])
-            forward.append(weight * jnp.where(low, swap_halves(two), one))
-            backward.append(weight * jnp.where(low, two, swap_halves(one)))
+            mine = first if n < MODES // 2 else jnp.logical_not(first)
+            forward.append(weight * jnp.where(mine, own[2 * spot], other[2 * spot]))
+            backward.append(weight * jnp.where(mine, own[2 * spot + 1], other[2 * spot + 1]))
 
         def step(i, carry, decay=decay, half=half, source=near):
             carry = [decay[n] * carry[n] for n in range(MODES)]
@@ -338,6 +349,7 @@
     pieces = 2 * MODES
     core = lax.axis_index("core").astype(jnp.int32).reshape(1)
     tile = struct(pieces, 8, LANES)
+    swaps = struct(pieces + 2, 8, LANES)
     rows = struct(pieces * ROWS, 1, LANES)
     works = struct(2, block * 8, LANES)
     whole = struct(*query.shape, dtype=jnp.bfloat16)
@@ -345,13 +357,18 @@
     inputs = tuple(pltpu.with_memory_space_constraint(x, pltpu.HBM) for x in (query, key, value, grad_out))
     buffers = [pltpu.VMEM(query.shape, jnp.bfloat16)] * 4
     arrivals = [pltpu.SemaphoreType.DMA((4, 2, repeat))]
-    work_u, work_g, keep, send, within = pl.pallas_call(
+    work_u, work_g, keep, send = pl.pallas_call(
         sums_kernel,
         name="sums",
-        out_shape=(works, works, tile, tile, struct(pieces, LANES)),
+        out_shape=(works, works, swaps, swaps),
         in_specs=[SMEM] + [HBM] * 5,
-        out_specs=(VMEM,) * 5,
-        scratch_shapes=buffers + [pltpu.VMEM(rate.shape, F32)] + arrivals + [pltpu.SemaphoreType.DMA],
+        out_specs=(VMEM,) * 4,
+        scratch_shapes=buffers
+        + [pltpu.VMEM(rate.shape, F32)]
+        + [pltpu.VMEM(tile.shape, F32)] * 2
+        + [pltpu.VMEM((pieces, LANES), F32)]
+        + arrivals
+        + [pltpu.SemaphoreType.DMA],
         compiler_params=room(12),
     )(core, *inputs, pltpu.with_memory_space_constraint(rate, pltpu.HBM))
     near, back = pl.pallas_call(
@@ -370,13 +387,14 @@
         functools.partial(pair_kernel, block=block),
         name="pair",
         out_shape=rows,
-        in_specs=[SMEM] + [VMEM] * 4,
+        in_specs=[SMEM] + [VMEM] * 3,
         out_specs=VMEM,
         compiler_params=room(4),
-    )(core, keep, other, within, rate)
+    )(core, keep, other, rate)
     gathered = lax.all_to_all(joined, ("xh", "z"), 0, 0, tiled=True)
     gathered, near, back = lax.optimization_barrier((gathered, near, back))
-    pace = lax.dynamic_slice(rate, (lax.axis_index("z"), lax.axis_index("xh") * LANES), (1, LANES))
+    mode = lax.axis_index("core") * (MODES // 2) + lax.axis_index("z") // 2
+    pace = lax.dynamic_slice(rate, (mode, lax.axis_index("xh") * LANES), (1, LANES))
     scanned = pl.pallas_call(
         functools.partial(scan_kernel, block=2 * block),
         name="scan",
@@ -390,17 +408,17 @@
     state, state_send, total = pl.pallas_call(
         functools.partial(split_kernel, block=block),
         name="split",
-        out_shape=(tile, tile, struct(group, pieces, LANES)),
+        out_shape=(tile, tile, struct(group, MODES, LANES)),
         in_specs=[SMEM] + [VMEM] * 4,
         out_specs=(VMEM, VMEM, HBM),
-        scratch_shapes=[pltpu.VMEM((pieces, LANES), F32), pltpu.SemaphoreType.DMA((group,))],
+        scratch_shapes=[pltpu.VMEM((MODES, LANES), F32), pltpu.SemaphoreType.DMA((group,))],
         compiler_params=room(4),
     )(core, returned, keep, other, rate)
     state_other = lax.ppermute(state_send, "core", exchange)
     shares = lax.all_to_all(total, ("core", "tensor"), 0, 0, tiled=True)
-    summed = jnp.sum(shares, axis=0)
+    summed = jnp.sum(shares.reshape(2, group // 2, MODES, LANES), axis=1).reshape(2, 2, MODES // 2, LANES)
+    summed = jnp.concatenate([summed[:, 0].reshape(MODES, LANES), summed[:, 1].reshape(MODES, LANES)], axis=1)
     length = block * lax.axis_size(("xh", "z", "core"))
-    summed = jnp.concatenate([summed[:MODES], summed[MODES:]], axis=1)
     grad_residue = summed / float(seq_count * length)
     mixed, grad_query, grad_key, grad_value = pl.pallas_call(
         final_kernel,

time: 85.7 us -> 88.1 us (1.028)
  waiting for transfers between devices: 13 us -> 15.6 us
    all_to_all x1, waiting for transfers between devices: 0.01 us -> 3.83 us  [staged(): shares = lax.all_to_all(total, ('core', 'tensor'), 0, 0, tiled=True)]
    ppermute x1, waiting for transfers between devices: 1.22 us -> 0.01 us  [staged(): state_other = lax.ppermute(state_send, 'core', exchange)]
  transfers between devices with their start and end apart: 4 -> 4, of which waited for: 3 -> 3; matrix products, arithmetic and copies ran while one was open for 0% -> 1% of each run, Pallas kernels for 13% -> 6%
where the time goes in v7:
time: 88.1 us; the launch traced here: 87.6 us
  starting transfers between devices  30.2 us (34%)
  blocking collectives  21.6 us (25%)
  Pallas kernels  18.1 us (21%)
  waiting for transfers between devices  15.6 us (18%)
    all_to_all x1, blocking collectives, staged(): returned = lax.all_to_all(scanned, ('xh', 'z'), 0, 0, tiled=True)  21.6 us
    all_to_all x1, starting transfers between devices, staged(): gathered = lax.all_to_all(joined, ('xh', 'z'), 0, 0, tiled=True)  12.3 us
    all_to_all x1, waiting for transfers between devices, staged(): gathered = lax.all_to_all(joined, ('xh', 'z'), 0, 0, tiled=True)  10.8 us
    ppermute x1, starting transfers between devices, staged(): other = lax.ppermute(send, 'core', exchange)  8.75 us
    all_to_all x1, starting transfers between devices, staged(): shares = lax.all_to_all(total, ('core', 'tensor'), 0, 0, tiled=True)  7.18 us
    pallas_call x1, Pallas kernels, staged(): pl.pallas_call(near_kernel, name='near', out_shape=(works, works), in_spe...  5.62 us
    pallas_call x1, Pallas kernels, staged(): pl.pallas_call(sums_kernel, name='sums', out_shape=(works, works, swaps,...  5.46 us
    pallas_call x1, Pallas kernels, staged(): pl.pallas_call(final_kernel, name='final', out_shape=(whole,) * 4, in_spe...  5.33 us
  transfers between devices with their start and end apart: 4, of which 3 were waited for; matrix products, arithmetic and copies ran while one was open for 1% of the time, Pallas kernels for 6%

profile of v7, /device:TPU:1, one launch (start us, length us, event | category | flops | bytes accessed | tf_op | source)
XLA Modules:
  0.0 87.6 jit_solution(200436559104863164)
XLA Ops:
  0.6 0.0 copy-start
  0.6 5.5 %sums.1 = (f32[2,1024,128]{2,1,0:T(8,128)S(1)}, f32[2,1024,128]{2,1,0:T(8,128)S(1)}, f32[34,8,128]{2,1,0:T(8,128)S(1)}, f32[34,8,128]{2,1,0:T(8,128)S(1)}) custom-call(s32[1]{0:T(128)} %bitcast.core, bf16[2,128,1024]{2,1,0:T(8,128)(2,1)} %query_in.3, bf16[2,128,1024]{2,1,0:T(8,128)(2,1)} %key_in.3, bf16[2,128,1024]{2,1,0:T(8,128)(2,1)} %value_in.3, ...), custom_call_target="tpu_custom_call" | custom-call | tf_op jit(solution)/shard_map/sums/pallas_call | solution.py:360
  6.1 8.7 %collective-permute-start = (f32[34,8,128]{2,1,0:T(8,128)S(1)}, f32[34,8,128]{2,1,0:T(8,128)S(1)}, u32[]{:S(2)}, u32[]{:S(2)}) collective-permute-start(f32[34,8,128]{2,1,0:T(8,128)S(1)} %get-tuple-element.22), channel_id=1, source_target_pairs={{0,8},{8,0},{1,9},{9,1},{2,10},{10,2},{3,11},{11,3},{4,12},{12,4},... | collective-permute-start | bytes 417800 | tf_op jit(solution)/shard_map/ppermute | solution.py:385
  14.9 1.0 %collective-permute-done.other = f32[34,8,128]{2,1,0:T(8,128)S(1)} collective-permute-done((f32[34,8,128]{2,1,0:T(8,128)S(1)}, f32[34,8,128]{2,1,0:T(8,128)S(1)}, u32[]{:S(2)}, u32[]{:S(2)}) %collective-permute-start) | collective-permute-done | bytes 139296 | tf_op jit(solution)/shard_map/ppermute | solution.py:385
  15.8 0.0 copy-done
  15.8 0.7 pair.1
  16.6 12.3 %all-to-all-start = ((f32[288,1,128]{2,1,0:T(1,128)}), f32[288,1,128]{2,1,0:T(1,128)S(1)}, u32[]{:S(2)}, u32[]{:S(2)}) async-start(f32[288,1,128]{2,1,0:T(1,128)} %pair.1), calls=%async_computation | async-start | bytes 294912 | tf_op jit(solution)/shard_map/all_to_all | solution.py:394
  28.9 0.0 copy-start.1
  28.9 0.1 dynamic_slice.3.pace
  29.0 0.6 copy-done.1
  29.6 5.6 %near.1 = (f32[2,1024,128]{2,1,0:T(8,128)S(1)}, f32[2,1024,128]{2,1,0:T(8,128)S(1)}) custom-call(f32[2,1024,128]{2,1,0:T(8,128)S(1)} %get-tuple-element.23.work_u, f32[2,1024,128]{2,1,0:T(8,128)S(1)} %get-tuple-element.24.work_g, f32[16,256]{1,0:T(8,128)S(1)} %copy-done.1, f32[16,256]{1,0:T(8,128)S(1)} %copy-done), custom_call_target="tpu_custom_call", output_to_operand_aliasing={{0}: (0, {}), {1}: (1, {})} | custom-call | flops 67108864 | bytes 4194304 | tf_op jit(solution)/shard_map/near/pallas_call | solution.py:374
  35.3 10.8 %all-to-all-done.pieces = f32[288,1,128]{2,1,0:T(1,128)S(1)} async-done(((f32[288,1,128]{2,1,0:T(1,128)}), f32[288,1,128]{2,1,0:T(1,128)S(1)}, u32[]{:S(2)}, u32[]{:S(2)}) %all-to-all-start) | async-done | bytes 147488 | tf_op jit(solution)/shard_map/all_to_all | solution.py:394
  46.1 0.1 scan.1
  46.2 21.6 %all_to_all.15.pieces = f32[288,1,128]{2,1,0:T(1,128)S(1)} all-to-all(f32[288,1,128]{2,1,0:T(1,128)S(1)} %scan.1), channel_id=1, replica_groups=mesh['xh'=2,'z'=16,'core'=2,'tensor'=8] {'xh','z'}, dimensions={0} | all-to-all | bytes 294912 | tf_op jit(solution)/shard_map/all_to_all | solution.py:406
  67.8 0.8 split.1
  68.6 7.2 %all-to-all-start.2 = ((f32[16,16,128]{2,1,0:T(8,128)}), f32[16,16,128]{2,1,0:T(8,128)S(1)}, u32[]{:S(2)}, u32[]{:S(2)}) async-start(f32[16,16,128]{2,1,0:T(8,128)} %get-tuple-element.36), calls=%async_computation.2 | async-start | bytes 262144 | tf_op jit(solution)/shard_map/all_to_all | solution.py:418
  75.8 2.0 %collective-permute-start.1 = (f32[32,8,128]{2,1,0:T(8,128)S(1)}, f32[32,8,128]{2,1,0:T(8,128)S(1)}, u32[]{:S(2)}, u32[]{:S(2)}) collective-permute-start(f32[32,8,128]{2,1,0:T(8,128)S(1)} %get-tuple-element.31), channel_id=1, source_target_pairs={{0,8},{8,0},{1,9},{9,1},{2,10},{10,2},{3,11},{11,3},{4,12},{12,4},... | collective-permute-start | bytes 393224 | tf_op jit(solution)/shard_map/ppermute | solution.py:417
  77.8 3.8 %all-to-all-done.2 = f32[16,16,128]{2,1,0:T(8,128)S(1)} async-done(((f32[16,16,128]{2,1,0:T(8,128)}), f32[16,16,128]{2,1,0:T(8,128)S(1)}, u32[]{:S(2)}, u32[]{:S(2)}) %all-to-all-start.2) | async-done | bytes 131104 | tf_op jit(solution)/shard_map/all_to_all | solution.py:418
  81.7 0.6 maximum_multiply_fusion
  82.3 0.0 collective-permute-done.1.other
  82.3 5.3 %final.1 = (bf16[2,128,1024]{2,1,0:T(8,128)(2,1)}, bf16[2,128,1024]{2,1,0:T(8,128)(2,1)}, bf16[2,128,1024]{2,1,0:T(8,128)(2,1)}, bf16[2,128,1024]{2,1,0:T(8,128)(2,1)}) custom-call(s32[1]{0:T(128)} %bitcast.core, bf16[2,128,1024]{2,1,0:T(8,128)(2,1)} %query_in.3, bf16[2,128,1024]{2,1,0:T(8,128)(2,1)} %key_in.3, bf16[2,128,1024]{2,1,0:T(8,128)(2,1)} %value_in.3, ...), custom_call_target="tpu_custom_call" | custom-call | tf_op jit(solution)/shard_map/final/pallas_call | solution.py:423
  (2 shorter events, 0.0 us)
Async XLA Ops:
  0.6 15.2 %copy-start = (f32[16,256]{1,0:T(8,128)S(1)}, f32[16,256]{1,0:T(8,128)}, u32[]{:S(2)}) copy-start(f32[16,256]{1,0:T(8,128)} %rate.7) | copy-start | bytes 49156
  6.1 9.7 %collective-permute-start = (f32[34,8,128]{2,1,0:T(8,128)S(1)}, f32[34,8,128]{2,1,0:T(8,128)S(1)}, u32[]{:S(2)}, u32[]{:S(2)}) collective-permute-start(f32[34,8,128]{2,1,0:T(8,128)S(1)} %get-tuple-element.22), channel_id=1, source_target_pairs={{0,8},{8,0},{1,9},{9,1},{2,10},{10,2},{3,11},{11,3},{4,12},{12,4},... | collective-permute-start | bytes 417800 | tf_op jit(solution)/shard_map/ppermute | solution.py:385
  16.6 29.5 %all-to-all-start = ((f32[288,1,128]{2,1,0:T(1,128)}), f32[288,1,128]{2,1,0:T(1,128)S(1)}, u32[]{:S(2)}, u32[]{:S(2)}) async-start(f32[288,1,128]{2,1,0:T(1,128)} %pair.1), calls=%async_computation | async-start | bytes 294912 | tf_op jit(solution)/shard_map/all_to_all | solution.py:394
  28.9 0.7 copy-start.1
  68.6 13.0 %all-to-all-start.2 = ((f32[16,16,128]{2,1,0:T(8,128)}), f32[16,16,128]{2,1,0:T(8,128)S(1)}, u32[]{:S(2)}, u32[]{:S(2)}) async-start(f32[16,16,128]{2,1,0:T(8,128)} %get-tuple-element.36), calls=%async_computation.2 | async-start | bytes 262144 | tf_op jit(solution)/shard_map/all_to_all | solution.py:418
  75.8 6.5 %collective-permute-start.1 = (f32[32,8,128]{2,1,0:T(8,128)S(1)}, f32[32,8,128]{2,1,0:T(8,128)S(1)}, u32[]{:S(2)}, u32[]{:S(2)}) collective-permute-start(f32[32,8,128]{2,1,0:T(8,128)S(1)} %get-tuple-element.31), channel_id=1, source_target_pairs={{0,8},{8,0},{1,9},{9,1},{2,10},{10,2},{3,11},{11,3},{4,12},{12,4},... | collective-permute-start | bytes 393224 | tf_op jit(solution)/shard_map/ppermute | solution.py:417

commit v8 on v7

--- a/solution.py
+++ b/solution.py
@@ -253,7 +253,7 @@
 
 def final_kernel(
     core,
-    query_in,
+    query,
     key_in,
     value_in,
     grad_in,
@@ -268,7 +268,6 @@
     grad_key_out,
     grad_value_out,
     work,
-    query,
     key,
     value,
     grad,
@@ -284,7 +283,7 @@
     first = core[0] == 0
     outs = ((mixed, mixed_out), (grad_query, grad_query_out), (grad_key, grad_key_out), (grad_value, grad_value_out))
 
-    fore, aft = ((query_in, query), (grad_in, grad)), ((value_in, value), (key_in, key))
+    fore, aft = ((grad_in, grad),), ((value_in, value), (key_in, key))
     for half in range(2):
         fetch(fore, in_sems, half, repeat, False)
         fetch(aft, in_sems, half, repeat, False, 2)
@@ -424,11 +423,11 @@
         final_kernel,
         name="final",
         out_shape=(whole,) * 4,
-        in_specs=[SMEM] + [HBM] * 4 + [VMEM] * 6,
+        in_specs=[SMEM] + [VMEM] + [HBM] * 3 + [VMEM] * 6,
         out_specs=(HBM,) * 4,
-        scratch_shapes=[pltpu.VMEM((block * 8, LANES), F32)] + buffers * 2 + arrivals * 2,
+        scratch_shapes=[pltpu.VMEM((block * 8, LANES), F32)] + buffers[:3] + buffers + arrivals * 2,
         compiler_params=room(12),
-    )(core, *inputs, residue, rate, near, back, state, state_other)
+    )(core, query, *inputs[1:], residue, rate, near, back, state, state_other)
     return (mixed, grad_query, grad_key, grad_value, grad_residue)
 
 

time: 88.1 us -> 88 us (level)
  no operation moved by 1% of the time
where the time goes in v8:
time: 88 us; the launch traced here: 87.5 us
  starting transfers between devices  30.2 us (34%)
  blocking collectives  21.6 us (25%)
  Pallas kernels  18 us (20%)
  waiting for transfers between devices  15.6 us (18%)
    all_to_all x1, blocking collectives, staged(): returned = lax.all_to_all(scanned, ('xh', 'z'), 0, 0, tiled=True)  21.6 us
    all_to_all x1, starting transfers between devices, staged(): gathered = lax.all_to_all(joined, ('xh', 'z'), 0, 0, tiled=True)  12.3 us
    all_to_all x1, waiting for transfers between devices, staged(): gathered = lax.all_to_all(joined, ('xh', 'z'), 0, 0, tiled=True)  10.8 us
    ppermute x1, starting transfers between devices, staged(): other = lax.ppermute(send, 'core', exchange)  8.75 us
    all_to_all x1, starting transfers between devices, staged(): shares = lax.all_to_all(total, ('core', 'tensor'), 0, 0, tiled=True)  7.18 us
    pallas_call x1, Pallas kernels, staged(): pl.pallas_call(near_kernel, name='near', out_shape=(works, works), in_spe...  5.62 us
    pallas_call x1, Pallas kernels, staged(): pl.pallas_call(sums_kernel, name='sums', out_shape=(works, works, swaps,...  5.46 us
    pallas_call x1, Pallas kernels, staged(): pl.pallas_call(final_kernel, name='final', out_shape=(whole,) * 4, in_spe...  5.2 us
  transfers between devices with their start and end apart: 4, of which 3 were waited for; matrix products, arithmetic and copies ran while one was open for 1% of the time, Pallas kernels for 6%

profile of v8, /device:TPU:1, one launch (start us, length us, event | category | flops | bytes accessed | tf_op | source)
XLA Modules:
  0.0 87.5 jit_solution(13734479492563320052)
XLA Ops:
  0.6 0.0 copy-start.1
  0.6 5.5 %sums.1 = (f32[2,1024,128]{2,1,0:T(8,128)S(1)}, f32[2,1024,128]{2,1,0:T(8,128)S(1)}, f32[34,8,128]{2,1,0:T(8,128)S(1)}, f32[34,8,128]{2,1,0:T(8,128)S(1)}) custom-call(s32[1]{0:T(128)} %bitcast.core, bf16[2,128,1024]{2,1,0:T(8,128)(2,1)} %query.1, bf16[2,128,1024]{2,1,0:T(8,128)(2,1)} %key_in.3, bf16[2,128,1024]{2,1,0:T(8,128)(2,1)} %value_in.3, ...), custom_call_target="tpu_custom_call" | custom-call | tf_op jit(solution)/shard_map/sums/pallas_call | solution.py:359
  6.1 8.7 %collective-permute-start = (f32[34,8,128]{2,1,0:T(8,128)S(1)}, f32[34,8,128]{2,1,0:T(8,128)S(1)}, u32[]{:S(2)}, u32[]{:S(2)}) collective-permute-start(f32[34,8,128]{2,1,0:T(8,128)S(1)} %get-tuple-element.22), channel_id=1, source_target_pairs={{0,8},{8,0},{1,9},{9,1},{2,10},{10,2},{3,11},{11,3},{4,12},{12,4},... | collective-permute-start | bytes 417800 | tf_op jit(solution)/shard_map/ppermute | solution.py:384
  14.9 1.0 %collective-permute-done.other = f32[34,8,128]{2,1,0:T(8,128)S(1)} collective-permute-done((f32[34,8,128]{2,1,0:T(8,128)S(1)}, f32[34,8,128]{2,1,0:T(8,128)S(1)}, u32[]{:S(2)}, u32[]{:S(2)}) %collective-permute-start) | collective-permute-done | bytes 139296 | tf_op jit(solution)/shard_map/ppermute | solution.py:384
  15.8 0.0 copy-done.1
  15.8 0.7 pair.1
  16.6 12.3 %all-to-all-start = ((f32[288,1,128]{2,1,0:T(1,128)}), f32[288,1,128]{2,1,0:T(1,128)S(1)}, u32[]{:S(2)}, u32[]{:S(2)}) async-start(f32[288,1,128]{2,1,0:T(1,128)} %pair.1), calls=%async_computation | async-start | bytes 294912 | tf_op jit(solution)/shard_map/all_to_all | solution.py:393
  28.9 0.0 copy-start.2
  28.9 0.1 dynamic_slice.3.pace
  29.0 0.6 copy-done.2
  29.6 5.6 %near.1 = (f32[2,1024,128]{2,1,0:T(8,128)S(1)}, f32[2,1024,128]{2,1,0:T(8,128)S(1)}) custom-call(f32[2,1024,128]{2,1,0:T(8,128)S(1)} %get-tuple-element.23.work_u, f32[2,1024,128]{2,1,0:T(8,128)S(1)} %get-tuple-element.24.work_g, f32[16,256]{1,0:T(8,128)S(1)} %copy-done.2, f32[16,256]{1,0:T(8,128)S(1)} %copy-done.1), custom_call_target="tpu_custom_call", output_to_operand_aliasing={{0}: (0, {}), {1}: (1, {})} | custom-call | flops 67108864 | bytes 4194304 | tf_op jit(solution)/shard_map/near/pallas_call | solution.py:373
  35.3 10.8 %all-to-all-done.pieces = f32[288,1,128]{2,1,0:T(1,128)S(1)} async-done(((f32[288,1,128]{2,1,0:T(1,128)}), f32[288,1,128]{2,1,0:T(1,128)S(1)}, u32[]{:S(2)}, u32[]{:S(2)}) %all-to-all-start) | async-done | bytes 147488 | tf_op jit(solution)/shard_map/all_to_all | solution.py:393
  46.1 0.1 scan.1
  46.2 21.6 %all_to_all.15.pieces = f32[288,1,128]{2,1,0:T(1,128)S(1)} all-to-all(f32[288,1,128]{2,1,0:T(1,128)S(1)} %scan.1), channel_id=1, replica_groups=mesh['xh'=2,'z'=16,'core'=2,'tensor'=8] {'xh','z'}, dimensions={0} | all-to-all | bytes 294912 | tf_op jit(solution)/shard_map/all_to_all | solution.py:405
  67.8 0.0 copy-start
  67.8 0.8 split.1
  68.6 7.2 %all-to-all-start.2 = ((f32[16,16,128]{2,1,0:T(8,128)}), f32[16,16,128]{2,1,0:T(8,128)S(1)}, u32[]{:S(2)}, u32[]{:S(2)}) async-start(f32[16,16,128]{2,1,0:T(8,128)} %get-tuple-element.36), calls=%async_computation.2 | async-start | bytes 262144 | tf_op jit(solution)/shard_map/all_to_all | solution.py:417
  75.8 2.0 %collective-permute-start.1 = (f32[32,8,128]{2,1,0:T(8,128)S(1)}, f32[32,8,128]{2,1,0:T(8,128)S(1)}, u32[]{:S(2)}, u32[]{:S(2)}) collective-permute-start(f32[32,8,128]{2,1,0:T(8,128)S(1)} %get-tuple-element.31), channel_id=1, source_target_pairs={{0,8},{8,0},{1,9},{9,1},{2,10},{10,2},{3,11},{11,3},{4,12},{12,4},... | collective-permute-start | bytes 393224 | tf_op jit(solution)/shard_map/ppermute | solution.py:416
  77.8 3.8 %all-to-all-done.2 = f32[16,16,128]{2,1,0:T(8,128)S(1)} async-done(((f32[16,16,128]{2,1,0:T(8,128)}), f32[16,16,128]{2,1,0:T(8,128)S(1)}, u32[]{:S(2)}, u32[]{:S(2)}) %all-to-all-start.2) | async-done | bytes 131104 | tf_op jit(solution)/shard_map/all_to_all | solution.py:417
  81.7 0.6 maximum_multiply_fusion
  82.3 0.0 collective-permute-done.1.other
  82.3 0.0 copy-done
  82.3 5.2 %final.1 = (bf16[2,128,1024]{2,1,0:T(8,128)(2,1)}, bf16[2,128,1024]{2,1,0:T(8,128)(2,1)}, bf16[2,128,1024]{2,1,0:T(8,128)(2,1)}, bf16[2,128,1024]{2,1,0:T(8,128)(2,1)}) custom-call(s32[1]{0:T(128)} %bitcast.core, bf16[2,128,1024]{2,1,0:T(8,128)(2,1)S(1)} %copy-done, bf16[2,128,1024]{2,1,0:T(8,128)(2,1)} %key_in.3, bf16[2,128,1024]{2,1,0:T(8,128)(2,1)} %value_in.3, ...), custom_call_target="tpu_custom_call" | custom-call | tf_op jit(solution)/shard_map/final/pallas_call | solution.py:422
  (2 shorter events, 0.0 us)
Async XLA Ops:
  0.6 15.2 %copy-start.1 = (f32[16,256]{1,0:T(8,128)S(1)}, f32[16,256]{1,0:T(8,128)}, u32[]{:S(2)}) copy-start(f32[16,256]{1,0:T(8,128)} %rate.7) | copy-start | bytes 49156
  6.1 9.7 %collective-permute-start = (f32[34,8,128]{2,1,0:T(8,128)S(1)}, f32[34,8,128]{2,1,0:T(8,128)S(1)}, u32[]{:S(2)}, u32[]{:S(2)}) collective-permute-start(f32[34,8,128]{2,1,0:T(8,128)S(1)} %get-tuple-element.22), channel_id=1, source_target_pairs={{0,8},{8,0},{1,9},{9,1},{2,10},{10,2},{3,11},{11,3},{4,12},{12,4},... | collective-permute-start | bytes 417800 | tf_op jit(solution)/shard_map/ppermute | solution.py:384
  16.6 29.5 %all-to-all-start = ((f32[288,1,128]{2,1,0:T(1,128)}), f32[288,1,128]{2,1,0:T(1,128)S(1)}, u32[]{:S(2)}, u32[]{:S(2)}) async-start(f32[288,1,128]{2,1,0:T(1,128)} %pair.1), calls=%async_computation | async-start | bytes 294912 | tf_op jit(solution)/shard_map/all_to_all | solution.py:393
  28.9 0.7 copy-start.2
  67.8 14.5 %copy-start = (bf16[2,128,1024]{2,1,0:T(8,128)(2,1)S(1)}, bf16[2,128,1024]{2,1,0:T(8,128)(2,1)}, u32[]{:S(2)}) copy-start(bf16[2,128,1024]{2,1,0:T(8,128)(2,1)} %query.1) | copy-start | bytes 1572868
  68.6 13.0 %all-to-all-start.2 = ((f32[16,16,128]{2,1,0:T(8,128)}), f32[16,16,128]{2,1,0:T(8,128)S(1)}, u32[]{:S(2)}, u32[]{:S(2)}) async-start(f32[16,16,128]{2,1,0:T(8,128)} %get-tuple-element.36), calls=%async_computation.2 | async-start | bytes 262144 | tf_op jit(solution)/shard_map/all_to_all | solution.py:417
  75.8 6.5 %collective-permute-start.1 = (f32[32,8,128]{2,1,0:T(8,128)S(1)}, f32[32,8,128]{2,1,0:T(8,128)S(1)}, u32[]{:S(2)}, u32[]{:S(2)}) collective-permute-start(f32[32,8,128]{2,1,0:T(8,128)S(1)} %get-tuple-element.31), channel_id=1, source_target_pairs={{0,8},{8,0},{1,9},{9,1},{2,10},{10,2},{3,11},{11,3},{4,12},{12,4},... | collective-permute-start | bytes 393224 | tf_op jit(solution)/shard_map/ppermute | solution.py:416
